TPU v7x, 32 devices: a whole 2x2x4 slice. The times are simulated.
32 devices in a mesh: dp: 4 (over z), adapter: 2 (over x), tensor: 4 (over y, core).
Axes of the slice: x: 2, y: 2, z: 4, core: 2. Of those that a mesh axis runs over, the one named last changes fastest.
Arguments:
- tokens: bfloat16 [6144, 8192], P(('dp', 'adapter'), 'tensor'), may hold values from -6 to 6
- frozen_value_weight: bfloat16 [8192, 1024], P('tensor'), may hold values from -0.0625 to 0.0625
- adapter_down_weight: bfloat16 [24, 64, 8192], P(('adapter', 'tensor')), may hold values from -0.0625 to 0.0625
- adapter_up_weight: bfloat16 [24, 64, 1024], P(('adapter', 'tensor')), may hold values from -0.75 to 0.75
- cotangent: bfloat16 [6144, 1024], P(('dp', 'adapter')), may hold values from -12 to 12
- language_pair_index: int32 [6144], P(('dp', 'adapter')), may hold values from 0 to 23, as said below
- language_pair_counts: int32 [8, 24], P(('dp', 'adapter')), may hold values from 0 to 64, as said below
- adapter_owner_table: int32 [24], replicated, may hold values from 0 to 23, as said below
Outputs:
- mixed_out: bfloat16 [6144, 1024], P(('dp', 'adapter'), 'tensor')
- token_input_gradient: bfloat16 [6144, 8192], P(('dp', 'adapter'), 'tensor')
- grad_down: bfloat16 [24, 64, 8192], P(('adapter', 'tensor'), 'dp')
- grad_up: bfloat16 [24, 64, 1024], P(('adapter', 'tensor'), 'dp')
Inputs may be any that keep to these rules, and one draw needn't show every extreme that they name: `language_pair_index`: within one row block (the 768 rows of one index of dp+adapter), at most 192 rows have pairs whose stored index adapter_owner_table[p] lies in one owner's range [o * 3, (o + 1) * 3); for each dp index one owner gets exactly 192 rows from every row block of that dp index. language_pair_counts[g, p] is the number of rows of row block g whose pair id is p; in every row block some pair has exactly (192 + 3 - 1) // 3 rows. `adapter_owner_table`: A permutation of 0 to 23.
All inputs are finite; a program needn't handle non-finite values.
Results may differ from a plain program's by a relative error of at most 0.012.
Values may be sent and summed in bfloat16 or wider, within the bound.
No kernel may reach another device: no remote copies, remote signals or barrier semaphores. Data moves between devices by JAX's collectives and lax.ppermute only.
A program may use at most 128 MiB of HBM per device.

v0:
```python
import jax
import jax.numpy as jnp
from jax import lax
from jax.sharding import PartitionSpec as P

ADAPTER_SCALE = 0.5
CHUNKS = 2
SPLIT = 128


def exchange(pieces, axes):
    return lax.all_to_all(pieces, axes, split_axis=0, concat_axis=0, tiled=True)


def column_blocks(matrix, blocks):
    width = matrix.shape[1] // blocks
    return jnp.stack([matrix[:, i * width : (i + 1) * width] for i in range(blocks)])


def shift(array, axis, step):
    size = lax.axis_size(axis)
    return lax.ppermute(array, axis, [(i, (i + step) % size) for i in range(size)])


def tensor_sum(partial):
    size = lax.axis_size("tensor")
    total = partial
    bit = 1
    while bit < size:
        other = lax.ppermute(total, "tensor", [(i, i ^ bit) for i in range(size)])
        total = (total.astype(jnp.float32) + other.astype(jnp.float32)).astype(jnp.bfloat16)
        bit *= 2
    return total


def dot(a, b, ca, cb):
    return lax.dot_general(a, b, (((ca,), (cb,)), ((), ())), preferred_element_type=jnp.float32)


class Columns:
    def __init__(self, first, adapters, rank, parts):
        width = adapters * rank
        column = jnp.arange(width, dtype=jnp.int32)
        piece = rank // parts
        self.slot = first + (column % (adapters * piece)) // piece
        self.rank = (column // (adapters * piece)) * piece + column % piece
        self.select = (jnp.arange(rank, dtype=jnp.int32)[:, None] == self.rank[None, :]).astype(
            jnp.bfloat16
        )

    def spread(self, compact, slots):
        mine = slots[:, None] == self.slot[None, :]
        return jnp.where(mine, dot(compact, self.select, 1, 0), 0.0).astype(jnp.bfloat16)

    def gather(self, full, slots):
        mine = slots[:, None] == self.slot[None, :]
        return dot(jnp.where(mine, full, 0.0).astype(jnp.bfloat16), self.select, 1, 1)


def shards(
    tokens,
    frozen_value_weight,
    adapter_down_weight,
    adapter_up_weight,
    cotangent,
    language_pair_index,
    language_pair_counts,
    adapter_owner_table,
):
    sides = lax.axis_size("adapter")
    shares = lax.axis_size("tensor")
    planes = lax.axis_size("dp")
    side = lax.axis_index("adapter")
    share = lax.axis_index("tensor")
    plane = lax.axis_index("dp")
    rows, width = tokens.shape
    stored, rank, _ = adapter_down_weight.shape
    values = cotangent.shape[1]
    value_width = values // shares
    own = shares * stored
    total = sides * own
    piece = rank // planes

    down_flat = adapter_down_weight.reshape(stored * rank, shares * width)
    up_flat = adapter_up_weight.reshape(stored * rank, values)

    def to_all(blocks):
        return jnp.broadcast_to(blocks[None], (sides,) + blocks.shape).reshape(
            (sides * shares,) + blocks.shape[1:]
        )

    ups = exchange(to_all(column_blocks(up_flat, shares)), ("adapter", "tensor"))
    ups = ups.reshape(total * rank, value_width)
    quarter = lax.dynamic_slice_in_dim(adapter_down_weight, plane * piece, piece, 1)
    quarter = column_blocks(quarter.reshape(stored * piece, shares * width), shares)
    quarters = exchange(to_all(quarter), ("adapter", "tensor")).reshape(
        sides, own * piece, width
    )
    own_down = exchange(column_blocks(down_flat, shares), "tensor").reshape(own * rank, width)
    other_downs = [
        lax.all_gather(
            lax.dynamic_index_in_dim(quarters, (side - j) % sides, 0, keepdims=False),
            "dp",
            axis=0,
            tiled=True,
        )
        for j in range(1, sides)
    ]

    pairs = jnp.arange(adapter_owner_table.shape[0], dtype=jnp.int32)
    matches = language_pair_index[:, None] == pairs[None, :]
    slots = jnp.sum(jnp.where(matches, adapter_owner_table[None, :], 0), axis=1)
    row_counts = jnp.sum(jnp.where(matches, language_pair_counts[0][None, :], 0), axis=1)
    row_weight = 1.0 / row_counts.astype(jnp.float32)
    scaled = (cotangent.astype(jnp.float32) * row_weight[:, None]).astype(jnp.bfloat16)
    scaled_part = lax.dynamic_slice_in_dim(scaled, share * value_width, value_width, 1)

    every = Columns(0, total, rank, 1)
    mine = Columns(side * own, own, rank, 1)
    mine_parts = Columns(side * own, own, rank, planes)
    others = [Columns(((side - j) % sides) * own, own, rank, planes) for j in range(1, sides)]

    base_term = dot(tokens, frozen_value_weight, 1, 0).astype(jnp.bfloat16)
    base_share = lax.psum_scatter(base_term, "tensor", scatter_dimension=1, tiled=True)

    back_part = every.gather(ADAPTER_SCALE * dot(scaled_part, ups, 1, 1), slots)
    back = tensor_sum(back_part.astype(jnp.bfloat16))

    tag = jnp.stack([slots // SPLIT, slots % SPLIT], axis=1).astype(jnp.bfloat16)
    message = jnp.concatenate([back, tag], axis=1)
    messages = [message] + [shift(message, "adapter", j) for j in range(1, sides)]
    spread_back = []
    for got in messages:
        numbers = got[:, rank:].astype(jnp.int32)
        spread_back.append(
            mine_parts.spread(got[:, :rank], numbers[:, 0] * SPLIT + numbers[:, 1])
        )

    chunk = width // CHUNKS
    down_chunks = []
    for c in range(CHUNKS):
        block = tokens[:, c * chunk : (c + 1) * chunk]
        blocks = [block] + [shift(block, "adapter", j) for j in range(1, sides)]
        part = sum(dot(b, g, 0, 0) for b, g in zip(spread_back, blocks))
        part = part.astype(jnp.bfloat16).reshape(planes * shares, stored * piece, chunk)
        parts = exchange(part, ("dp", "tensor"))
        parts = parts.reshape(planes, shares, stored * piece, chunk)
        down_chunks.append(jnp.sum(parts.astype(jnp.float32), axis=0).astype(jnp.bfloat16))
    grad_down = jnp.concatenate(
        [down_chunks[c][s] for s in range(shares) for c in range(CHUNKS)], axis=1
    ).reshape(stored, piece, shares * width)

    input_gradient = dot(scaled, frozen_value_weight, 1, 1)
    input_gradient += dot(mine.spread(back, slots), own_down, 1, 0)
    low_part = mine.gather(dot(tokens, own_down, 1, 1), slots)
    for columns, other_down in zip(others, other_downs):
        input_gradient += dot(columns.spread(back, slots), other_down, 1, 0)
        low_part += columns.gather(dot(tokens, other_down, 1, 1), slots)
    low = tensor_sum(low_part.astype(jnp.bfloat16))

    spread_low = every.spread(low, slots)
    delta = ADAPTER_SCALE * dot(spread_low, ups, 1, 0)
    mixed_out = (base_share.astype(jnp.float32) + delta).astype(jnp.bfloat16)
    up_part = (ADAPTER_SCALE * dot(spread_low, scaled_part, 0, 0)).astype(jnp.bfloat16)
    up_part = up_part.reshape(sides, shares, stored, planes, piece, value_width)
    up_part = up_part.transpose(3, 0, 1, 2, 4, 5).reshape(
        planes * sides * shares, stored * piece, value_width
    )
    up_parts = exchange(up_part, ("dp", "adapter", "tensor"))
    up_parts = up_parts.reshape(planes * sides, shares, stored * piece, value_width)
    up_sum = jnp.sum(up_parts.astype(jnp.float32), axis=0).astype(jnp.bfloat16)
    grad_up = jnp.concatenate([up_sum[s] for s in range(shares)], axis=1).reshape(
        stored, piece, values
    )
    return mixed_out, input_gradient.astype(jnp.bfloat16), grad_down, grad_up


def solution(mesh):
    return jax.shard_map(
        shards,
        mesh=mesh,
        in_specs=(
            P(("dp", "adapter"), "tensor"),
            P("tensor", None),
            P(("adapter", "tensor"), None, None),
            P(("adapter", "tensor"), None, None),
            P(("dp", "adapter"), None),
            P(("dp", "adapter")),
            P(("dp", "adapter"), None),
            P(),
        ),
        out_specs=(
            P(("dp", "adapter"), "tensor"),
            P(("dp", "adapter"), "tensor"),
            P(("adapter", "tensor"), "dp", None),
            P(("adapter", "tensor"), "dp", None),
        ),
        check_vma=False,
    )
```

profile of v0, /device:TPU:0, one launch (start us, length us, event | category | flops | bytes accessed | tf_op | source)
XLA Modules:
  0.0 287.2 jit_solution(11422209470200756058)
XLA Ops:
  8.0 1.1 slice_bitcast_fusion.11
  9.1 1.0 broadcast_in_dim.43
  10.1 5.2 %all-to-all-start.2 = ((bf16[8,192,256]{2,1,0:T(8,128)(2,1)}), bf16[8,192,256]{2,1,0:T(8,128)(2,1)}, u32[]{:S(2)}, u32[]{:S(2)}) async-start(bf16[8,192,256]{2,1,0:T(8,128)(2,1)} %bitcast.21), calls=%async_computation.3 | async-start | bytes 1572864 | tf_op jit(solution)/shard_map/all_to_all | solution.py:12
  15.3 4.0 %fusion.100 = (bf16[768,1024]{1,0:T(8,128)(2,1)}, bf16[768,1024]{1,0:T(8,128)(2,1)}) fusion(bf16[768,2048]{1,0:T(8,128)(2,1)} %param.8), kind=kLoop, calls=%fused_computation.182 | loop fusion | bytes 6291456 | tf_op jit(solution)/shard_map/slice | solution.py:142
  19.2 2.1 collective-permute-start.6
  21.6 1.0 pad_maximum_fusion.1
  22.7 1.8 slice_bitcast_fusion.3
  24.4 3.1 %all-to-all-done.2 = bf16[8,192,256]{2,1,0:T(8,128)(2,1)} async-done(((bf16[8,192,256]{2,1,0:T(8,128)(2,1)}), bf16[8,192,256]{2,1,0:T(8,128)(2,1)}, u32[]{:S(2)}, u32[]{:S(2)}) %all-to-all-start.2) | async-done | bytes 786464 | tf_op jit(solution)/shard_map/all_to_all | solution.py:12
  27.5 2.5 broadcast_in_dim.41
  30.0 3.6 %all-to-all-start.1 = ((bf16[8,48,2048]{2,1,0:T(8,128)(2,1)}), bf16[8,48,2048]{2,1,0:T(8,128)(2,1)S(1)}, u32[]{:S(2)}, u32[]{:S(2)}) async-start(bf16[8,48,2048]{2,1,0:T(8,128)(2,1)} %bitcast.12), calls=%async_computation.2 | async-start | bytes 3145728 | tf_op jit(solution)/shard_map/all_to_all | solution.py:12
  33.6 3.1 %pad_maximum_fusion = bf16[4,192,2048]{2,1,0:T(8,128)(2,1)} fusion(bf16[1,192,2048]{2,1,0:T(8,128)(2,1)S(1)} %copy-done.2, bf16[1,192,2048]{2,1,0:T(8,128)(2,1)} %get-tuple-element.10, bf16[1,192,2048]{2,1,0:T(8,128)(2,1)} %get-tuple-element.11, bf16[1,192,2048]{2,1,0:T(8,128)(2,1)S(1)} %copy-done.1), kind=kLoop, calls=%fused_computation.5 | loop fusion | flops 4718592 | bytes 6291456 | tf_op jit(solution)/shard_map/stack | solution.py:17
  36.7 0.3 multiply_convert_fusion
  37.1 3.1 %fusion.35 = bf16[768,64]{0,1:T(8,128)(2,1)S(1)} fusion(bf16[1536,256]{1,0:T(8,128)(2,1)} %bitcast.22, s32[1536]{0:T(1024)S(1)} %get-tuple-element.36, s32[768]{0:T(1024)S(1)} %get-tuple-element.5, bf16[768,1024]{1,0:T(8,128)(2,1)S(1)} %multiply_convert_fusion, s32[]{:T(128)S(6)} %select_n.211, s32[1536]{0:T(1024)S(1)} %get-tuple-element.37), kind=kOutput, calls=%fused_computation.46 | convolution fusion | flops 759840768 | bytes 1298436 | tf_op jit(solution)/shard_map/dot_general | solution.py:37
  40.2 0.5 collective-permute-start.2
  40.7 0.9 collective-permute-done.2
  41.7 1.9 collective-permute-start.3
  43.6 33.8 %all-to-all-done.1 = bf16[8,48,2048]{2,1,0:T(8,128)(2,1)S(1)} async-done(((bf16[8,48,2048]{2,1,0:T(8,128)(2,1)}), bf16[8,48,2048]{2,1,0:T(8,128)(2,1)S(1)}, u32[]{:S(2)}, u32[]{:S(2)}) %all-to-all-start.1) | async-done | bytes 1572896 | tf_op jit(solution)/shard_map/all_to_all | solution.py:12
  77.5 4.7 %all-to-all-start = ((bf16[4,192,2048]{2,1,0:T(8,128)(2,1)}), bf16[4,192,2048]{2,1,0:T(8,128)(2,1)}, u32[]{:S(2)}, u32[]{:S(2)}) async-start(bf16[4,192,2048]{2,1,0:T(8,128)(2,1)} %pad_maximum_fusion), calls=%async_computation.1 | async-start | bytes 6291456 | tf_op jit(solution)/shard_map/all_to_all | solution.py:12
  82.3 0.5 collective-permute-start.4
  82.8 0.5 fusion.41
  83.3 4.9 %fusion.96 = f32[768,1024]{1,0:T(8,128)} fusion(bf16[768,2048]{1,0:T(8,128)(2,1)} %param.8, bf16[768,768]{0,1:T(8,128)(2,1)S(1)} %fusion.41, s32[768]{0:T(1024)S(1)} %fusion.84, s32[768]{0:T(1024)S(1)} %fusion.86), kind=kOutput, calls=%fused_computation.178 | convolution fusion | flops 1209139200 | bytes 5904384 | tf_op jit(solution)/shard_map/dot_general | solution.py:37
  88.3 1.0 constant_dynamic-slice_fusion
  89.3 0.5 select_convert_fusion
  89.8 1.0 copy-done.19
  90.8 5.0 %add_convert_fusion.1 = bf16[768,1024]{1,0:T(8,128)(2,1)} fusion(f32[768,1024]{1,0:T(8,128)} %fusion.96, bf16[768,768]{0,1:T(8,128)(2,1)S(1)} %select_convert_fusion, bf16[768,1024]{1,0:T(8,128)(2,1)} %collective-permute-done.6), kind=kOutput, calls=%fused_computation.9 | convolution fusion | flops 1209532416 | bytes 7471104 | tf_op jit(solution)/shard_map/dot_general | solution.py:37
  95.8 23.3 %all-to-all-done = bf16[4,192,2048]{2,1,0:T(8,128)(2,1)} async-done(((bf16[4,192,2048]{2,1,0:T(8,128)(2,1)}), bf16[4,192,2048]{2,1,0:T(8,128)(2,1)}, u32[]{:S(2)}, u32[]{:S(2)}) %all-to-all-start) | async-done | bytes 3145760 | tf_op jit(solution)/shard_map/all_to_all | solution.py:12
  119.1 5.4 %all-to-all-start.4 = ((bf16[16,48,1024]{2,1,0:T(8,128)(2,1)}), bf16[16,48,1024]{2,1,0:T(8,128)(2,1)S(1)}, u32[]{:S(2)}, u32[]{:S(2)}) async-start(bf16[16,48,1024]{2,1,0:T(8,128)(2,1)} %bitcast.27), calls=%async_computation.5 | async-start | bytes 3145728 | tf_op jit(solution)/shard_map/all_to_all | solution.py:12
  124.5 0.5 collective-permute-start.5
  125.0 3.2 %fusion.98 = f32[768,1024]{1,0:T(8,128)S(1)} fusion(bf16[768,2048]{1,0:T(8,128)(2,1)} %param.8, bf16[768,768]{0,1:T(8,128)(2,1)} %copy-done.7, s32[768]{0:T(1024)S(1)} %fusion.84, s32[768]{0:T(1024)S(1)} %fusion.86), kind=kOutput, calls=%fused_computation.180 | convolution fusion | flops 1209139200 | bytes 5904384 | tf_op jit(solution)/shard_map/dot_general | solution.py:37
  128.2 33.1 %collective-permute-done.5 = bf16[768,1024]{1,0:T(8,128)(2,1)S(1)} collective-permute-done((bf16[768,1024]{1,0:T(8,128)(2,1)S(1)}, bf16[768,1024]{1,0:T(8,128)(2,1)S(1)}, u32[]{:S(2)}, u32[]{:S(2)}) %collective-permute-start.5) | collective-permute-done | bytes 1572896 | tf_op jit(solution)/shard_map/ppermute | solution.py:22
  161.3 2.5 add_convert_fusion.2
  163.9 17.2 %all-to-all-done.4 = bf16[16,48,1024]{2,1,0:T(8,128)(2,1)S(1)} async-done(((bf16[16,48,1024]{2,1,0:T(8,128)(2,1)}), bf16[16,48,1024]{2,1,0:T(8,128)(2,1)S(1)}, u32[]{:S(2)}, u32[]{:S(2)}) %all-to-all-start.4) | async-done | bytes 1572896 | tf_op jit(solution)/shard_map/all_to_all | solution.py:12
  181.1 10.0 %all-to-all-start.3 = ((bf16[16,48,1024]{2,1,0:T(8,128)(2,1)}), bf16[16,48,1024]{2,1,0:T(8,128)(2,1)S(1)}, u32[]{:S(2)}, u32[]{:S(2)}) async-start(bf16[16,48,1024]{2,1,0:T(8,128)(2,1)} %bitcast.99), calls=%async_computation.4 | async-start | bytes 3145728 | tf_op jit(solution)/shard_map/all_to_all | solution.py:12
  191.1 0.2 reduce-scatter.2.cloned.1.call-start
  191.4 7.8 %convolution_convert_fusion = bf16[768,1024]{1,0:T(8,128)(2,1)} fusion(bf16[768,2048]{1,0:T(8,128)(2,1)} %param.8, bf16[2048,1024]{1,0:T(8,128)(2,1)} %param.9), kind=kOutput, calls=%fused_computation.24 | convolution fusion | flops 3222011904 | bytes 8912896 | tf_op jit(solution)/shard_map/dot_general | solution.py:37
  199.1 0.6 broadcast_add_fusion
  199.8 8.7 %fusion.104 = f32[768,2048]{1,0:T(8,128)} fusion(bf16[768,1024]{1,0:T(8,128)(2,1)} %copy-done.5, bf16[2048,1024]{1,0:T(8,128)(2,1)} %param.9), kind=kOutput, calls=%fused_computation.186 | convolution fusion | flops 3221225472 | bytes 12058624 | tf_op jit(solution)/shard_map/dot_general | solution.py:37
  208.5 7.6 %fusion.13 = f32[768,2048]{1,0:T(8,128)} fusion(bf16[768,2048]{1,0:T(8,128)(2,1)} %bitcast.5, bf16[768,64]{0,1:T(8,128)(2,1)S(1)} %add_convert_fusion.3, s32[768]{0:T(1024)S(1)} %get-tuple-element.5, s32[768]{0:T(1024)S(1)} %get-tuple-element.35, s32[768]{0:T(1024)S(1)} %get-tuple-element.34), kind=kOutput, calls=%fused_computation.26 | convolution fusion | flops 2493235200 | bytes 9544704 | tf_op jit(solution)/shard_map/dot_general | solution.py:37
  216.1 0.3 reduce_sum.60
  216.5 0.7 fusion.101
  217.1 6.1 %all-to-all-done.3 = bf16[16,48,1024]{2,1,0:T(8,128)(2,1)S(1)} async-done(((bf16[16,48,1024]{2,1,0:T(8,128)(2,1)}), bf16[16,48,1024]{2,1,0:T(8,128)(2,1)S(1)}, u32[]{:S(2)}, u32[]{:S(2)}) %all-to-all-start.3) | async-done | bytes 1572896 | tf_op jit(solution)/shard_map/all_to_all | solution.py:12
  223.2 0.3 reduce_sum.59
  223.6 0.6 constant_dynamic-update-slice_fusion.7
  224.2 0.6 constant_dynamic-update-slice_fusion.6
  224.9 0.6 constant_dynamic-update-slice_fusion.5
  225.5 0.6 constant_dynamic-update-slice_fusion.4
  226.2 6.7 %fusion.17 = f32[768,64]{0,1:T(8,128)} fusion(bf16[768,2048]{1,0:T(8,128)(2,1)} %param.8, bf16[1,768,2048]{2,1,0:T(8,128)(2,1)} %all-gather.3.cloned.1.call-done, s32[768]{0:T(1024)S(1)} %get-tuple-element.5, s32[768]{0:T(1024)S(1)} %copy-done.12, s32[768]{0:T(1024)S(1)} %fusion.70), kind=kOutput, calls=%fused_computation.30 | convolution fusion | flops 2493235200 | bytes 6497280 | tf_op jit(solution)/shard_map/dot_general | solution.py:37
  232.9 5.2 %fusion.34 = bf16[768,64]{0,1:T(8,128)(2,1)S(1)} fusion(f32[768,64]{0,1:T(8,128)} %fusion.17, bf16[768,2048]{1,0:T(8,128)(2,1)} %bitcast.5, bf16[768,2048]{1,0:T(8,128)(2,1)S(1)} %copy-done.3, s32[768]{0:T(1024)S(1)} %get-tuple-element.5, s32[768]{0:T(1024)} %copy-done.16, s32[768]{0:T(1024)} %copy-done.15), kind=kOutput, calls=%fused_computation.45 | convolution fusion | flops 2493333504 | bytes 6595584 | tf_op jit(solution)/shard_map/dot_general | solution.py:37
  238.0 0.8 collective-permute-start
  238.8 0.6 constant_dynamic-update-slice_fusion.3
  239.5 0.3 collective-permute-done
  239.8 2.7 collective-permute-start.1
  242.5 0.6 constant_dynamic-update-slice_fusion.2
  243.2 2.7 collective-permute-done.1
  245.8 1.5 fusion
  247.4 2.2 fusion.5
  249.6 1.0 copy.17
  250.5 7.8 %all-to-all-start.5 = ((bf16[32,48,256]{2,1,0:T(8,128)(2,1)}), bf16[32,48,256]{2,1,0:T(8,128)(2,1)S(1)}, u32[]{:S(2)}, u32[]{:S(2)}) async-start(bf16[32,48,256]{2,1,0:T(8,128)(2,1)} %bitcast.38), calls=%async_computation.6 | async-start | bytes 1572864 | tf_op jit(solution)/shard_map/all_to_all | solution.py:12
  258.4 0.7 constant_dynamic-update-slice_fusion.1
  259.0 0.6 constant_dynamic-update-slice_fusion
  259.7 10.1 %add_convert_fusion = bf16[768,2048]{1,0:T(8,128)(2,1)} fusion(f32[768,2048]{1,0:T(8,128)} %fusion.104, f32[768,2048]{1,0:T(8,128)} %fusion.13, bf16[1,768,2048]{2,1,0:T(8,128)(2,1)} %all-gather.3.cloned.1.call-done, bf16[768,768]{0,1:T(8,128)(2,1)S(1)} %copy-done.8, s32[768]{0:T(1024)S(1)} %get-tuple-element.5, s32[768]{0:T(1024)S(1)} %copy-done.13), kind=kOutput, calls=%fused_computation | convolution fusion | flops 2421817344 | bytes 20060160 | tf_op jit(solution)/shard_map/dot_general | solution.py:37
  269.8 3.5 %fusion.15 = bf16[768,256]{1,0:T(8,128)(2,1)} fusion(bf16[768,1536]{1,0:T(8,128)(2,1)} %copy-done.21, bf16[1536,256]{1,0:T(8,128)(2,1)} %bitcast.22, bf16[768,256]{1,0:T(8,128)(2,1)} %reduce-scatter.2.cloned.1.call-done), kind=kOutput, calls=%fused_computation.29 | convolution fusion | flops 604766208 | bytes 3932160 | tf_op jit(solution)/shard_map/dot_general | solution.py:37
  273.2 5.8 %all-to-all-done.5 = bf16[32,48,256]{2,1,0:T(8,128)(2,1)S(1)} async-done(((bf16[32,48,256]{2,1,0:T(8,128)(2,1)}), bf16[32,48,256]{2,1,0:T(8,128)(2,1)S(1)}, u32[]{:S(2)}, u32[]{:S(2)}) %all-to-all-start.5) | async-done | bytes 786464 | tf_op jit(solution)/shard_map/all_to_all | solution.py:12
  279.1 0.6 pad_maximum_fusion.4
  (72 shorter events, 0.8 us)
Async XLA Ops:
  10.1 17.4 %all-to-all-start.2 = ((bf16[8,192,256]{2,1,0:T(8,128)(2,1)}), bf16[8,192,256]{2,1,0:T(8,128)(2,1)}, u32[]{:S(2)}, u32[]{:S(2)}) async-start(bf16[8,192,256]{2,1,0:T(8,128)(2,1)} %bitcast.21), calls=%async_computation.3 | async-start | bytes 1572864 | tf_op jit(solution)/shard_map/all_to_all | solution.py:12
  15.3 6.1 %copy-start = (bf16[3,64,8192]{2,1,0:T(8,128)(2,1)S(1)}, bf16[3,64,8192]{2,1,0:T(8,128)(2,1)}, u32[]{:S(2)}) copy-start(bf16[3,64,8192]{2,1,0:T(8,128)(2,1)} %param.10) | copy-start | bytes 9437188
  19.2 2.2 copy-start.14
  19.2 2.2 copy-start.17
  19.2 2.2 copy-start.18
  19.2 70.6 %collective-permute-start.6 = (bf16[768,1024]{1,0:T(8,128)(2,1)}, bf16[768,1024]{1,0:T(8,128)(2,1)}, u32[]{:S(2)}, u32[]{:S(2)}) collective-permute-start(bf16[768,1024]{1,0:T(8,128)(2,1)} %get-tuple-element.6), channel_id=1, source_target_pairs={{0,4},{4,0},{1,5},{5,1},{2,6},{6,2},{3,7},{7,3},{8,12},{12,8},{9,1... | collective-permute-start | bytes 4718600 | tf_op jit(solution)/shard_map/ppermute | solution.py:22
  24.4 9.2 %copy-start.1 = (bf16[1,192,2048]{2,1,0:T(8,128)(2,1)S(1)}, bf16[1,192,2048]{2,1,0:T(8,128)(2,1)}, u32[]{:S(2)}) copy-start(bf16[1,192,2048]{2,1,0:T(8,128)(2,1)} %get-tuple-element.8) | copy-start | bytes 2359300
  24.4 9.2 %copy-start.2 = (bf16[1,192,2048]{2,1,0:T(8,128)(2,1)S(1)}, bf16[1,192,2048]{2,1,0:T(8,128)(2,1)}, u32[]{:S(2)}) copy-start(bf16[1,192,2048]{2,1,0:T(8,128)(2,1)} %get-tuple-element.9) | copy-start | bytes 2359300
  30.0 47.5 %all-to-all-start.1 = ((bf16[8,48,2048]{2,1,0:T(8,128)(2,1)}), bf16[8,48,2048]{2,1,0:T(8,128)(2,1)S(1)}, u32[]{:S(2)}, u32[]{:S(2)}) async-start(bf16[8,48,2048]{2,1,0:T(8,128)(2,1)} %bitcast.12), calls=%async_computation.2 | async-start | bytes 3145728 | tf_op jit(solution)/shard_map/all_to_all | solution.py:12
  33.6 3.5 %copy-start.11 = (s32[1536]{0:T(1024)}, s32[1536]{0:T(1024)S(1)}, u32[]{:S(2)}) copy-start(s32[1536]{0:T(1024)S(1)} %get-tuple-element.37) | copy-start | bytes 18436
  33.6 3.1 %copy-start.4 = (bf16[768,1024]{1,0:T(8,128)(2,1)S(1)}, bf16[768,1024]{1,0:T(8,128)(2,1)}, u32[]{:S(2)}) copy-start(bf16[768,1024]{1,0:T(8,128)(2,1)} %param.12) | copy-start | bytes 4718596
  37.1 3.2 %copy-start.5 = (bf16[768,1024]{1,0:T(8,128)(2,1)}, bf16[768,1024]{1,0:T(8,128)(2,1)S(1)}, u32[]{:S(2)}) copy-start(bf16[768,1024]{1,0:T(8,128)(2,1)S(1)} %multiply_convert_fusion) | copy-start | bytes 4718596
  40.2 1.4 collective-permute-start.2
  41.7 40.6 %collective-permute-start.3 = (bf16[768,64]{0,1:T(8,128)(2,1)S(1)}, bf16[768,64]{0,1:T(8,128)(2,1)S(1)}, u32[]{:S(2)}, u32[]{:S(2)}) collective-permute-start(bf16[768,64]{0,1:T(8,128)(2,1)S(1)} %add_convert_fusion.4), channel_id=1, source_target_pairs={{0,2},{1,3},{2,0},{3,1},{4,6},{5,7},{6,4},{7,5},{8,10},{9,11},{10,... | collective-permute-start | bytes 294920 | tf_op jit(solution)/shard_map/ppermute | solution.py:30
  77.5 41.7 %all-to-all-start = ((bf16[4,192,2048]{2,1,0:T(8,128)(2,1)}), bf16[4,192,2048]{2,1,0:T(8,128)(2,1)}, u32[]{:S(2)}, u32[]{:S(2)}) async-start(bf16[4,192,2048]{2,1,0:T(8,128)(2,1)} %pad_maximum_fusion), calls=%async_computation.1 | async-start | bytes 6291456 | tf_op jit(solution)/shard_map/all_to_all | solution.py:12
  82.1 144.0 %all-gather.3.cloned.1.call-start = ((), (), s32[]{:S(2)}) async-start(), calls=%async_computation.8 | async-start | bytes 3932160 | tf_op jit(solution)/shard_map/all_gather | solution.py:101
  82.3 5.9 %collective-permute-start.4 = (bf16[768,66]{0,1:T(8,128)(2,1)S(1)}, bf16[768,66]{0,1:T(8,128)(2,1)S(1)}, u32[]{:S(2)}, u32[]{:S(2)}) collective-permute-start(bf16[768,66]{0,1:T(8,128)(2,1)S(1)} %pad_maximum_fusion.3), channel_id=1, source_target_pairs={{0,4},{4,0},{1,5},{5,1},{2,6},{6,2},{3,7},{7,3},{8,12},{12,8},{9,1... | collective-permute-start | bytes 304136 | tf_op jit(solution)/shard_map/ppermute | solution.py:22
  83.3 4.9 %copy-start.7 = (bf16[768,768]{0,1:T(8,128)(2,1)}, bf16[768,768]{0,1:T(8,128)(2,1)S(1)}, u32[]{:S(2)}) copy-start(bf16[768,768]{0,1:T(8,128)(2,1)S(1)} %fusion.41) | copy-start | bytes 3538948
  89.8 1.0 copy-start.19
  95.8 28.7 %copy-start.6 = (bf16[768,1024]{1,0:T(8,128)(2,1)S(1)}, bf16[768,1024]{1,0:T(8,128)(2,1)}, u32[]{:S(2)}) copy-start(bf16[768,1024]{1,0:T(8,128)(2,1)} %get-tuple-element.7) | copy-start | bytes 4718596
  119.1 61.9 %all-to-all-start.4 = ((bf16[16,48,1024]{2,1,0:T(8,128)(2,1)}), bf16[16,48,1024]{2,1,0:T(8,128)(2,1)S(1)}, u32[]{:S(2)}, u32[]{:S(2)}) async-start(bf16[16,48,1024]{2,1,0:T(8,128)(2,1)} %bitcast.27), calls=%async_computation.5 | async-start | bytes 3145728 | tf_op jit(solution)/shard_map/all_to_all | solution.py:12
  124.5 36.8 %copy-start.20 = (bf16[768,768]{0,1:T(8,128)(2,1)S(1)}, bf16[768,768]{0,1:T(8,128)(2,1)}, u32[]{:S(2)}) copy-start(bf16[768,768]{0,1:T(8,128)(2,1)} %copy-done.19) | copy-start | bytes 3538948
  124.5 36.8 %collective-permute-start.5 = (bf16[768,1024]{1,0:T(8,128)(2,1)S(1)}, bf16[768,1024]{1,0:T(8,128)(2,1)S(1)}, u32[]{:S(2)}, u32[]{:S(2)}) collective-permute-start(bf16[768,1024]{1,0:T(8,128)(2,1)S(1)} %copy-done.6), channel_id=1, source_target_pairs={{0,4},{4,0},{1,5},{5,1},{2,6},{6,2},{3,7},{7,3},{8,12},{12,8},{9,1... | collective-permute-start | bytes 4718600 | tf_op jit(solution)/shard_map/ppermute | solution.py:22
  181.1 42.1 %all-to-all-start.3 = ((bf16[16,48,1024]{2,1,0:T(8,128)(2,1)}), bf16[16,48,1024]{2,1,0:T(8,128)(2,1)S(1)}, u32[]{:S(2)}, u32[]{:S(2)}) async-start(bf16[16,48,1024]{2,1,0:T(8,128)(2,1)} %bitcast.99), calls=%async_computation.4 | async-start | bytes 3145728 | tf_op jit(solution)/shard_map/all_to_all | solution.py:12
  191.1 78.6 %reduce-scatter.2.cloned.1.call-start = ((), (), s32[]{:S(2)}) async-start(), calls=%async_computation.7 | async-start | bytes 1966080 | tf_op jit(solution)/shard_map/reduce_scatter | solution.py:124
  199.8 8.8 %copy-start.15 = (s32[768]{0:T(1024)}, s32[768]{0:T(1024)S(1)}, u32[]{:S(2)}) copy-start(s32[768]{0:T(1024)S(1)} %get-tuple-element.34) | copy-start | bytes 9220
  199.8 8.8 %copy-start.16 = (s32[768]{0:T(1024)}, s32[768]{0:T(1024)S(1)}, u32[]{:S(2)}) copy-start(s32[768]{0:T(1024)S(1)} %get-tuple-element.35) | copy-start | bytes 9220
  217.1 9.0 %copy-start.12 = (s32[768]{0:T(1024)S(1)}, s32[768]{0:T(1024)}, u32[]{:S(2)}) copy-start(s32[768]{0:T(1024)} %broadcast_add_fusion) | copy-start | bytes 9220
  226.2 6.7 %copy-start.3 = (bf16[768,2048]{1,0:T(8,128)(2,1)S(1)}, bf16[768,2048]{1,0:T(8,128)(2,1)}, u32[]{:S(2)}) copy-start(bf16[768,2048]{1,0:T(8,128)(2,1)} %param.8) | copy-start | bytes 9437188
  232.9 9.7 %copy-start.10 = (bf16[1,48,1024]{2,1,0:T(8,128)(2,1)S(1)}, bf16[1,48,1024]{2,1,0:T(8,128)(2,1)}, u32[]{:S(2)}) copy-start(bf16[1,48,1024]{2,1,0:T(8,128)(2,1)} %get-tuple-element.17) | copy-start | bytes 294916
  238.0 1.7 collective-permute-start
  239.8 6.0 %collective-permute-start.1 = (bf16[768,64]{0,1:T(8,128)(2,1)S(1)}, bf16[768,64]{0,1:T(8,128)(2,1)S(1)}, u32[]{:S(2)}, u32[]{:S(2)}) collective-permute-start(bf16[768,64]{0,1:T(8,128)(2,1)S(1)} %add_convert_fusion.6), channel_id=1, source_target_pairs={{0,2},{1,3},{2,0},{3,1},{4,6},{5,7},{6,4},{7,5},{8,10},{9,11},{10,... | collective-permute-start | bytes 294920 | tf_op jit(solution)/shard_map/ppermute | solution.py:30
  247.3 2.2 copy-start.21
  249.5 9.5 %copy-start.9 = (bf16[1,48,1024]{2,1,0:T(8,128)(2,1)S(1)}, bf16[1,48,1024]{2,1,0:T(8,128)(2,1)}, u32[]{:S(2)}) copy-start(bf16[1,48,1024]{2,1,0:T(8,128)(2,1)} %get-tuple-element.16) | copy-start | bytes 294916
  249.5 10.1 %copy-start.8 = (bf16[768,768]{0,1:T(8,128)(2,1)S(1)}, bf16[768,768]{0,1:T(8,128)(2,1)}, u32[]{:S(2)}) copy-start(bf16[768,768]{0,1:T(8,128)(2,1)} %copy-done.7) | copy-start | bytes 3538948
  249.5 10.1 %copy-start.13 = (s32[768]{0:T(1024)S(1)}, s32[768]{0:T(1024)}, u32[]{:S(2)}) copy-start(s32[768]{0:T(1024)} %broadcast_add_fusion) | copy-start | bytes 9220
  250.5 28.5 %all-to-all-start.5 = ((bf16[32,48,256]{2,1,0:T(8,128)(2,1)}), bf16[32,48,256]{2,1,0:T(8,128)(2,1)S(1)}, u32[]{:S(2)}, u32[]{:S(2)}) async-start(bf16[32,48,256]{2,1,0:T(8,128)(2,1)} %bitcast.38), calls=%async_computation.6 | async-start | bytes 1572864 | tf_op jit(solution)/shard_map/all_to_all | solution.py:12
Sparse Core Ops, SparseCore 0:
  89.4 95.6 all-gather.2
Sparse Core Ops, SparseCore 1:
  199.2 33.4 reduce-scatter.1
where the time goes:
time: 288 us; the launch traced here: 287 us
  waiting for transfers between devices  126 us (44%)
  matrix products  73 us (25%)
  starting transfers between devices  45.8 us (16%)
  local copies, waits for them, and re-layouts  19.3 us (7%)
  between operations  15.9 us (6%)
  other arithmetic  6.77 us (2%)
    all_to_all x6, waiting for transfers between devices, exchange(): return lax.all_to_all(pieces, axes, split_axis=0, concat_axis=0, tiled=True)  89.2 us
    dot_general x16, matrix products, dot(): lax.dot_general(a, b, (((ca,), (cb,)), ((), ())), preferred_element_type=...  73 us
    all_to_all x6, starting transfers between devices, exchange(): return lax.all_to_all(pieces, axes, split_axis=0, concat_axis=0, tiled=True)  36.7 us
    ppermute x3, waiting for transfers between devices, shift(): lax.ppermute(array, axis, [(i, (i + step) % size) for i in range(size)])  33.2 us
    ppermute x4, starting transfers between devices, tensor_sum(): other = lax.ppermute(total, 'tensor', [(i, i ^ bit) for i in range(size)])  5.91 us
  transfers between devices with their start and end apart: 15, of which 10 were waited for; matrix products, arithmetic and copies ran while one was open for 33% of the time, Pallas kernels for 0%

commit v1 on v0

v1 whole, which is shorter than its diff:
```python
import jax
import jax.numpy as jnp
from jax import lax
from jax.sharding import PartitionSpec as P

ADAPTER_SCALE = 0.5
CHUNKS = 2
SPLIT = 128


def exchange(pieces, axes):
    return lax.all_to_all(pieces, axes, split_axis=0, concat_axis=0, tiled=True)


def column_blocks(matrix, blocks):
    width = matrix.shape[1] // blocks
    return jnp.stack([matrix[:, i * width : (i + 1) * width] for i in range(blocks)])


def shift(array, axis, step):
    size = lax.axis_size(axis)
    return lax.ppermute(array, axis, [(i, (i + step) % size) for i in range(size)])


def tensor_sum(partial):
    size = lax.axis_size("tensor")
    total = partial
    bit = 1
    while bit < size:
        other = lax.ppermute(total, "tensor", [(i, i ^ bit) for i in range(size)])
        total = (total.astype(jnp.float32) + other.astype(jnp.float32)).astype(jnp.bfloat16)
        bit *= 2
    return total


def dot(a, b, ca, cb):
    return lax.dot_general(a, b, (((ca,), (cb,)), ((), ())), preferred_element_type=jnp.float32)


class Columns:
    def __init__(self, first, adapters, rank, parts):
        width = adapters * rank
        column = jnp.arange(width, dtype=jnp.int32)
        piece = rank // parts
        self.slot = first + (column % (adapters * piece)) // piece
        self.rank = (column // (adapters * piece)) * piece + column % piece
        self.select = (jnp.arange(rank, dtype=jnp.int32)[:, None] == self.rank[None, :]).astype(
            jnp.bfloat16
        )

    def spread(self, compact, slots):
        mine = slots[:, None] == self.slot[None, :]
        return jnp.where(mine, dot(compact, self.select, 1, 0), 0.0).astype(jnp.bfloat16)

    def gather(self, full, slots):
        mine = slots[:, None] == self.slot[None, :]
        return dot(jnp.where(mine, full, 0.0).astype(jnp.bfloat16), self.select, 1, 1).astype(
            jnp.bfloat16
        )


def after(value, *earlier):
    return lax.optimization_barrier((value,) + earlier)[0]


def scatter_columns(term):
    size = lax.axis_size("tensor")
    share = lax.axis_index("tensor")
    width = term.shape[1] // size
    blocks = [
        lax.dynamic_slice_in_dim(term, (share ^ i) * width, width, 1) for i in range(size)
    ]
    bit = 1
    while bit < size:
        pairs = [(i, i ^ bit) for i in range(size)]
        kept = [i for i in range(size) if i % (2 * bit) == 0]
        send = jnp.concatenate([blocks[i ^ bit] for i in kept], axis=1)
        got = lax.ppermute(send, "tensor", pairs)
        for n, i in enumerate(kept):
            blocks[i] = (
                blocks[i].astype(jnp.float32)
                + got[:, n * width : (n + 1) * width].astype(jnp.float32)
            ).astype(jnp.bfloat16)
        bit *= 2
    return blocks[0]


def shards(
    tokens,
    frozen_value_weight,
    adapter_down_weight,
    adapter_up_weight,
    cotangent,
    language_pair_index,
    language_pair_counts,
    adapter_owner_table,
):
    sides = lax.axis_size("adapter")
    shares = lax.axis_size("tensor")
    planes = lax.axis_size("dp")
    side = lax.axis_index("adapter")
    share = lax.axis_index("tensor")
    rows, width = tokens.shape
    stored, rank, _ = adapter_down_weight.shape
    values = cotangent.shape[1]
    value_width = values // shares
    own = shares * stored
    total = sides * own
    piece = rank // planes
    steps = range(1, sides)

    pairs = jnp.arange(adapter_owner_table.shape[0], dtype=jnp.int32)
    matches = language_pair_index[:, None] == pairs[None, :]
    slots = jnp.sum(jnp.where(matches, adapter_owner_table[None, :], 0), axis=1)
    row_counts = jnp.sum(jnp.where(matches, language_pair_counts[0][None, :], 0), axis=1)
    row_weight = 1.0 / row_counts.astype(jnp.float32)
    scaled = (cotangent.astype(jnp.float32) * row_weight[:, None]).astype(jnp.bfloat16)
    scaled_part = lax.dynamic_slice_in_dim(scaled, share * value_width, value_width, 1)

    tag_rows = -(-rows // value_width)
    tags = jnp.pad(slots, (0, tag_rows * value_width - rows)).reshape(tag_rows, value_width)
    tags = jnp.concatenate([tags // SPLIT, tags % SPLIT]).astype(jnp.bfloat16)
    tags = jnp.pad(tags, ((0, -2 * tag_rows % 16), (0, 0)))
    message = jnp.concatenate([scaled_part, tags])
    scaled_of, slots_of = [scaled_part], [slots]
    for j in steps:
        got = shift(message, "adapter", j)
        scaled_of.append(got[:rows])
        numbers = got[rows : rows + 2 * tag_rows].astype(jnp.int32)
        numbers = numbers[:tag_rows] * SPLIT + numbers[tag_rows:]
        slots_of.append(numbers.reshape(-1)[:rows])

    up_blocks = column_blocks(adapter_up_weight.reshape(stored * rank, values), shares)
    up_blocks = jnp.broadcast_to(up_blocks[None], (sides,) + up_blocks.shape)
    ups = exchange(
        up_blocks.reshape(sides * shares, stored * rank, value_width), ("adapter", "tensor")
    ).reshape(total * rank, value_width)
    own_ups = lax.dynamic_slice_in_dim(ups, side * own * rank, own * rank, 0)
    own_down = exchange(
        column_blocks(adapter_down_weight.reshape(stored * rank, shares * width), shares), "tensor"
    ).reshape(own * rank, width)

    chunk = width // CHUNKS
    token_chunks = []
    for c in range(CHUNKS):
        block = tokens[:, c * chunk : (c + 1) * chunk]
        token_chunks.append([block] + [shift(block, "adapter", j) for j in steps])
    crossed = token_chunks[-1][1:]
    other_downs = [shift(after(own_down, *crossed), "adapter", j) for j in steps]

    every = Columns(0, total, rank, 1)
    mine = Columns(side * own, own, rank, 1)
    mine_parts = Columns(side * own, own, rank, planes)
    others = [Columns(((side - j) % sides) * own, own, rank, 1) for j in steps]

    def over_tensor(parts):
        joined = tensor_sum(jnp.concatenate(parts, axis=1))
        return [joined[:, i * rank : (i + 1) * rank] for i in range(sides)]

    base_term = dot(tokens, frozen_value_weight, 1, 0).astype(jnp.bfloat16)
    base_share = scatter_columns(base_term)

    back_of = over_tensor(
        [
            mine.gather(ADAPTER_SCALE * dot(part, own_ups, 1, 1), numbers)
            for part, numbers in zip(scaled_of, slots_of)
        ]
    )
    spread_back = [mine_parts.spread(b, n) for b, n in zip(back_of, slots_of)]

    low_full = [0.0] * sides
    parts_down = []
    for c in range(CHUNKS):
        part = sum(dot(b, g, 0, 0) for b, g in zip(spread_back, token_chunks[c]))
        parts_down.append(part.astype(jnp.bfloat16))
        weights = own_down[:, c * chunk : (c + 1) * chunk]
        for i in range(sides):
            low_full[i] += dot(token_chunks[c][i], weights, 1, 1)
    low_of = over_tensor([mine.gather(f, n) for f, n in zip(low_full, slots_of)])
    up_part = ADAPTER_SCALE * sum(
        dot(mine_parts.spread(v, n), part, 0, 0)
        for v, n, part in zip(low_of, slots_of, scaled_of)
    )
    parts_down[-1] = jnp.concatenate([parts_down[-1], up_part.astype(jnp.bfloat16)], axis=1)

    sums = []
    for part in parts_down:
        columns = part.shape[1]
        got = exchange(part.reshape(planes * shares, stored * piece, columns), ("dp", "tensor"))
        got = got.reshape(planes, shares, stored * piece, columns)
        sums.append(jnp.sum(got.astype(jnp.float32), axis=0).astype(jnp.bfloat16))
    grad_down = jnp.concatenate(
        [sums[c][s][:, :chunk] for s in range(shares) for c in range(CHUNKS)], axis=1
    ).reshape(stored, piece, shares * width)
    grad_up = jnp.concatenate([sums[-1][s][:, chunk:] for s in range(shares)], axis=1).reshape(
        stored, piece, values
    )

    low, back = low_of[0], back_of[0]
    for j in steps:
        reply = shift(jnp.concatenate([low_of[j], back_of[j]], axis=1), "adapter", -j)
        low = low + reply[:, :rank]
        back = back + reply[:, rank:]
    delta = ADAPTER_SCALE * dot(every.spread(low, slots), ups, 1, 0)
    mixed_out = (base_share.astype(jnp.float32) + delta).astype(jnp.bfloat16)

    input_gradient = dot(scaled, frozen_value_weight, 1, 1)
    input_gradient += dot(mine.spread(back, slots), own_down, 1, 0)
    for columns, other_down in zip(others, other_downs):
        input_gradient += dot(columns.spread(back, slots), other_down, 1, 0)
    return mixed_out, input_gradient.astype(jnp.bfloat16), grad_down, grad_up


def solution(mesh):
    return jax.shard_map(
        shards,
        mesh=mesh,
        in_specs=(
            P(("dp", "adapter"), "tensor"),
            P("tensor", None),
            P(("adapter", "tensor"), None, None),
            P(("adapter", "tensor"), None, None),
            P(("dp", "adapter"), None),
            P(("dp", "adapter")),
            P(("dp", "adapter"), None),
            P(),
        ),
        out_specs=(
            P(("dp", "adapter"), "tensor"),
            P(("dp", "adapter"), "tensor"),
            P(("adapter", "tensor"), "dp", None),
            P(("adapter", "tensor"), "dp", None),
        ),
        check_vma=False,
    )
```

time: 288 us -> 227 us (0.79)
  waiting for transfers between devices: 126 us -> 81.8 us
  between operations: 15.9 us -> 1.19 us
  starting transfers between devices: 45.8 us -> 32.5 us
  other arithmetic: 6.77 us -> 17.3 us
  matrix products: 73 us -> 81.4 us
  local copies, waits for them, and re-layouts: 19.3 us -> 12.1 us
    all_to_all x6 -> x4, waiting for transfers between devices: 89.2 us -> 0.01 us  [exchange(): return lax.all_to_all(pieces, axes, split_axis=0, concat_axis=0, tiled=True)]
    ppermute x3 -> x5, waiting for transfers between devices: 33.2 us -> 57.9 us  [shift(): lax.ppermute(array, axis, [(i, (i + step) % size) for i in range(size)])]
    ppermute x4, waiting for transfers between devices: 3.88 us -> 23.9 us  [tensor_sum(): other = lax.ppermute(total, 'tensor', [(i, i ^ bit) for i in range(size)])]
    all_to_all x6 -> x4, starting transfers between devices: 36.7 us -> 23.5 us  [exchange(): return lax.all_to_all(pieces, axes, split_axis=0, concat_axis=0, tiled=True)]
    dot_general x16 -> x20, matrix products: 73 us -> 81.4 us  [dot(): lax.dot_general(a, b, (((ca,), (cb,)), ((), ())), preferred_element_type=...]
    concatenate x2 -> x8, other arithmetic: 0.67 us -> 6.52 us  [the longest x1 2.41 us: shards(): jnp.concatenate([parts_down[-1], up_part.astype(jnp.bfloat16)], axis=1)]
    convert_element_type x3 -> x4, other arithmetic: 0.08 us -> 3.62 us  [tensor_sum(): (total.astype(jnp.float32) + other.astype(jnp.float32)).astype(jnp.bfloat16)]
  transfers between devices with their start and end apart: 15 -> 15, of which waited for: 10 -> 5; matrix products, arithmetic and copies ran while one was open for 33% -> 46% of each run, Pallas kernels for 0% -> 0%
where the time goes in v1:
time: 227 us; the launch traced here: 226 us
  waiting for transfers between devices  81.8 us (36%)
  matrix products  81.4 us (36%)
  starting transfers between devices  32.5 us (14%)
  other arithmetic  17.3 us (8%)
  local copies, waits for them, and re-layouts  12.1 us (5%)
    dot_general x20, matrix products, dot(): lax.dot_general(a, b, (((ca,), (cb,)), ((), ())), preferred_element_type=...  81.4 us
    ppermute x5, waiting for transfers between devices, shift(): lax.ppermute(array, axis, [(i, (i + step) % size) for i in range(size)])  57.9 us
    ppermute x4, waiting for transfers between devices, tensor_sum(): other = lax.ppermute(total, 'tensor', [(i, i ^ bit) for i in range(size)])  23.9 us
    all_to_all x4, starting transfers between devices, exchange(): return lax.all_to_all(pieces, axes, split_axis=0, concat_axis=0, tiled=True)  23.5 us
  transfers between devices with their start and end apart: 15, of which 5 were waited for; matrix products, arithmetic and copies ran while one was open for 46% of the time, Pallas kernels for 0%

profile of v1, /device:TPU:0, one launch (start us, length us, event | category | flops | bytes accessed | tf_op | source)
XLA Modules:
  0.0 226.3 jit_solution(8231157520305683299)
XLA Ops:
  0.7 1.2 slice_bitcast_fusion.11
  1.9 0.9 broadcast_in_dim.44
  2.9 5.2 %all-to-all-start.1 = ((bf16[8,192,256]{2,1,0:T(8,128)(2,1)}), bf16[8,192,256]{2,1,0:T(8,128)(2,1)}, u32[]{:S(2)}, u32[]{:S(2)}) async-start(bf16[8,192,256]{2,1,0:T(8,128)(2,1)} %bitcast.14), calls=%async_computation.1 | async-start | bytes 1572864 | tf_op jit(solution)/shard_map/all_to_all | solution.py:12
  8.2 0.3 multiply_convert_fusion
  8.6 1.2 copy-done.2
  9.8 0.8 pad_maximum_fusion.3
  10.6 2.0 collective-permute-start.2
  12.6 2.0 fusion.159
  14.7 2.1 slice_bitcast_fusion.3
  16.8 1.9 pad_maximum_fusion
  18.7 10.2 %collective-permute-done.2 = bf16[784,256]{1,0:T(8,128)(2,1)} collective-permute-done((bf16[784,256]{1,0:T(8,128)(2,1)}, bf16[784,256]{1,0:T(8,128)(2,1)}, u32[]{:S(2)}, u32[]{:S(2)}) %collective-permute-start.2) | collective-permute-done | bytes 401440 | tf_op jit(solution)/shard_map/ppermute | solution.py:22
  28.9 0.7 slice_convert_fusion
  29.6 4.7 %all-to-all-start = ((bf16[4,192,2048]{2,1,0:T(8,128)(2,1)}), bf16[4,192,2048]{2,1,0:T(8,128)(2,1)}, u32[]{:S(2)}, u32[]{:S(2)}) async-start(bf16[4,192,2048]{2,1,0:T(8,128)(2,1)} %pad_maximum_fusion), calls=%async_computation | async-start | bytes 6291456 | tf_op jit(solution)/shard_map/all_to_all | solution.py:12
  34.2 2.5 %fusion.65 = bf16[768,64]{0,1:T(8,128)(2,1)} fusion(bf16[768,256]{1,0:T(8,128)(2,1)S(1)} %constant_dynamic-slice_fusion, s32[768]{0:T(1024)S(1)} %get-tuple-element.31, s32[768]{0:T(1024)S(1)} %get-tuple-element.7, bf16[1536,256]{1,0:T(8,128)(2,1)} %bitcast.15, s32[]{:T(128)S(6)} %select_n.218, s32[768]{0:T(1024)S(1)} %get-tuple-element.30), kind=kOutput, calls=%fused_computation.74 | convolution fusion | flops 379944960 | bytes 893956 | tf_op jit(solution)/shard_map/dot_general | solution.py:37
  36.7 2.7 %fusion.64 = bf16[768,64]{0,1:T(8,128)(2,1)} fusion(s32[768]{0:T(1024)S(1)} %get-tuple-element.31, s32[768]{0:T(1024)S(1)} %eq.232, bf16[784,256]{1,0:T(8,128)(2,1)} %collective-permute-done.2, bf16[1536,256]{1,0:T(8,128)(2,1)} %bitcast.15, s32[]{:T(128)S(6)} %select_n.218, s32[768]{0:T(1024)S(1)} %get-tuple-element.30), kind=kOutput, calls=%fused_computation.73 | convolution fusion | flops 379944960 | bytes 893956 | tf_op jit(solution)/shard_map/dot_general | solution.py:37
  39.4 1.6 pad_maximum_fusion.6
  41.1 0.4 collective-permute-start.7
  41.5 6.7 %convolution_convert_fusion = bf16[768,1024]{1,0:T(8,128)(2,1)} fusion(bf16[768,2048]{1,0:T(8,128)(2,1)S(1)} %copy-done.1, bf16[2048,1024]{1,0:T(8,128)(2,1)} %param.9), kind=kOutput, calls=%fused_computation.26 | convolution fusion | flops 3222011904 | bytes 8912896 | tf_op jit(solution)/shard_map/dot_general | solution.py:37
  48.2 1.2 constant_dynamic-slice_fusion.2
  49.4 1.8 add_convert_fusion.8
  51.1 1.7 collective-permute-start.8
  52.8 0.9 pad_maximum_fusion.2
  54.0 21.5 %collective-permute-done.8 = bf16[768,128]{0,1:T(8,128)(2,1)} collective-permute-done((bf16[768,128]{0,1:T(8,128)(2,1)}, bf16[768,128]{0,1:T(8,128)(2,1)}, u32[]{:S(2)}, u32[]{:S(2)}) %collective-permute-start.8) | collective-permute-done | bytes 196640 | tf_op jit(solution)/shard_map/ppermute | solution.py:30
  75.5 1.1 add_convert_fusion.7
  76.5 0.5 fusion.4
  77.1 0.1 copy-done.4
  77.2 0.5 fusion.2
  77.7 1.4 fusion.156
  79.2 4.1 %add_convert_fusion.2 = bf16[768,1024]{1,0:T(8,128)(2,1)} fusion(f32[768,1024]{1,0:T(8,128)S(1)} %fusion.156, bf16[768,768]{1,0:T(8,128)(2,1)S(1)} %fusion.4, bf16[768,1024]{1,0:T(8,128)(2,1)} %collective-permute-done.3), kind=kOutput, calls=%fused_computation.7 | convolution fusion | flops 1209532416 | bytes 7471104 | tf_op jit(solution)/shard_map/dot_general | solution.py:37
  83.3 5.4 %all-to-all-start.2 = ((bf16[16,48,1024]{2,1,0:T(8,128)(2,1)}), bf16[16,48,1024]{2,1,0:T(8,128)(2,1)S(1)}, u32[]{:S(2)}, u32[]{:S(2)}) async-start(bf16[16,48,1024]{2,1,0:T(8,128)(2,1)} %bitcast.16), calls=%async_computation.2 | async-start | bytes 3145728 | tf_op jit(solution)/shard_map/all_to_all | solution.py:12
  88.7 7.1 %collective-permute-done.4 = bf16[768,1024]{1,0:T(8,128)(2,1)} collective-permute-done((bf16[768,1024]{1,0:T(8,128)(2,1)}, bf16[768,1024]{1,0:T(8,128)(2,1)}, u32[]{:S(2)}, u32[]{:S(2)}) %collective-permute-start.4) | collective-permute-done | bytes 1572896 | tf_op jit(solution)/shard_map/ppermute | solution.py:22
  95.8 4.7 %fusion.14 = f32[768,768]{0,1:T(8,128)} fusion(bf16[768,1024]{1,0:T(8,128)(2,1)} %collective-permute-done.4, bf16[768,2048]{1,0:T(8,128)(2,1)} %bitcast.5), kind=kOutput, calls=%fused_computation.32 | convolution fusion | flops 1207959552 | bytes 5505024 | tf_op jit(solution)/shard_map/dot_general | solution.py:37
  100.5 4.7 %fusion.58 = bf16[768,64]{0,1:T(8,128)(2,1)S(1)} fusion(f32[768,768]{0,1:T(8,128)} %fusion.14, bf16[768,1024]{1,0:T(8,128)(2,1)} %collective-permute-done.3, bf16[768,2048]{1,0:T(8,128)(2,1)} %bitcast.5, s32[768]{0:T(1024)S(1)} %get-tuple-element.31, s32[768]{0:T(1024)S(1)} %eq.232, s32[768]{0:T(1024)S(1)} %get-tuple-element.30), kind=kOutput, calls=%fused_computation.71 | convolution fusion | flops 1285914624 | bytes 5612544 | tf_op jit(solution)/shard_map/dot_general | solution.py:37
  105.3 4.7 %fusion.18 = f32[768,768]{0,1:T(8,128)} fusion(bf16[768,2048]{1,0:T(8,128)(2,1)} %bitcast.5, bf16[768,2048]{1,0:T(8,128)(2,1)} %param.8), kind=kOutput, calls=%fused_computation.36 | convolution fusion | flops 1207959552 | bytes 5505024 | tf_op jit(solution)/shard_map/dot_general | solution.py:37
  110.0 4.7 %fusion.61 = bf16[768,64]{0,1:T(8,128)(2,1)S(1)} fusion(f32[768,768]{0,1:T(8,128)} %fusion.18, bf16[768,2048]{1,0:T(8,128)(2,1)} %bitcast.5, s32[768]{0:T(1024)S(1)} %get-tuple-element.31, s32[768]{0:T(1024)S(1)} %get-tuple-element.7, s32[768]{0:T(1024)S(1)} %get-tuple-element.30, bf16[768,2048]{1,0:T(8,128)(2,1)} %param.8), kind=kOutput, calls=%fused_computation.72 | convolution fusion | flops 1285914624 | bytes 5612544 | tf_op jit(solution)/shard_map/dot_general | solution.py:37
  114.8 3.3 %fusion.152 = f32[768,1024]{1,0:T(8,128)S(1)} fusion(bf16[768,768]{1,0:T(8,128)(2,1)} %copy-done.21, bf16[768,2048]{1,0:T(8,128)(2,1)} %param.8), kind=kOutput, calls=%fused_computation.233 | convolution fusion | flops 1207959552 | bytes 5898240 | tf_op jit(solution)/shard_map/dot_general | solution.py:37
  118.2 1.5 collective-permute-start.6
  119.7 2.9 %add_convert_fusion.1 = bf16[768,1024]{1,0:T(8,128)(2,1)S(1)} fusion(f32[768,1024]{1,0:T(8,128)S(1)} %fusion.152, bf16[768,768]{1,0:T(8,128)(2,1)S(1)} %copy-done.20, bf16[768,1024]{1,0:T(8,128)(2,1)} %collective-permute-done.4), kind=kOutput, calls=%fused_computation.6 | convolution fusion | flops 1209532416 | bytes 7471104 | tf_op jit(solution)/shard_map/dot_general | solution.py:37
  122.6 0.6 collective-permute-start.10
  123.3 2.4 %collective-permute-done.6 = bf16[768,128]{0,1:T(8,128)(2,1)S(1)} collective-permute-done((bf16[768,128]{0,1:T(8,128)(2,1)S(1)}, bf16[768,128]{0,1:T(8,128)(2,1)S(1)}, u32[]{:S(2)}, u32[]{:S(2)}) %collective-permute-start.6) | collective-permute-done | bytes 196640 | tf_op jit(solution)/shard_map/ppermute | solution.py:30
  125.7 0.7 add_convert_fusion.9
  126.4 2.9 %fusion.12 = f32[768,256]{1,0:T(8,128)} fusion(s32[768]{0:T(1024)} %copy-done.15, s32[768]{0:T(1024)S(1)} %eq.232, bf16[784,256]{1,0:T(8,128)(2,1)} %collective-permute-done.2, s32[768]{0:T(1024)S(1)} %copy-done.14, bf16[768,128]{0,1:T(8,128)(2,1)} %add_convert_fusion.9), kind=kOutput, calls=%fused_computation.30 | convolution fusion | flops 379305984 | bytes 1288192 | tf_op jit(solution)/shard_map/dot_general | solution.py:37
  129.3 2.9 %fusion.23 = bf16[768,256]{1,0:T(8,128)(2,1)} fusion(f32[768,256]{1,0:T(8,128)} %fusion.12, bf16[768,256]{1,0:T(8,128)(2,1)S(1)} %constant_dynamic-slice_fusion, s32[768]{0:T(1024)} %copy-done.15, s32[768]{0:T(1024)S(1)} %get-tuple-element.7, s32[768]{0:T(1024)S(1)} %copy-done.14, bf16[768,128]{0,1:T(8,128)(2,1)} %add_convert_fusion.9), kind=kOutput, calls=%fused_computation.41 | convolution fusion | flops 379895808 | bytes 1681408 | tf_op jit(solution)/shard_map/dot_general | solution.py:37
  132.3 2.4 %pad_maximum_fusion.1 = bf16[768,1280]{1,0:T(8,128)(2,1)} fusion(bf16[768,256]{1,0:T(8,128)(2,1)} %fusion.23, bf16[768,1024]{1,0:T(8,128)(2,1)S(1)} %add_convert_fusion.1), kind=kLoop, calls=%fused_computation.25 | loop fusion | flops 3932160 | bytes 3932160 | tf_op jit(solution)/shard_map/concatenate | solution.py:184
  134.7 8.2 %all-to-all-start.3 = ((bf16[16,48,1280]{2,1,0:T(8,128)(2,1)}), bf16[16,48,1280]{2,1,0:T(8,128)(2,1)S(1)}, u32[]{:S(2)}, u32[]{:S(2)}) async-start(bf16[16,48,1280]{2,1,0:T(8,128)(2,1)} %bitcast.19), calls=%async_computation.3 | async-start | bytes 3932160 | tf_op jit(solution)/shard_map/all_to_all | solution.py:12
  142.9 8.8 %fusion.161 = f32[768,2048]{1,0:T(8,128)} fusion(bf16[768,1024]{1,0:T(8,128)(2,1)} %copy-done.2, bf16[2048,1024]{1,0:T(8,128)(2,1)} %param.9), kind=kOutput, calls=%fused_computation.241 | convolution fusion | flops 3221225472 | bytes 12058624 | tf_op jit(solution)/shard_map/dot_general | solution.py:37
  151.8 1.2 add_convert_fusion.5
  153.0 2.0 collective-permute-start.1
  155.0 0.5 collective-permute-start.9
  155.5 0.6 fusion.125
  156.1 0.6 add_select_fusion.1
  156.7 40.6 %collective-permute-done.9 = bf16[768,128]{0,1:T(8,128)(2,1)S(1)} collective-permute-done((bf16[768,128]{0,1:T(8,128)(2,1)S(1)}, bf16[768,128]{0,1:T(8,128)(2,1)S(1)}, u32[]{:S(2)}, u32[]{:S(2)}) %collective-permute-start.9) | collective-permute-done | bytes 196640 | tf_op jit(solution)/shard_map/ppermute | solution.py:22
  197.3 1.6 fusion.75
  198.9 0.7 copy-done.18
  199.6 3.9 %add_convert_fusion.3 = bf16[768,256]{1,0:T(8,128)(2,1)} fusion(bf16[768,256]{1,0:T(8,128)(2,1)} %copy-done.18, bf16[768,512]{1,0:T(8,128)(2,1)} %collective-permute-done, bf16[1536,256]{1,0:T(8,128)(2,1)} %bitcast.15, s32[1536]{0:T(1024)S(1)} %get-tuple-element.32, s32[768]{0:T(1024)S(1)} %get-tuple-element.7, ...), kind=kOutput, calls=%fused_computation.80 | convolution fusion | flops 761020416 | bytes 2573316 | tf_op jit(solution)/shard_map/dot_general | solution.py:37
  203.5 7.6 %fusion.30 = f32[768,2048]{1,0:T(8,128)} fusion(bf16[768,2048]{1,0:T(8,128)(2,1)} %bitcast.5, bf16[768,768]{1,0:T(8,128)(2,1)} %fusion.75, s32[768]{0:T(1024)S(1)} %copy-done.12, s32[768]{0:T(1024)S(1)} %get-tuple-element.7), kind=kOutput, calls=%fused_computation.44 | convolution fusion | flops 2417098752 | bytes 10622976 | tf_op jit(solution)/shard_map/dot_general | solution.py:37
  211.0 1.1 reduce_sum.44
  212.2 1.1 fusion.160
  213.2 0.6 constant_dynamic-update-slice_fusion.7
  213.9 10.2 %add_convert_fusion = bf16[768,2048]{1,0:T(8,128)(2,1)} fusion(f32[768,2048]{1,0:T(8,128)} %fusion.161, f32[768,2048]{1,0:T(8,128)} %fusion.30, bf16[768,2048]{1,0:T(8,128)(2,1)} %collective-permute-done.10, bf16[768,768]{1,0:T(8,128)(2,1)} %fusion.75, s32[768]{0:T(1024)S(1)} %copy-done.9, s32[768]{0:T(1024)S(1)} %get-tuple-element.7), kind=kOutput, calls=%fused_computation | convolution fusion | flops 2421817344 | bytes 20060160 | tf_op jit(solution)/shard_map/dot_general | solution.py:37
  224.1 0.5 reduce_sum.45
  224.8 0.4 copy-done.7
  225.4 0.7 pad_maximum_fusion.8
  226.1 0.2 copy-done.8
  (87 shorter events, 1.0 us)
Async XLA Ops:
  0.6 7.4 %copy-start.17 = (s32[24]{0:T(128)S(1)}, s32[24]{0:T(128)}, u32[]{:S(2)}) copy-start(s32[24]{0:T(128)} %param.15) | copy-start | bytes 292
  0.6 7.4 %copy-start.16 = (s32[1,24]{1,0:T(1,128)S(1)}, s32[1,24]{1,0:T(1,128)}, u32[]{:S(2)}) copy-start(s32[1,24]{1,0:T(1,128)} %param.14) | copy-start | bytes 292
  0.7 7.4 %copy-start.10 = (s32[768]{0:T(1024)S(1)}, s32[768]{0:T(1024)}, u32[]{:S(2)}) copy-start(s32[768]{0:T(1024)} %param.13) | copy-start | bytes 9220
  0.7 7.6 %copy-start.3 = (bf16[768,1024]{1,0:T(8,128)(2,1)S(1)}, bf16[768,1024]{1,0:T(8,128)(2,1)}, u32[]{:S(2)}) copy-start(bf16[768,1024]{1,0:T(8,128)(2,1)} %param.12) | copy-start | bytes 4718596
  2.9 26.7 %all-to-all-start.1 = ((bf16[8,192,256]{2,1,0:T(8,128)(2,1)}), bf16[8,192,256]{2,1,0:T(8,128)(2,1)}, u32[]{:S(2)}, u32[]{:S(2)}) async-start(bf16[8,192,256]{2,1,0:T(8,128)(2,1)} %bitcast.14), calls=%async_computation.1 | async-start | bytes 1572864 | tf_op jit(solution)/shard_map/all_to_all | solution.py:12
  8.2 4.4 %copy-start = (bf16[768,2048]{1,0:T(8,128)(2,1)S(1)}, bf16[768,2048]{1,0:T(8,128)(2,1)}, u32[]{:S(2)}) copy-start(bf16[768,2048]{1,0:T(8,128)(2,1)} %param.8) | copy-start | bytes 9437188
  8.6 1.2 copy-start.2
  10.6 18.3 %collective-permute-start.2 = (bf16[784,256]{1,0:T(8,128)(2,1)}, bf16[784,256]{1,0:T(8,128)(2,1)}, u32[]{:S(2)}, u32[]{:S(2)}) collective-permute-start(bf16[784,256]{1,0:T(8,128)(2,1)} %pad_maximum_fusion.3), channel_id=1, source_target_pairs={{0,4},{4,0},{1,5},{5,1},{2,6},{6,2},{3,7},{7,3},{8,12},{12,8},{9,1... | collective-permute-start | bytes 1204232 | tf_op jit(solution)/shard_map/ppermute | solution.py:22
  14.6 64.6 %collective-permute-start.3 = (bf16[768,1024]{1,0:T(8,128)(2,1)}, bf16[768,1024]{1,0:T(8,128)(2,1)}, u32[]{:S(2)}, u32[]{:S(2)}) collective-permute-start(bf16[768,1024]{1,0:T(8,128)(2,1)} %get-tuple-element.8), channel_id=1, source_target_pairs={{0,4},{4,0},{1,5},{5,1},{2,6},{6,2},{3,7},{7,3},{8,12},{12,8},{9,1... | collective-permute-start | bytes 4718600 | tf_op jit(solution)/shard_map/ppermute | solution.py:22
  16.8 93.2 %copy-start.11 = (s32[768]{0:T(1024)}, s32[768]{0:T(1024)S(1)}, u32[]{:S(2)}) copy-start(s32[768]{0:T(1024)S(1)} %get-tuple-element.31) | copy-start | bytes 9220
  29.6 53.7 %all-to-all-start = ((bf16[4,192,2048]{2,1,0:T(8,128)(2,1)}), bf16[4,192,2048]{2,1,0:T(8,128)(2,1)}, u32[]{:S(2)}, u32[]{:S(2)}) async-start(bf16[4,192,2048]{2,1,0:T(8,128)(2,1)} %pad_maximum_fusion), calls=%async_computation | async-start | bytes 6291456 | tf_op jit(solution)/shard_map/all_to_all | solution.py:12
  36.7 4.8 %copy-start.1 = (bf16[768,2048]{1,0:T(8,128)(2,1)S(1)}, bf16[768,2048]{1,0:T(8,128)(2,1)}, u32[]{:S(2)}) copy-start(bf16[768,2048]{1,0:T(8,128)(2,1)} %param.8) | copy-start | bytes 9437188
  41.1 8.3 %collective-permute-start.7 = (bf16[768,128]{0,1:T(8,128)(2,1)}, bf16[768,128]{0,1:T(8,128)(2,1)}, u32[]{:S(2)}, u32[]{:S(2)}) collective-permute-start(bf16[768,128]{0,1:T(8,128)(2,1)} %pad_maximum_fusion.6), channel_id=1, source_target_pairs={{0,1},{1,0},{2,3},{3,2},{4,5},{5,4},{6,7},{7,6},{8,9},{9,8},{10,11... | collective-permute-start | bytes 589832 | tf_op jit(solution)/shard_map/ppermute | solution.py:30
  51.1 24.3 %collective-permute-start.8 = (bf16[768,128]{0,1:T(8,128)(2,1)}, bf16[768,128]{0,1:T(8,128)(2,1)}, u32[]{:S(2)}, u32[]{:S(2)}) collective-permute-start(bf16[768,128]{0,1:T(8,128)(2,1)} %add_convert_fusion.8), channel_id=1, source_target_pairs={{0,2},{1,3},{2,0},{3,1},{4,6},{5,7},{6,4},{7,5},{8,10},{9,11},{10,... | collective-permute-start | bytes 589832 | tf_op jit(solution)/shard_map/ppermute | solution.py:30
  53.8 98.0 %collective-permute-start = (bf16[768,512]{1,0:T(8,128)(2,1)}, bf16[768,512]{1,0:T(8,128)(2,1)}, u32[]{:S(2)}, u32[]{:S(2)}) collective-permute-start(bf16[768,512]{1,0:T(8,128)(2,1)} %pad_maximum_fusion.2), channel_id=1, source_target_pairs={{0,1},{1,0},{2,3},{3,2},{4,5},{5,4},{6,7},{7,6},{8,9},{9,8},{10,11... | collective-permute-start | bytes 2359304 | tf_op jit(solution)/shard_map/ppermute | solution.py:78
  53.8 42.0 %collective-permute-start.4 = (bf16[768,1024]{1,0:T(8,128)(2,1)}, bf16[768,1024]{1,0:T(8,128)(2,1)}, u32[]{:S(2)}, u32[]{:S(2)}) collective-permute-start(bf16[768,1024]{1,0:T(8,128)(2,1)} %get-tuple-element.9), channel_id=1, source_target_pairs={{0,4},{4,0},{1,5},{5,1},{2,6},{6,2},{3,7},{7,3},{8,12},{12,8},{9,1... | collective-permute-start | bytes 4718600 | tf_op jit(solution)/shard_map/ppermute | solution.py:22
  54.0 23.1 %copy-start.13 = (s32[768]{0:T(1024)}, s32[768]{0:T(1024)S(1)}, u32[]{:S(2)}) copy-start(s32[768]{0:T(1024)S(1)} %get-tuple-element.34) | copy-start | bytes 9220
  54.0 23.1 %copy-start.15 = (s32[768]{0:T(1024)}, s32[768]{0:T(1024)S(1)}, u32[]{:S(2)}) copy-start(s32[768]{0:T(1024)S(1)} %get-tuple-element.35) | copy-start | bytes 9220
  76.5 0.7 copy-start.4
  77.2 2.0 copy-start.19
  77.7 1.5 copy-start.21
  83.3 51.4 %all-to-all-start.2 = ((bf16[16,48,1024]{2,1,0:T(8,128)(2,1)}), bf16[16,48,1024]{2,1,0:T(8,128)(2,1)S(1)}, u32[]{:S(2)}, u32[]{:S(2)}) async-start(bf16[16,48,1024]{2,1,0:T(8,128)(2,1)} %bitcast.16), calls=%async_computation.2 | async-start | bytes 3145728 | tf_op jit(solution)/shard_map/all_to_all | solution.py:12
  114.8 5.0 %copy-start.20 = (bf16[768,768]{1,0:T(8,128)(2,1)S(1)}, bf16[768,768]{1,0:T(8,128)(2,1)}, u32[]{:S(2)}) copy-start(bf16[768,768]{1,0:T(8,128)(2,1)} %copy-done.19) | copy-start | bytes 3538948
  114.8 3.4 %collective-permute-start.5 = (bf16[768,128]{0,1:T(8,128)(2,1)S(1)}, bf16[768,128]{0,1:T(8,128)(2,1)S(1)}, u32[]{:S(2)}, u32[]{:S(2)}) collective-permute-start(bf16[768,128]{0,1:T(8,128)(2,1)S(1)} %pad_maximum_fusion.5), channel_id=1, source_target_pairs={{0,1},{1,0},{2,3},{3,2},{4,5},{5,4},{6,7},{7,6},{8,9},{9,8},{10,11... | collective-permute-start | bytes 589832 | tf_op jit(solution)/shard_map/ppermute | solution.py:30
  118.2 8.2 %copy-start.14 = (s32[768]{0:T(1024)S(1)}, s32[768]{0:T(1024)}, u32[]{:S(2)}) copy-start(s32[768]{0:T(1024)} %copy-done.13) | copy-start | bytes 9220
  118.2 7.5 %collective-permute-start.6 = (bf16[768,128]{0,1:T(8,128)(2,1)S(1)}, bf16[768,128]{0,1:T(8,128)(2,1)S(1)}, u32[]{:S(2)}, u32[]{:S(2)}) collective-permute-start(bf16[768,128]{0,1:T(8,128)(2,1)S(1)} %add_convert_fusion.10), channel_id=1, source_target_pairs={{0,2},{1,3},{2,0},{3,1},{4,6},{5,7},{6,4},{7,5},{8,10},{9,11},{10,... | collective-permute-start | bytes 589832 | tf_op jit(solution)/shard_map/ppermute | solution.py:30
  122.6 91.2 %collective-permute-start.10 = (bf16[768,2048]{1,0:T(8,128)(2,1)}, bf16[768,2048]{1,0:T(8,128)(2,1)}, u32[]{:S(2)}, u32[]{:S(2)}) collective-permute-start(bf16[768,2048]{1,0:T(8,128)(2,1)} %bitcast.5), channel_id=1, source_target_pairs={{0,4},{4,0},{1,5},{5,1},{2,6},{6,2},{3,7},{7,3},{8,12},{12,8},{9,1... | collective-permute-start | bytes 9437192 | tf_op jit(solution)/shard_map/ppermute | solution.py:22
  134.7 89.4 %all-to-all-start.3 = ((bf16[16,48,1280]{2,1,0:T(8,128)(2,1)}), bf16[16,48,1280]{2,1,0:T(8,128)(2,1)S(1)}, u32[]{:S(2)}, u32[]{:S(2)}) async-start(bf16[16,48,1280]{2,1,0:T(8,128)(2,1)} %bitcast.19), calls=%async_computation.3 | async-start | bytes 3932160 | tf_op jit(solution)/shard_map/all_to_all | solution.py:12
  142.9 12.1 %slice-start = ((bf16[768,128]{0,1:T(8,128)(2,1)}), bf16[768,64]{0,1:T(8,128)(2,1)S(1)}, s32[]{:S(2)}) async-start(bf16[768,128]{0,1:T(8,128)(2,1)} %copy-done.4), calls=%async_computation.4 | async-start | bytes 196608 | tf_op jit(solution)/shard_map/slice | solution.py:158
  142.9 12.1 %slice-start.1 = ((bf16[768,128]{0,1:T(8,128)(2,1)}), bf16[768,64]{0,1:T(8,128)(2,1)S(1)}, s32[]{:S(2)}) async-start(bf16[768,128]{0,1:T(8,128)(2,1)} %add_convert_fusion.9), calls=%async_computation.5 | async-start | bytes 196608 | tf_op jit(solution)/shard_map/slice | solution.py:158
  142.9 54.4 %copy-start.5 = (bf16[768,128]{0,1:T(8,128)(2,1)S(1)}, bf16[768,128]{0,1:T(8,128)(2,1)}, u32[]{:S(2)}) copy-start(bf16[768,128]{0,1:T(8,128)(2,1)} %copy-done.4) | copy-start | bytes 589828
  153.0 45.9 %collective-permute-start.1 = (bf16[768,256]{1,0:T(8,128)(2,1)S(1)}, bf16[768,256]{1,0:T(8,128)(2,1)S(1)}, u32[]{:S(2)}, u32[]{:S(2)}) collective-permute-start(bf16[768,256]{1,0:T(8,128)(2,1)S(1)} %add_convert_fusion.5), channel_id=1, source_target_pairs={{0,2},{1,3},{2,0},{3,1},{4,6},{5,7},{6,4},{7,5},{8,10},{9,11},{10,... | collective-permute-start | bytes 1179656 | tf_op jit(solution)/shard_map/ppermute | solution.py:78
  155.0 42.3 %collective-permute-start.9 = (bf16[768,128]{0,1:T(8,128)(2,1)S(1)}, bf16[768,128]{0,1:T(8,128)(2,1)S(1)}, u32[]{:S(2)}, u32[]{:S(2)}) collective-permute-start(bf16[768,128]{0,1:T(8,128)(2,1)S(1)} %pad_maximum_fusion.7), channel_id=1, source_target_pairs={{0,4},{4,0},{1,5},{5,1},{2,6},{6,2},{3,7},{7,3},{8,12},{12,8},{9,1... | collective-permute-start | bytes 589832 | tf_op jit(solution)/shard_map/ppermute | solution.py:22
  197.3 1.6 copy-start.6
  198.9 0.7 copy-start.18
  199.6 3.9 %copy-start.12 = (s32[768]{0:T(1024)S(1)}, s32[768]{0:T(1024)}, u32[]{:S(2)}) copy-start(s32[768]{0:T(1024)} %copy-done.11) | copy-start | bytes 9220
  211.0 2.9 %copy-start.9 = (s32[768]{0:T(1024)S(1)}, s32[768]{0:T(1024)}, u32[]{:S(2)}) copy-start(s32[768]{0:T(1024)} %fusion.125) | copy-start | bytes 9220
  224.1 1.1 copy-start.7
  225.4 0.9 copy-start.8

commit v2 on v1

v2 whole, which is shorter than its diff:
```python
import functools

import jax
import jax.numpy as jnp
from jax import lax
from jax.experimental import pallas as pl
from jax.experimental.pallas import tpu as pltpu
from jax.sharding import PartitionSpec as P

ADAPTER_SCALE = 0.5
PIECES = (2, 4, 4)
SPLIT = 128
LANES = 128
VMEM = 56 * 1024 * 1024


def exchange(pieces, axes):
    return lax.all_to_all(pieces, axes, split_axis=0, concat_axis=0, tiled=True)


def shift(array, axis, step):
    size = lax.axis_size(axis)
    return lax.ppermute(array, axis, [(i, (i + step) % size) for i in range(size)])


def swap(array, axis, bit):
    return lax.ppermute(array, axis, [(i, i ^ bit) for i in range(lax.axis_size(axis))])


def after(value, *earlier):
    return lax.optimization_barrier((value,) + earlier)[0]


def add(a, b):
    return (a.astype(jnp.float32) + b.astype(jnp.float32)).astype(jnp.bfloat16)


def bits_below(size):
    return [1 << i for i in range(size.bit_length() - 1)]


def tensor_sum(total):
    for bit in bits_below(lax.axis_size("tensor")):
        total = add(total, swap(total, "tensor", bit))
    return total


def scatter_columns(term):
    size = lax.axis_size("tensor")
    share = lax.axis_index("tensor")
    width = term.shape[1] // size
    blocks = [
        lax.dynamic_slice_in_dim(term, (share ^ i) * width, width, 1) for i in range(size)
    ]
    for bit in bits_below(size):
        kept = [i for i in range(size) if i % (2 * bit) == 0]
        got = swap(jnp.concatenate([blocks[i ^ bit] for i in kept], axis=1), "tensor", bit)
        for n, i in enumerate(kept):
            blocks[i] = add(blocks[i], got[:, n * width : (n + 1) * width])
    return blocks[0]


def dot(a, b, ca, cb):
    return lax.dot_general(a, b, (((ca,), (cb,)), ((), ())), preferred_element_type=jnp.float32)


def call(body, grid, in_specs, out_spec, out_shape, operands, flops, scratch=()):
    moved = sum(x.size * x.dtype.itemsize for x in operands)
    return pl.pallas_call(
        body,
        grid=grid,
        in_specs=in_specs,
        out_specs=out_spec,
        out_shape=out_shape,
        scratch_shapes=list(scratch),
        compiler_params=pltpu.CompilerParams(vmem_limit_bytes=VMEM),
        cost_estimate=pl.CostEstimate(flops=flops, bytes_accessed=moved, transcendentals=0),
    )(*operands)


def whole(array):
    return pl.BlockSpec(array.shape, lambda i: (0,) * array.ndim)


def fold_body(count, rank, scale, *refs):
    lines, weight, column_slots, slots = refs[:count], refs[count], refs[count + 1], refs[count + 2]
    out = refs[-1]
    step = max(rank, LANES)
    results = []
    for n in range(count):
        full = dot(lines[n][...], weight[...], 1, 1)
        full = jnp.where(slots[:, n : n + 1] == column_slots[...], full, 0.0)
        total = full[:, :step]
        for i in range(step, full.shape[1], step):
            total += full[:, i : i + step]
        results.append(sum(total[:, i : i + rank] for i in range(0, step, rank)))
    result = scale * jnp.concatenate(results, axis=1)
    if len(refs) == count + 5:
        result += refs[count + 3][...]
    out[...] = result.astype(out.dtype)


def fold_product(lines, weight, block, column_slots, slots, rank, scale, before, dtype):
    count = len(lines)
    rows = slots.shape[0]
    tile = rows // 2
    offset, depth = block
    specs = [
        pl.BlockSpec((tile, depth), functools.partial(lambda o, i: (i, o), 0))
        if line.shape[1] == depth
        else pl.BlockSpec((tile, depth), lambda i: (i, offset))
        for line in lines
    ]
    specs.append(pl.BlockSpec((weight.shape[0], depth), lambda i: (0, offset)))
    specs.append(whole(column_slots))
    specs.append(pl.BlockSpec((tile, count), lambda i: (i, 0)))
    operands = list(lines) + [weight, column_slots, slots]
    out_spec = pl.BlockSpec((tile, count * rank), lambda i: (i, 0))
    if before is not None:
        specs.append(out_spec)
        operands.append(before)
    return call(
        functools.partial(fold_body, count, rank, scale),
        (2,),
        specs,
        out_spec,
        jax.ShapeDtypeStruct((rows, count * rank), dtype),
        operands,
        2 * count * rows * weight.shape[0] * depth,
    )


def weight_body(count, rank, scale, *refs):
    compact, row_slots, column_slots, select = refs[:4]
    lines, out, spread = refs[4 : 4 + count], refs[-2], refs[-1]

    @pl.when(pl.program_id(0) == 0)
    def _():
        for n in range(count):
            wide = dot(select[...], compact[:, n * rank : (n + 1) * rank], 1, 1)
            mine = column_slots[...] == row_slots[n : n + 1, :]
            spread[n] = jnp.where(mine, wide, 0.0).astype(jnp.bfloat16)

    total = dot(spread[0], lines[0][...], 1, 0)
    for n in range(1, count):
        total += dot(spread[n], lines[n][...], 1, 0)
    out[...] = (scale * total).astype(out.dtype)


def weight_product(compact, row_slots, column_slots, select, lines, block, scale):
    count = len(lines)
    rows = row_slots.shape[1]
    columns, rank = select.shape
    offset, width = block
    tile = min(width, 512)
    per = width // tile
    specs = [whole(x) for x in (compact, row_slots, column_slots, select)]
    for line in lines:
        skip = 0 if line.shape[1] == width else offset * per
        specs.append(pl.BlockSpec((rows, tile), functools.partial(lambda s, i: (0, s + i), skip)))
    return call(
        functools.partial(weight_body, count, rank, scale),
        (per,),
        specs,
        pl.BlockSpec((columns, tile), lambda i: (0, i)),
        jax.ShapeDtypeStruct((columns, width), jnp.bfloat16),
        [compact, row_slots, column_slots, select] + list(lines),
        2 * count * rows * columns * width,
        [pltpu.VMEM((count, columns, rows), jnp.bfloat16)],
    )


def input_body(count, *refs):
    scaled, frozen, compact, slots, column_slots, select = refs[:6]
    downs, out, spread = refs[6 : 6 + count], refs[-2], refs[-1]

    @pl.when(pl.program_id(0) == 0)
    def _():
        for n in range(count):
            wide = dot(compact[...], select[n], 1, 0)
            mine = slots[...] == column_slots[n : n + 1, :]
            spread[n] = jnp.where(mine, wide, 0.0).astype(jnp.bfloat16)

    total = dot(scaled[...], frozen[...], 1, 1)
    for n in range(count):
        total += dot(spread[n], downs[n][...], 1, 0)
    out[...] = total.astype(out.dtype)


def input_product(scaled, frozen, compact, slots, column_slots, select, downs):
    count = len(downs)
    rows, values = scaled.shape
    columns, width = downs[0].shape
    tile = max(LANES, 1024 // count)
    specs = [whole(scaled), pl.BlockSpec((tile, values), lambda i: (i, 0))]
    specs += [whole(x) for x in (compact, slots, column_slots, select)]
    specs += [pl.BlockSpec((columns, tile), lambda i: (0, i))] * count
    return call(
        functools.partial(input_body, count),
        (width // tile,),
        specs,
        pl.BlockSpec((rows, tile), lambda i: (0, i)),
        jax.ShapeDtypeStruct((rows, width), jnp.bfloat16),
        [scaled, frozen, compact, slots, column_slots, select] + list(downs),
        2 * rows * width * (values + count * columns),
        [pltpu.VMEM((count, rows, columns), jnp.bfloat16)],
    )


def output_body(base, compact, slots, column_slots, select, ups, out):
    wide = dot(compact[...], select[...], 1, 0)
    spread = jnp.where(slots[...] == column_slots[...], wide, 0.0).astype(jnp.bfloat16)
    delta = ADAPTER_SCALE * dot(spread, ups[...], 1, 0)
    out[...] = (base[...].astype(jnp.float32) + delta).astype(out.dtype)


def output_product(base, compact, slots, column_slots, select, ups):
    rows, width = base.shape
    tile = rows // 2 if ups.shape[0] <= 2048 else 64
    line = lambda i: (i, 0)
    specs = [pl.BlockSpec((tile, x.shape[1]), line) for x in (base, compact, slots)]
    specs += [whole(x) for x in (column_slots, select, ups)]
    return call(
        output_body,
        (rows // tile,),
        specs,
        pl.BlockSpec((tile, width), line),
        jax.ShapeDtypeStruct((rows, width), jnp.bfloat16),
        [base, compact, slots, column_slots, select, ups],
        2 * rows * width * ups.shape[0],
    )


def choose(ranks, rank):
    return (jnp.arange(rank, dtype=jnp.int32)[:, None] == ranks[None, :]).astype(jnp.bfloat16)


def shards(
    tokens,
    frozen_value_weight,
    adapter_down_weight,
    adapter_up_weight,
    cotangent,
    language_pair_index,
    language_pair_counts,
    adapter_owner_table,
):
    sides = lax.axis_size("adapter")
    shares = lax.axis_size("tensor")
    planes = lax.axis_size("dp")
    side = lax.axis_index("adapter")
    share = lax.axis_index("tensor")
    plane = lax.axis_index("dp")
    rows, width = tokens.shape
    stored, rank, _ = adapter_down_weight.shape
    values = cotangent.shape[1]
    value_width = values // shares
    own = shares * stored
    total = sides * own
    piece = rank // planes
    lot = stored * piece
    steps = range(1, sides)

    quarter = lax.dynamic_slice_in_dim(adapter_down_weight, plane * piece, piece, 1)
    quarter = quarter.reshape(lot, shares * width)
    up_flat = adapter_up_weight.reshape(stored * rank, values)
    parcel = jnp.stack(
        [
            jnp.concatenate(
                [quarter[:, s * width : (s + 1) * width]]
                + [
                    up_flat[g * lot : (g + 1) * lot, s * value_width : (s + 1) * value_width]
                    for g in range(planes)
                ],
                axis=1,
            )
            for s in range(shares)
        ]
    )
    parcel = jnp.broadcast_to(parcel[None], (sides,) + parcel.shape)
    got = exchange(parcel.reshape((sides * shares,) + parcel.shape[2:]), ("adapter", "tensor"))
    ups = jnp.stack(
        [
            got[:, :, width + g * value_width : width + (g + 1) * value_width]
            for g in range(planes)
        ],
        axis=1,
    ).reshape(total * rank, value_width)
    own_ups = lax.dynamic_slice_in_dim(ups, side * own * rank, own * rank, 0)
    other_downs = []
    for j in steps:
        block = lax.dynamic_slice(
            got, (((side - j) % sides) * shares, 0, 0), (shares, lot, width)
        ).reshape(own * piece, width)
        order = [0]
        for bit in reversed(bits_below(planes)):
            block = jnp.concatenate([block, swap(block, "dp", bit)])
            order += [o ^ bit for o in order]
        other_downs.append(block)

    pairs = jnp.arange(adapter_owner_table.shape[0], dtype=jnp.int32)
    matches = language_pair_index[:, None] == pairs[None, :]
    slots = jnp.sum(jnp.where(matches, adapter_owner_table[None, :], 0), axis=1)
    row_counts = jnp.sum(jnp.where(matches, language_pair_counts[0][None, :], 0), axis=1)
    row_weight = 1.0 / row_counts.astype(jnp.float32)
    scaled = (cotangent.astype(jnp.float32) * row_weight[:, None]).astype(jnp.bfloat16)
    scaled_part = lax.dynamic_slice_in_dim(scaled, share * value_width, value_width, 1)

    tag_rows = -(-rows // value_width)
    tags = jnp.pad(slots, (0, tag_rows * value_width - rows)).reshape(tag_rows, value_width)
    tags = jnp.concatenate([tags // SPLIT, tags % SPLIT]).astype(jnp.bfloat16)
    tags = jnp.pad(tags, ((0, -2 * tag_rows % 16), (0, 0)))
    message = jnp.concatenate([scaled_part, tags])
    scaled_of, slots_of = [scaled_part], [slots]
    for j in steps:
        answer = shift(message, "adapter", j)
        scaled_of.append(answer[:rows])
        numbers = answer[rows : rows + 2 * tag_rows].astype(jnp.int32)
        numbers = numbers[:tag_rows] * SPLIT + numbers[tag_rows:]
        slots_of.append(numbers.reshape(-1)[:rows])
    row_slots = jnp.stack(slots_of)
    slot_columns = row_slots.T

    pieces, position = [], 0
    for part in PIECES:
        piece_width = width // part
        others = tokens[:, position : position + piece_width]
        pieces.append(
            (
                (position // piece_width, piece_width),
                [tokens] + [shift(others, "adapter", j) for j in steps],
            )
        )
        position += piece_width

    base_term = dot(tokens, frozen_value_weight, 1, 0).astype(jnp.bfloat16)
    base_share = scatter_columns(base_term)

    column = jnp.arange(own * rank, dtype=jnp.int32)
    sent_slots = (side * shares + (share ^ (column // (stored * rank)))) * stored
    sent_slots += (column // rank) % stored
    part_local = (column % (own * piece)) // piece
    part_ranks = (column // (own * piece)) * piece + column % piece
    part_slots = side * own + part_local
    natural_slots = side * own + column // rank
    part_select = choose(part_ranks, rank).T

    back_part = fold_product(
        scaled_of,
        own_ups,
        (0, value_width),
        natural_slots[None, :],
        slot_columns,
        rank,
        ADAPTER_SCALE,
        None,
        jnp.bfloat16,
    )
    back_all = tensor_sum(back_part)

    down_flat = after(adapter_down_weight.reshape(stored * rank, shares * width), back_all)
    sent = [
        lax.dynamic_slice_in_dim(down_flat, (share ^ k) * width, width, 1) for k in range(shares)
    ]
    own_down = jnp.concatenate(
        [sent[0]] + [swap(sent[k], "tensor", k) for k in range(1, shares)]
    )

    low_part = None
    parts_down = []
    for n, (block, lines) in enumerate(pieces):
        parts_down.append(
            weight_product(
                back_all, row_slots, part_slots[:, None], part_select, lines, block, 1.0
            )
        )
        last = n == len(pieces) - 1
        low_part = fold_product(
            lines,
            own_down,
            block,
            sent_slots[None, :],
            slot_columns,
            rank,
            1.0,
            low_part,
            jnp.bfloat16 if last else jnp.float32,
        )
    low_all = tensor_sum(low_part)
    up_part = weight_product(
        low_all,
        row_slots,
        part_slots[:, None],
        part_select,
        scaled_of,
        (0, value_width),
        ADAPTER_SCALE,
    )
    last_width = parts_down[-1].shape[1]
    parts_down[-1] = jnp.concatenate([parts_down[-1], up_part], axis=1)

    sums = []
    for part in parts_down:
        columns = part.shape[1]
        arrived = exchange(part.reshape(planes * shares, lot, columns), ("dp", "tensor"))
        arrived = arrived.reshape(planes, shares, lot, columns)
        sums.append(jnp.sum(arrived.astype(jnp.float32), axis=0).astype(jnp.bfloat16))
    grad_down = jnp.concatenate(
        [
            sums[n][s][:, : pieces[n][0][1]]
            for s in range(shares)
            for n in range(len(pieces))
        ],
        axis=1,
    ).reshape(stored, piece, shares * width)
    grad_up = jnp.concatenate(
        [sums[-1][s][:, last_width:] for s in range(shares)], axis=1
    ).reshape(stored, piece, values)

    low, back = low_all[:, :rank], back_all[:, :rank]
    for j in steps:
        here = slice(j * rank, (j + 1) * rank)
        reply = jnp.concatenate([low_all[:, here], back_all[:, here]], axis=1)
        reply = shift(reply, "adapter", -j)
        low = low + reply[:, :rank]
        back = back + reply[:, rank:]

    every = jnp.arange(total * rank, dtype=jnp.int32)
    mixed_out = output_product(
        base_share, low, slots[:, None], (every // rank)[None, :], choose(every % rank, rank), ups
    )

    base_of = jnp.array(order, jnp.int32)[column // (own * piece)]
    other_ranks = (plane ^ base_of) * piece + column % piece
    input_gradient = input_product(
        scaled,
        frozen_value_weight,
        back,
        slots[:, None],
        jnp.stack(
            [sent_slots] + [((side - j) % sides) * own + part_local for j in steps]
        ),
        jnp.stack([choose(column % rank, rank)] + [choose(other_ranks, rank) for _ in steps]),
        [own_down] + other_downs,
    )
    return mixed_out, input_gradient, grad_down, grad_up


def solution(mesh):
    return jax.shard_map(
        shards,
        mesh=mesh,
        in_specs=(
            P(("dp", "adapter"), "tensor"),
            P("tensor", None),
            P(("adapter", "tensor"), None, None),
            P(("adapter", "tensor"), None, None),
            P(("dp", "adapter"), None),
            P(("dp", "adapter")),
            P(("dp", "adapter"), None),
            P(),
        ),
        out_specs=(
            P(("dp", "adapter"), "tensor"),
            P(("dp", "adapter"), "tensor"),
            P(("adapter", "tensor"), "dp", None),
            P(("adapter", "tensor"), "dp", None),
        ),
        check_vma=False,
    )
```

time: 227 us -> 277 us (1.22)
  matrix products: 81.4 us -> 6.68 us
  Pallas kernels: 0 us -> 54.7 us
  waiting for transfers between devices: 81.8 us -> 126 us
  other arithmetic: 17.3 us -> 33.5 us
  local copies, waits for them, and re-layouts: 12.1 us -> 17.2 us
  starting transfers between devices: 32.5 us -> 36.2 us
    dot_general x20 -> x1, matrix products: 81.4 us -> 6.68 us  [dot(): lax.dot_general(a, b, (((ca,), (cb,)), ((), ())), preferred_element_type=...]
    pallas_call x0 -> x10, Pallas kernels: none -> 54.7 us  [call(): pl.pallas_call(body, grid=grid, in_specs=in_specs, out_specs=out_spec, ou...]
    ppermute x6 -> x11, waiting for transfers between devices: 23.9 us -> 73 us  [swap(): lax.ppermute(array, axis, [(i, i ^ bit) for i in range(lax.axis_size(axis...]
    ppermute x5, waiting for transfers between devices: 57.9 us -> 47.9 us  [shift(): lax.ppermute(array, axis, [(i, (i + step) % size) for i in range(size)])]
    concatenate x6 -> x7, other arithmetic: 5.71 us -> 12.5 us  [the longest x2 4.72 us: shards(): block = jnp.concatenate([block, swap(block, 'dp', bit)])]
    all_to_all x4, waiting for transfers between devices: 0.01 us -> 5.46 us  [exchange(): return lax.all_to_all(pieces, axes, split_axis=0, concat_axis=0, tiled=True)]
    dynamic_slice x0 -> x4, local copies, waits for them, and re-layouts: none -> 4.92 us  [the longest x1 1.72 us: shards(): lax.dynamic_slice_in_dim(down_flat, (share ^ k) * width, width, 1)]
    ppermute x6 -> x11, starting transfers between devices: 5.78 us -> 9.24 us  [swap(): lax.ppermute(array, axis, [(i, i ^ bit) for i in range(lax.axis_size(axis...]
  transfers between devices with their start and end apart: 15 -> 20, of which waited for: 5 -> 9; matrix products, arithmetic and copies ran while one was open for 46% -> 18% of each run, Pallas kernels for 0% -> 20%
where the time goes in v2:
time: 277 us; the launch traced here: 276 us
  waiting for transfers between devices  126 us (45%)
  Pallas kernels  54.7 us (20%)
  starting transfers between devices  36.2 us (13%)
  other arithmetic  33.5 us (12%)
  local copies, waits for them, and re-layouts  17.2 us (6%)
  matrix products  6.68 us (2%)
    ppermute x11, waiting for transfers between devices, swap(): lax.ppermute(array, axis, [(i, i ^ bit) for i in range(lax.axis_size(axis...  73 us
    pallas_call x10, Pallas kernels, call(): pl.pallas_call(body, grid=grid, in_specs=in_specs, out_specs=out_spec, ou...  54.7 us
    ppermute x5, waiting for transfers between devices, shift(): lax.ppermute(array, axis, [(i, (i + step) % size) for i in range(size)])  47.9 us
    all_to_all x4, starting transfers between devices, exchange(): return lax.all_to_all(pieces, axes, split_axis=0, concat_axis=0, tiled=True)  22.2 us
    ppermute x11, starting transfers between devices, swap(): lax.ppermute(array, axis, [(i, i ^ bit) for i in range(lax.axis_size(axis...  9.24 us
    dot_general x1, matrix products, dot(): lax.dot_general(a, b, (((ca,), (cb,)), ((), ())), preferred_element_type=...  6.68 us
    convert_element_type x6, other arithmetic, add(): return (a.astype(jnp.float32) + b.astype(jnp.float32)).astype(jnp.bfloat16)  6.08 us
  transfers between devices with their start and end apart: 20, of which 9 were waited for; matrix products, arithmetic and copies ran while one was open for 18% of the time, Pallas kernels for 20%

profile of v2, /device:TPU:0, one launch (start us, length us, event | category | flops | bytes accessed | tf_op | source)
XLA Modules:
  0.0 275.9 jit_solution(18367774535679937443)
XLA Ops:
  0.6 1.2 constant_dynamic-slice_fusion.6
  2.2 1.7 broadcast_in_dim.28
  3.9 5.3 %all-to-all-start = ((bf16[8,48,3072]{2,1,0:T(8,128)(2,1)}), bf16[8,48,3072]{2,1,0:T(8,128)(2,1)}, u32[]{:S(2)}, u32[]{:S(2)}) async-start(bf16[8,48,3072]{2,1,0:T(8,128)(2,1)} %bitcast.8), calls=%async_computation | async-start | bytes 4718592 | tf_op jit(solution)/shard_map/all_to_all | solution.py:18
  9.4 1.9 multiply_convert_fusion.refs_0_
  11.4 0.9 pad_maximum_fusion.7
  12.3 2.1 collective-permute-start.3
  14.4 1.4 slice.213
  15.8 1.3 fusion.43
  17.1 2.0 collective-permute-start.9
  19.5 6.7 %convolution_convert_fusion = bf16[768,1024]{1,0:T(8,128)(2,1)} fusion(bf16[768,2048]{1,0:T(8,128)(2,1)S(1)} %copy-done, bf16[2048,1024]{1,0:T(8,128)(2,1)} %refs_1_.1), kind=kOutput, calls=%fused_computation.3 | convolution fusion | flops 3222011904 | bytes 8912896 | tf_op jit(solution)/shard_map/dot_general | solution.py:64
  26.8 1.1 fusion.7.refs_2_
  27.9 0.8 fusion.14.refs_3_
  28.8 18.1 %collective-permute-done.3 = bf16[784,256]{1,0:T(8,128)(2,1)} collective-permute-done((bf16[784,256]{1,0:T(8,128)(2,1)}, bf16[784,256]{1,0:T(8,128)(2,1)}, u32[]{:S(2)}, u32[]{:S(2)}) %collective-permute-start.3) | collective-permute-done | bytes 401440 | tf_op jit(solution)/shard_map/ppermute | solution.py:23
  46.9 0.7 slice_convert_fusion
  48.2 0.9 copy.26.refs_4_
  49.2 1.8 slice.247.refs_1_.refs_5_
  50.9 1.3 slice_bitcast_fusion.3
  52.4 0.9 copy-done.4
  53.3 0.8 constant_dynamic-slice_fusion.5.refs_2_
  54.1 3.3 %shard_map.120 = bf16[768,128]{1,0:T(8,128)(2,1)} custom-call(bf16[768,256]{1,0:T(8,128)(2,1)} %copy-done.9, bf16[768,256]{1,0:T(8,128)(2,1)} %slice.247.refs_1_.refs_5_, bf16[768,256]{1,0:T(8,128)(2,1)} %constant_dynamic-slice_fusion.5.refs_2_, s32[1,768]{1,0:T(1,128)} %fusion.41.refs_3_, s32[768,2]{1,0:T(8,128)} %copy.26.refs_4_), custom_call_target="tpu_custom_call" | custom-call | flops 603979776 | bytes 1188864 | tf_op jit(solution)/shard_map/pallas_call | solution.py:69
  57.5 1.6 collective-permute-done.4
  59.0 1.0 add_convert_fusion.6
  60.0 1.6 collective-permute-start.5
  61.7 5.4 %collective-permute-done.5 = bf16[768,128]{1,0:T(8,128)(2,1)S(1)} collective-permute-done((bf16[768,128]{1,0:T(8,128)(2,1)S(1)}, bf16[768,128]{1,0:T(8,128)(2,1)S(1)}, u32[]{:S(2)}, u32[]{:S(2)}) %collective-permute-start.5) | collective-permute-done | bytes 196640 | tf_op jit(solution)/shard_map/ppermute | solution.py:27
  67.0 0.7 add_convert_fusion.5.refs_0_
  67.8 29.7 %collective-permute-done.9.refs_1_.refs_5_ = bf16[768,512]{1,0:T(8,128)(2,1)} collective-permute-done((bf16[768,512]{1,0:T(8,128)(2,1)}, bf16[768,512]{1,0:T(8,128)(2,1)}, u32[]{:S(2)}, u32[]{:S(2)}) %collective-permute-start.9) | collective-permute-done | bytes 786464 | tf_op jit(solution)/shard_map/ppermute | solution.py:23
  97.5 4.6 %shard_map.127 = bf16[768,512]{1,0:T(8,128)(2,1)} custom-call(bf16[768,128]{1,0:T(8,128)(2,1)} %add_convert_fusion.5.refs_0_, s32[2,768]{1,0:T(2,128)} %get-tuple-element.54.refs_1_, s32[768,1]{1,0:T(8,128)} %fusion.7.refs_2_, bf16[768,64]{1,0:T(8,128)(2,1)} %fusion.14.refs_3_, bf16[768,2048]{1,0:T(8,128)(2,1)} %refs_4_.5, ...), custom_call_target="tpu_custom_call" | custom-call | flops 1207959552 | bytes 4236288 | tf_op jit(solution)/shard_map/pallas_call | solution.py:69
  102.1 6.7 %all-to-all-start.2 = ((bf16[16,48,512]{2,1,0:T(8,128)(2,1)}), bf16[16,48,512]{2,1,0:T(8,128)(2,1)}, u32[]{:S(2)}, u32[]{:S(2)}) async-start(bf16[16,48,512]{2,1,0:T(8,128)(2,1)} %bitcast.63), calls=%async_computation.2 | async-start | bytes 1572864 | tf_op jit(solution)/shard_map/all_to_all | solution.py:18
  108.9 0.7 add_convert_fusion.7.refs_5_
  109.6 1.2 constant_dynamic-slice_fusion.9
  110.8 0.9 pad_maximum_fusion.5
  112.3 1.7 constant_dynamic-slice_fusion.4
  114.3 1.7 collective-permute-start.7
  116.0 6.1 %shard_map.126 = bf16[768,1024]{1,0:T(8,128)(2,1)} custom-call(bf16[768,128]{1,0:T(8,128)(2,1)} %add_convert_fusion.5.refs_0_, s32[2,768]{1,0:T(2,128)} %get-tuple-element.54.refs_1_, s32[768,1]{1,0:T(8,128)} %fusion.7.refs_2_, bf16[768,64]{1,0:T(8,128)(2,1)} %fusion.14.refs_3_, bf16[768,2048]{1,0:T(8,128)(2,1)} %refs_4_.5, ...), custom_call_target="tpu_custom_call" | custom-call | flops 2415919104 | bytes 5022720 | tf_op jit(solution)/shard_map/pallas_call | solution.py:69
  122.2 5.5 %all-to-all-done.2 = bf16[16,48,512]{2,1,0:T(8,128)(2,1)} async-done(((bf16[16,48,512]{2,1,0:T(8,128)(2,1)}), bf16[16,48,512]{2,1,0:T(8,128)(2,1)}, u32[]{:S(2)}, u32[]{:S(2)}) %all-to-all-start.2) | async-done | bytes 786464 | tf_op jit(solution)/shard_map/all_to_all | solution.py:18
  127.6 5.5 %all-to-all-start.1 = ((bf16[16,48,1024]{2,1,0:T(8,128)(2,1)}), bf16[16,48,1024]{2,1,0:T(8,128)(2,1)S(1)}, u32[]{:S(2)}, u32[]{:S(2)}) async-start(bf16[16,48,1024]{2,1,0:T(8,128)(2,1)} %bitcast.64), calls=%async_computation.1 | async-start | bytes 3145728 | tf_op jit(solution)/shard_map/all_to_all | solution.py:18
  133.2 0.7 fusion.13.select
  133.9 1.2 constant_dynamic-slice_fusion
  135.1 2.9 %collective-permute-start.14 = (bf16[192,2048]{1,0:T(8,128)(2,1)S(1)}, bf16[192,2048]{1,0:T(8,128)(2,1)S(1)}, u32[]{:S(2)}, u32[]{:S(2)}) collective-permute-start(bf16[192,2048]{1,0:T(8,128)(2,1)S(1)} %bitcast.54), channel_id=1, source_target_pairs={{0,16},{8,24},{16,0},{24,8},{1,17},{9,25},{17,1},{25,9},{2,18},{10... | collective-permute-start | bytes 2359304 | tf_op jit(solution)/shard_map/ppermute | solution.py:27
  138.5 0.9 broadcast_in_dim.30.slots.refs_3_
  139.5 1.2 collective-permute-done.7
  140.7 25.9 %collective-permute-done.8 = bf16[192,2048]{1,0:T(8,128)(2,1)} collective-permute-done((bf16[192,2048]{1,0:T(8,128)(2,1)}, bf16[192,2048]{1,0:T(8,128)(2,1)}, u32[]{:S(2)}, u32[]{:S(2)}) %collective-permute-start.8) | collective-permute-done | bytes 786464 | tf_op jit(solution)/shard_map/ppermute | solution.py:27
  166.6 3.2 %pad_maximum_fusion.refs_2_.refs_6_ = bf16[768,2048]{1,0:T(8,128)(2,1)} fusion(bf16[192,2048]{1,0:T(8,128)(2,1)} %collective-permute-done.8, bf16[192,2048]{1,0:T(8,128)(2,1)} %collective-permute-done.7, bf16[192,2048]{1,0:T(8,128)(2,1)} %collective-permute-done.6, bf16[192,2048]{1,0:T(8,128)(2,1)} %get-tuple-element.10), kind=kLoop, calls=%fused_computation | loop fusion | flops 12582912 | bytes 6291456 | tf_op jit(solution)/shard_map/concatenate | solution.py:365
  169.8 6.1 %shard_map.121.refs_5_ = f32[768,128]{1,0:T(8,128)} custom-call(bf16[768,2048]{1,0:T(8,128)(2,1)} %refs_4_.5, bf16[768,1024]{1,0:T(8,128)(2,1)} %collective-permute-done.10.refs_1_.refs_5_, bf16[768,2048]{1,0:T(8,128)(2,1)} %pad_maximum_fusion.refs_2_.refs_6_, s32[1,768]{1,0:T(1,128)} %copy-done.13, s32[768,2]{1,0:T(8,128)} %copy.26.refs_4_), custom_call_target="tpu_custom_call" | custom-call | flops 2415919104 | bytes 7873536 | tf_op jit(solution)/shard_map/pallas_call | solution.py:69
  175.8 4.3 %shard_map.122.refs_5_ = f32[768,128]{1,0:T(8,128)} custom-call(bf16[768,2048]{1,0:T(8,128)(2,1)} %refs_4_.5, bf16[768,512]{1,0:T(8,128)(2,1)} %collective-permute-done.9.refs_1_.refs_5_, bf16[768,2048]{1,0:T(8,128)(2,1)} %pad_maximum_fusion.refs_2_.refs_6_, s32[1,768]{1,0:T(1,128)} %copy-done.13, s32[768,2]{1,0:T(8,128)} %copy.26.refs_4_, ...), custom_call_target="tpu_custom_call" | custom-call | flops 1207959552 | bytes 7480320 | tf_op jit(solution)/shard_map/pallas_call | solution.py:69
  180.1 4.2 %shard_map.123 = bf16[768,128]{1,0:T(8,128)(2,1)} custom-call(bf16[768,2048]{1,0:T(8,128)(2,1)} %refs_4_.5, bf16[768,512]{1,0:T(8,128)(2,1)} %collective-permute-done.2.refs_1_.refs_5_, bf16[768,2048]{1,0:T(8,128)(2,1)} %pad_maximum_fusion.refs_2_.refs_6_, s32[1,768]{1,0:T(1,128)} %copy-done.13, s32[768,2]{1,0:T(8,128)} %copy.26.refs_4_, ...), custom_call_target="tpu_custom_call" | custom-call | flops 1207959552 | bytes 7480320 | tf_op jit(solution)/shard_map/pallas_call | solution.py:69
  185.0 19.6 %collective-permute-done.14 = bf16[192,2048]{1,0:T(8,128)(2,1)S(1)} collective-permute-done((bf16[192,2048]{1,0:T(8,128)(2,1)S(1)}, bf16[192,2048]{1,0:T(8,128)(2,1)S(1)}, u32[]{:S(2)}, u32[]{:S(2)}) %collective-permute-start.14) | collective-permute-done | bytes 786464 | tf_op jit(solution)/shard_map/ppermute | solution.py:27
  204.7 1.2 pad_maximum_fusion.2
  206.0 1.7 collective-permute-start.12
  207.7 2.1 add_convert_fusion.1
  210.3 4.6 %shard_map.128 = bf16[768,512]{1,0:T(8,128)(2,1)} custom-call(bf16[768,128]{1,0:T(8,128)(2,1)} %add_convert_fusion.5.refs_0_, s32[2,768]{1,0:T(2,128)} %get-tuple-element.54.refs_1_, s32[768,1]{1,0:T(8,128)} %fusion.7.refs_2_, bf16[768,64]{1,0:T(8,128)(2,1)} %fusion.14.refs_3_, bf16[768,2048]{1,0:T(8,128)(2,1)} %refs_4_.5, ...), custom_call_target="tpu_custom_call" | custom-call | flops 1207959552 | bytes 4236288 | tf_op jit(solution)/shard_map/pallas_call | solution.py:69
  215.2 0.8 pad_maximum_fusion.8
  216.5 4.3 %shard_map.129 = bf16[768,256]{1,0:T(8,128)(2,1)} custom-call(bf16[768,128]{1,0:T(8,128)(2,1)} %copy-done.7, s32[2,768]{1,0:T(2,128)} %get-tuple-element.54.refs_1_, s32[768,1]{1,0:T(8,128)} %fusion.7.refs_2_, bf16[768,64]{1,0:T(8,128)(2,1)} %fusion.14.refs_3_, bf16[768,256]{1,0:T(8,128)(2,1)} %copy-done.9, bf16[768,256]{1,0:T(8,128)(2,1)} %slice.247.refs_1_.refs_5_), custom_call_target="tpu_custom_call" | custom-call | flops 603979776 | bytes 1090560 | tf_op jit(solution)/shard_map/pallas_call | solution.py:69
  220.8 2.2 pad_maximum_fusion.4
  223.0 4.6 %all-to-all-start.3 = ((bf16[16,48,768]{2,1,0:T(8,128)(2,1)}), bf16[16,48,768]{2,1,0:T(8,128)(2,1)}, u32[]{:S(2)}, u32[]{:S(2)}) async-start(bf16[16,48,768]{2,1,0:T(8,128)(2,1)} %bitcast.61), calls=%async_computation.3 | async-start | bytes 2359296 | tf_op jit(solution)/shard_map/all_to_all | solution.py:18
  227.6 2.1 add_convert_fusion.base
  229.8 1.9 slice_add_fusion
  231.7 4.0 %shard_map.124 = bf16[768,256]{1,0:T(8,128)(2,1)} custom-call(bf16[768,256]{1,0:T(8,128)(2,1)} %add_convert_fusion.base, bf16[768,64]{1,0:T(8,128)(2,1)} %get-tuple-element.53.compact, s32[768,1]{1,0:T(8,128)} %broadcast_in_dim.30.slots.refs_3_, s32[1,1536]{1,0:T(1,128)} %and_select_fusion.column_slots, bf16[64,1536]{1,0:T(8,128)(2,1)} %fusion.13.select, ...), custom_call_target="tpu_custom_call" | custom-call | flops 603979776 | bytes 1483776 | tf_op jit(solution)/shard_map/pallas_call | solution.py:69
  235.7 1.3 reduce_sum.57
  237.0 19.2 %collective-permute-done.15 = bf16[384,2048]{1,0:T(8,128)(2,1)} collective-permute-done((bf16[384,2048]{1,0:T(8,128)(2,1)}, bf16[384,2048]{1,0:T(8,128)(2,1)}, u32[]{:S(2)}, u32[]{:S(2)}) %collective-permute-start.15) | collective-permute-done | bytes 1572896 | tf_op jit(solution)/shard_map/ppermute | solution.py:27
  256.2 3.5 %pad_maximum_fusion.1.refs_7_ = bf16[768,2048]{1,0:T(8,128)(2,1)} fusion(bf16[384,2048]{1,0:T(8,128)(2,1)} %collective-permute-done.15, bf16[192,2048]{1,0:T(8,128)(2,1)S(1)} %collective-permute-done.14, bf16[192,2048]{1,0:T(8,128)(2,1)S(1)} %bitcast.56), kind=kLoop, calls=%fused_computation.1 | loop fusion | flops 9437184 | bytes 6291456 | tf_op jit(solution)/shard_map/concatenate | solution.py:297
  259.6 13.2 %shard_map.125 = bf16[768,2048]{1,0:T(8,128)(2,1)} custom-call(bf16[768,1024]{1,0:T(8,128)(2,1)} %copy-done.6, bf16[2048,1024]{1,0:T(8,128)(2,1)} %refs_1_.1, bf16[768,64]{1,0:T(8,128)(2,1)} %get-tuple-element.52.refs_2_, s32[768,1]{1,0:T(8,128)} %broadcast_in_dim.30.slots.refs_3_, s32[2,768]{1,0:T(2,128)} %pad_add_fusion.1.refs_4_, ...), custom_call_target="tpu_custom_call" | custom-call | flops 8053063680 | bytes 12362752 | tf_op jit(solution)/shard_map/pallas_call | solution.py:69
  273.2 1.5 reduce_sum.58
  275.0 0.7 pad_maximum_fusion.9
  (113 shorter events, 6.6 us)
Async XLA Ops:
  0.6 1.3 copy-start.12
  3.9 5.3 %copy-start.15 = (s32[768]{0:T(1024)S(1)}, s32[768]{0:T(1024)}, u32[]{:S(2)}) copy-start(s32[768]{0:T(1024)} %param.14) | copy-start | bytes 9220
  3.9 5.3 %copy-start.16 = (s32[24]{0:T(128)S(1)}, s32[24]{0:T(128)}, u32[]{:S(2)}) copy-start(s32[24]{0:T(128)} %param.16) | copy-start | bytes 292
  3.9 5.3 %copy-start.17 = (s32[1,24]{1,0:T(1,128)S(1)}, s32[1,24]{1,0:T(1,128)}, u32[]{:S(2)}) copy-start(s32[1,24]{1,0:T(1,128)} %param.15) | copy-start | bytes 292
  3.9 47.0 %all-to-all-start = ((bf16[8,48,3072]{2,1,0:T(8,128)(2,1)}), bf16[8,48,3072]{2,1,0:T(8,128)(2,1)}, u32[]{:S(2)}, u32[]{:S(2)}) async-start(bf16[8,48,3072]{2,1,0:T(8,128)(2,1)} %bitcast.8), calls=%async_computation | async-start | bytes 4718592 | tf_op jit(solution)/shard_map/all_to_all | solution.py:18
  9.2 5.2 %copy-start = (bf16[768,2048]{1,0:T(8,128)(2,1)S(1)}, bf16[768,2048]{1,0:T(8,128)(2,1)}, u32[]{:S(2)}) copy-start(bf16[768,2048]{1,0:T(8,128)(2,1)} %refs_4_.5) | copy-start | bytes 9437188
  11.3 5.8 %copy-start.6 = (bf16[768,1024]{1,0:T(8,128)(2,1)}, bf16[768,1024]{1,0:T(8,128)(2,1)S(1)}, u32[]{:S(2)}) copy-start(bf16[768,1024]{1,0:T(8,128)(2,1)S(1)} %multiply_convert_fusion.refs_0_) | copy-start | bytes 4718596
  11.4 5.7 %copy-start.9 = (bf16[768,256]{1,0:T(8,128)(2,1)}, bf16[768,256]{1,0:T(8,128)(2,1)S(1)}, u32[]{:S(2)}) copy-start(bf16[768,256]{1,0:T(8,128)(2,1)S(1)} %constant_dynamic-slice_fusion.7.refs_0_.refs_4_) | copy-start | bytes 1179652
  12.3 34.6 %collective-permute-start.3 = (bf16[784,256]{1,0:T(8,128)(2,1)}, bf16[784,256]{1,0:T(8,128)(2,1)}, u32[]{:S(2)}, u32[]{:S(2)}) collective-permute-start(bf16[784,256]{1,0:T(8,128)(2,1)} %pad_maximum_fusion.7), channel_id=1, source_target_pairs={{0,4},{4,0},{1,5},{5,1},{2,6},{6,2},{3,7},{7,3},{8,12},{12,8},{9,1... | collective-permute-start | bytes 1204232 | tf_op jit(solution)/shard_map/ppermute | solution.py:23
  15.8 100.3 %collective-permute-start.10 = (bf16[768,1024]{1,0:T(8,128)(2,1)}, bf16[768,1024]{1,0:T(8,128)(2,1)}, u32[]{:S(2)}, u32[]{:S(2)}) collective-permute-start(bf16[768,1024]{1,0:T(8,128)(2,1)} %slice.213), channel_id=1, source_target_pairs={{0,4},{4,0},{1,5},{5,1},{2,6},{6,2},{3,7},{7,3},{8,12},{12,8},{9,1... | collective-permute-start | bytes 4718600 | tf_op jit(solution)/shard_map/ppermute | solution.py:23
  17.1 80.4 %collective-permute-start.9 = (bf16[768,512]{1,0:T(8,128)(2,1)}, bf16[768,512]{1,0:T(8,128)(2,1)}, u32[]{:S(2)}, u32[]{:S(2)}) collective-permute-start(bf16[768,512]{1,0:T(8,128)(2,1)} %get-tuple-element.8), channel_id=1, source_target_pairs={{0,4},{4,0},{1,5},{5,1},{2,6},{6,2},{3,7},{7,3},{8,12},{12,8},{9,1... | collective-permute-start | bytes 2359304 | tf_op jit(solution)/shard_map/ppermute | solution.py:23
  19.1 161.0 %collective-permute-start.2 = (bf16[768,512]{1,0:T(8,128)(2,1)}, bf16[768,512]{1,0:T(8,128)(2,1)}, u32[]{:S(2)}, u32[]{:S(2)}) collective-permute-start(bf16[768,512]{1,0:T(8,128)(2,1)} %get-tuple-element.9), channel_id=1, source_target_pairs={{0,4},{4,0},{1,5},{5,1},{2,6},{6,2},{3,7},{7,3},{8,12},{12,8},{9,1... | collective-permute-start | bytes 2359304 | tf_op jit(solution)/shard_map/ppermute | solution.py:23
  52.4 0.9 copy-start.4
  57.4 1.7 collective-permute-start.4
  57.4 80.5 %copy-start.13 = (s32[1,768]{1,0:T(1,128)}, s32[1,768]{1,0:T(1,128)S(1)}, u32[]{:S(2)}) copy-start(s32[1,768]{1,0:T(1,128)S(1)} %fusion.39.refs_3_) | copy-start | bytes 9220
  60.0 7.0 %collective-permute-start.5 = (bf16[768,128]{1,0:T(8,128)(2,1)S(1)}, bf16[768,128]{1,0:T(8,128)(2,1)S(1)}, u32[]{:S(2)}, u32[]{:S(2)}) collective-permute-start(bf16[768,128]{1,0:T(8,128)(2,1)S(1)} %add_convert_fusion.6), channel_id=1, source_target_pairs={{0,2},{1,3},{2,0},{3,1},{4,6},{5,7},{6,4},{7,5},{8,10},{9,11},{10,... | collective-permute-start | bytes 589832 | tf_op jit(solution)/shard_map/ppermute | solution.py:27
  102.1 10.2 %copy-start.3 = (bf16[3,64,8192]{2,1,0:T(8,128)(2,1)S(1)}, bf16[3,64,8192]{2,1,0:T(8,128)(2,1)}, u32[]{:S(2)}) copy-start(bf16[3,64,8192]{2,1,0:T(8,128)(2,1)} %param.11) | copy-start | bytes 9437188
  102.1 25.6 %all-to-all-start.2 = ((bf16[16,48,512]{2,1,0:T(8,128)(2,1)}), bf16[16,48,512]{2,1,0:T(8,128)(2,1)}, u32[]{:S(2)}, u32[]{:S(2)}) async-start(bf16[16,48,512]{2,1,0:T(8,128)(2,1)} %bitcast.63), calls=%async_computation.2 | async-start | bytes 1572864 | tf_op jit(solution)/shard_map/all_to_all | solution.py:18
  114.0 25.5 %collective-permute-start.6 = (bf16[192,2048]{1,0:T(8,128)(2,1)}, bf16[192,2048]{1,0:T(8,128)(2,1)}, u32[]{:S(2)}, u32[]{:S(2)}) collective-permute-start(bf16[192,2048]{1,0:T(8,128)(2,1)} %get-tuple-element.13), channel_id=1, source_target_pairs={{0,1},{1,0},{2,3},{3,2},{4,5},{5,4},{6,7},{7,6},{8,9},{9,8},{10,11... | collective-permute-start | bytes 2359304 | tf_op jit(solution)/shard_map/ppermute | solution.py:27
  114.3 26.3 %collective-permute-start.7 = (bf16[192,2048]{1,0:T(8,128)(2,1)}, bf16[192,2048]{1,0:T(8,128)(2,1)}, u32[]{:S(2)}, u32[]{:S(2)}) collective-permute-start(bf16[192,2048]{1,0:T(8,128)(2,1)} %get-tuple-element.12), channel_id=1, source_target_pairs={{0,2},{1,3},{2,0},{3,1},{4,6},{5,7},{6,4},{7,5},{8,10},{9,11},{10,... | collective-permute-start | bytes 2359304 | tf_op jit(solution)/shard_map/ppermute | solution.py:27
  116.0 50.6 %collective-permute-start.8 = (bf16[192,2048]{1,0:T(8,128)(2,1)}, bf16[192,2048]{1,0:T(8,128)(2,1)}, u32[]{:S(2)}, u32[]{:S(2)}) collective-permute-start(bf16[192,2048]{1,0:T(8,128)(2,1)} %get-tuple-element.11), channel_id=1, source_target_pairs={{0,3},{1,2},{2,1},{3,0},{4,7},{5,6},{6,5},{7,4},{8,11},{9,10},{10,... | collective-permute-start | bytes 2359304 | tf_op jit(solution)/shard_map/ppermute | solution.py:27
  127.6 95.4 %all-to-all-start.1 = ((bf16[16,48,1024]{2,1,0:T(8,128)(2,1)}), bf16[16,48,1024]{2,1,0:T(8,128)(2,1)S(1)}, u32[]{:S(2)}, u32[]{:S(2)}) async-start(bf16[16,48,1024]{2,1,0:T(8,128)(2,1)} %bitcast.64), calls=%async_computation.1 | async-start | bytes 3145728 | tf_op jit(solution)/shard_map/all_to_all | solution.py:18
  135.1 69.6 %collective-permute-start.14 = (bf16[192,2048]{1,0:T(8,128)(2,1)S(1)}, bf16[192,2048]{1,0:T(8,128)(2,1)S(1)}, u32[]{:S(2)}, u32[]{:S(2)}) collective-permute-start(bf16[192,2048]{1,0:T(8,128)(2,1)S(1)} %bitcast.54), channel_id=1, source_target_pairs={{0,16},{8,24},{16,0},{24,8},{1,17},{9,25},{17,1},{25,9},{2,18},{10... | collective-permute-start | bytes 2359304 | tf_op jit(solution)/shard_map/ppermute | solution.py:27
  139.5 68.2 %collective-permute-start = (bf16[768,512]{1,0:T(8,128)(2,1)}, bf16[768,512]{1,0:T(8,128)(2,1)S(1)}, u32[]{:S(2)}, u32[]{:S(2)}) collective-permute-start(bf16[768,512]{1,0:T(8,128)(2,1)} %pad_maximum_fusion.5), channel_id=1, source_target_pairs={{0,1},{1,0},{2,3},{3,2},{4,5},{5,4},{6,7},{7,6},{8,9},{9,8},{10,11... | collective-permute-start | bytes 2359304 | tf_op jit(solution)/shard_map/ppermute | solution.py:27
  184.3 21.6 %copy-start.11 = (bf16[768,128]{1,0:T(8,128)(2,1)S(1)}, bf16[768,128]{1,0:T(8,128)(2,1)}, u32[]{:S(2)}) copy-start(bf16[768,128]{1,0:T(8,128)(2,1)} %shard_map.123) | copy-start | bytes 589828
  184.3 25.8 %copy-start.1 = (bf16[768,128]{1,0:T(8,128)(2,1)S(1)}, bf16[768,128]{1,0:T(8,128)(2,1)}, u32[]{:S(2)}) copy-start(bf16[768,128]{1,0:T(8,128)(2,1)} %add_convert_fusion.5.refs_0_) | copy-start | bytes 589828
  184.4 21.6 %collective-permute-start.11 = (bf16[768,128]{1,0:T(8,128)(2,1)}, bf16[768,128]{1,0:T(8,128)(2,1)S(1)}, u32[]{:S(2)}, u32[]{:S(2)}) collective-permute-start(bf16[768,128]{1,0:T(8,128)(2,1)} %shard_map.123), channel_id=1, source_target_pairs={{0,1},{1,0},{2,3},{3,2},{4,5},{5,4},{6,7},{7,6},{8,9},{9,8},{10,11... | collective-permute-start | bytes 589832 | tf_op jit(solution)/shard_map/ppermute | solution.py:27
  205.9 50.3 %collective-permute-start.15 = (bf16[384,2048]{1,0:T(8,128)(2,1)}, bf16[384,2048]{1,0:T(8,128)(2,1)}, u32[]{:S(2)}, u32[]{:S(2)}) collective-permute-start(bf16[384,2048]{1,0:T(8,128)(2,1)} %pad_maximum_fusion.2), channel_id=1, source_target_pairs={{0,8},{8,0},{16,24},{24,16},{1,9},{9,1},{17,25},{25,17},{2,10},{10... | collective-permute-start | bytes 4718600 | tf_op jit(solution)/shard_map/ppermute | solution.py:27
  206.0 9.0 %collective-permute-start.12 = (bf16[768,128]{1,0:T(8,128)(2,1)S(1)}, bf16[768,128]{1,0:T(8,128)(2,1)S(1)}, u32[]{:S(2)}, u32[]{:S(2)}) collective-permute-start(bf16[768,128]{1,0:T(8,128)(2,1)S(1)} %add_convert_fusion.4), channel_id=1, source_target_pairs={{0,2},{1,3},{2,0},{3,1},{4,6},{5,7},{6,4},{7,5},{8,10},{9,11},{10,... | collective-permute-start | bytes 589832 | tf_op jit(solution)/shard_map/ppermute | solution.py:27
  207.7 2.6 copy-start.10
  209.8 17.8 %collective-permute-start.1 = (bf16[768,256]{1,0:T(8,128)(2,1)}, bf16[768,256]{1,0:T(8,128)(2,1)}, u32[]{:S(2)}, u32[]{:S(2)}) collective-permute-start(bf16[768,256]{1,0:T(8,128)(2,1)} %add_convert_fusion.1), channel_id=1, source_target_pairs={{0,2},{1,3},{2,0},{3,1},{4,6},{5,7},{6,4},{7,5},{8,10},{9,11},{10,... | collective-permute-start | bytes 1179656 | tf_op jit(solution)/shard_map/ppermute | solution.py:27
  215.0 5.9 %copy-start.5 = (bf16[768,512]{1,0:T(8,128)(2,1)S(1)}, bf16[768,512]{1,0:T(8,128)(2,1)}, u32[]{:S(2)}) copy-start(bf16[768,512]{1,0:T(8,128)(2,1)} %shard_map.128) | copy-start | bytes 2359300
  215.0 1.5 copy-start.7
  216.0 13.8 %collective-permute-start.13 = (bf16[768,128]{1,0:T(8,128)(2,1)}, bf16[768,128]{1,0:T(8,128)(2,1)}, u32[]{:S(2)}, u32[]{:S(2)}) collective-permute-start(bf16[768,128]{1,0:T(8,128)(2,1)} %pad_maximum_fusion.8), channel_id=1, source_target_pairs={{0,4},{4,0},{1,5},{5,1},{2,6},{6,2},{3,7},{7,3},{8,12},{12,8},{9,1... | collective-permute-start | bytes 589832 | tf_op jit(solution)/shard_map/ppermute | solution.py:23
  220.8 9.0 %copy-start.2 = (bf16[768,128]{1,0:T(8,128)(2,1)S(1)}, bf16[768,128]{1,0:T(8,128)(2,1)}, u32[]{:S(2)}) copy-start(bf16[768,128]{1,0:T(8,128)(2,1)} %add_convert_fusion.5.refs_0_) | copy-start | bytes 589828
  220.8 9.0 %copy-start.8 = (bf16[768,128]{1,0:T(8,128)(2,1)S(1)}, bf16[768,128]{1,0:T(8,128)(2,1)}, u32[]{:S(2)}) copy-start(bf16[768,128]{1,0:T(8,128)(2,1)} %copy-done.7) | copy-start | bytes 589828
  223.0 50.2 %all-to-all-start.3 = ((bf16[16,48,768]{2,1,0:T(8,128)(2,1)}), bf16[16,48,768]{2,1,0:T(8,128)(2,1)}, u32[]{:S(2)}, u32[]{:S(2)}) async-start(bf16[16,48,768]{2,1,0:T(8,128)(2,1)} %bitcast.61), calls=%async_computation.3 | async-start | bytes 2359296 | tf_op jit(solution)/shard_map/all_to_all | solution.py:18
  275.0 0.9 copy-start.14

commit v3 on v2

v3 whole, which is shorter than its diff:
```python
import functools

import jax
import jax.numpy as jnp
from jax import lax
from jax.experimental import pallas as pl
from jax.experimental.pallas import tpu as pltpu
from jax.sharding import Mesh
from jax.sharding import PartitionSpec as P

ADAPTER_SCALE = 0.5
PIECES = (2, 2)
SPLIT = 128
HINT = 1000
LANES = 128
VMEM = 56 * 1024 * 1024


def exchange(pieces, axes):
    return lax.all_to_all(pieces, axes, split_axis=0, concat_axis=0, tiled=True)


def shift(array, axis, step):
    size = lax.axis_size(axis)
    return lax.ppermute(array, axis, [(i, (i + step) % size) for i in range(size)])


def swap(array, axis, bit):
    return lax.ppermute(array, axis, [(i, i ^ bit) for i in range(lax.axis_size(axis))])


def after(value, *earlier):
    return lax.optimization_barrier((value,) + earlier)[0]


def add(a, b):
    return (a.astype(jnp.float32) + b.astype(jnp.float32)).astype(jnp.bfloat16)


def bits_below(size):
    return [1 << i for i in range(size.bit_length() - 1)]


def tensor_sum(total, bits=None):
    for bit in bits_below(lax.axis_size("tensor")) if bits is None else bits:
        total = add(total, swap(total, "tensor", bit))
    return total


def scatter_columns(term):
    size = lax.axis_size("tensor")
    share = lax.axis_index("tensor")
    width = term.shape[1] // size
    blocks = [
        lax.dynamic_slice_in_dim(term, (share ^ i) * width, width, 1) for i in range(size)
    ]
    for bit in bits_below(size):
        kept = [i for i in range(size) if i % (2 * bit) == 0]
        got = swap(jnp.concatenate([blocks[i ^ bit] for i in kept], axis=1), "tensor", bit)
        for n, i in enumerate(kept):
            blocks[i] = add(blocks[i], got[:, n * width : (n + 1) * width])
    return blocks[0]


def dot(a, b, ca, cb):
    return lax.dot_general(a, b, (((ca,), (cb,)), ((), ())), preferred_element_type=jnp.float32)


def call(body, grid, in_specs, out_spec, out_shape, operands, flops, scratch=()):
    moved = sum(x.size * x.dtype.itemsize for x in operands)
    return pl.pallas_call(
        body,
        grid=grid,
        in_specs=in_specs,
        out_specs=out_spec,
        out_shape=out_shape,
        scratch_shapes=list(scratch),
        compiler_params=pltpu.CompilerParams(vmem_limit_bytes=VMEM),
        cost_estimate=pl.CostEstimate(flops=flops // HINT, bytes_accessed=moved // HINT, transcendentals=0),
    )(*operands)


def whole(array):
    return pl.BlockSpec(array.shape, lambda i: (0,) * array.ndim)


def fold_body(count, rank, scale, *refs):
    lines, weight, column_slots, slots = refs[:count], refs[count], refs[count + 1], refs[count + 2]
    out = refs[-1]
    step = max(rank, LANES)
    results = []
    for n in range(count):
        full = dot(lines[n][...], weight[...], 1, 1)
        full = jnp.where(slots[:, n : n + 1] == column_slots[...], full, 0.0)
        total = full[:, :step]
        for i in range(step, full.shape[1], step):
            total += full[:, i : i + step]
        results.append(sum(total[:, i : i + rank] for i in range(0, step, rank)))
    result = scale * jnp.concatenate(results, axis=1)
    if len(refs) == count + 5:
        result += refs[count + 3][...]
    out[...] = result.astype(out.dtype)


def fold_product(lines, weight, block, column_slots, slots, rank, scale, before, dtype):
    count = len(lines)
    rows = slots.shape[0]
    tile = rows // 2
    offset, depth = block
    specs = [
        pl.BlockSpec((tile, depth), functools.partial(lambda o, i: (i, o), 0))
        if line.shape[1] == depth
        else pl.BlockSpec((tile, depth), lambda i: (i, offset))
        for line in lines
    ]
    specs.append(pl.BlockSpec((weight.shape[0], depth), lambda i: (0, offset)))
    specs.append(whole(column_slots))
    specs.append(pl.BlockSpec((tile, count), lambda i: (i, 0)))
    operands = list(lines) + [weight, column_slots, slots]
    out_spec = pl.BlockSpec((tile, count * rank), lambda i: (i, 0))
    if before is not None:
        specs.append(out_spec)
        operands.append(before)
    return call(
        functools.partial(fold_body, count, rank, scale),
        (2,),
        specs,
        out_spec,
        jax.ShapeDtypeStruct((rows, count * rank), dtype),
        operands,
        2 * count * rows * weight.shape[0] * depth,
    )


def weight_body(count, rank, scale, *refs):
    compact, row_slots, column_slots, select = refs[:4]
    lines, out, spread = refs[4 : 4 + count], refs[-2], refs[-1]

    @pl.when(pl.program_id(0) == 0)
    def _():
        for n in range(count):
            wide = dot(select[...], compact[:, n * rank : (n + 1) * rank], 1, 1)
            mine = column_slots[...] == row_slots[n : n + 1, :]
            spread[n] = jnp.where(mine, wide, 0.0).astype(jnp.bfloat16)

    total = dot(spread[0], lines[0][...], 1, 0)
    for n in range(1, count):
        total += dot(spread[n], lines[n][...], 1, 0)
    out[...] = (scale * total).astype(out.dtype)


def weight_product(compact, row_slots, column_slots, select, lines, block, scale):
    count = len(lines)
    rows = row_slots.shape[1]
    columns, rank = select.shape
    offset, width = block
    tile = min(width, 512)
    per = width // tile
    specs = [whole(x) for x in (compact, row_slots, column_slots, select)]
    for line in lines:
        skip = 0 if line.shape[1] == width else offset * per
        specs.append(pl.BlockSpec((rows, tile), functools.partial(lambda s, i: (0, s + i), skip)))
    return call(
        functools.partial(weight_body, count, rank, scale),
        (per,),
        specs,
        pl.BlockSpec((columns, tile), lambda i: (0, i)),
        jax.ShapeDtypeStruct((columns, width), jnp.bfloat16),
        [compact, row_slots, column_slots, select] + list(lines),
        2 * count * rows * columns * width,
        [pltpu.VMEM((count, columns, rows), jnp.bfloat16)],
    )


def input_body(count, *refs):
    scaled, frozen, compact, slots = refs[:4]
    columns, selects, downs = (refs[4 + i * count : 4 + (i + 1) * count] for i in range(3))
    out, spreads = refs[-1 - count], refs[-count:]

    @pl.when(pl.program_id(0) == 0)
    def _():
        for n in range(count):
            wide = dot(compact[...], selects[n][...], 1, 0)
            mine = slots[...] == columns[n][...]
            spreads[n][...] = jnp.where(mine, wide, 0.0).astype(jnp.bfloat16)

    total = dot(scaled[...], frozen[...], 1, 1)
    for n in range(count):
        total += dot(spreads[n][...], downs[n][...], 1, 0)
    out[...] = total.astype(out.dtype)


def input_product(scaled, frozen, compact, slots, columns, selects, downs, tile):
    count = len(downs)
    rows, values = scaled.shape
    width = downs[0].shape[1]
    specs = [whole(scaled), pl.BlockSpec((tile, values), lambda i: (i, 0))]
    specs += [whole(x) for x in [compact, slots] + columns + selects]
    specs += [pl.BlockSpec((x.shape[0], tile), lambda i: (0, i)) for x in downs]
    return call(
        functools.partial(input_body, count),
        (width // tile,),
        specs,
        pl.BlockSpec((rows, tile), lambda i: (0, i)),
        jax.ShapeDtypeStruct((rows, width), jnp.bfloat16),
        [scaled, frozen, compact, slots] + columns + selects + list(downs),
        2 * rows * width * (values + sum(x.shape[0] for x in downs)),
        [pltpu.VMEM((rows, x.shape[0]), jnp.bfloat16) for x in downs],
    )


def output_body(count, *refs):
    compact, slots, column_slots, select, ups = refs[count : count + 5]
    out = refs[-1]
    wide = dot(compact[...], select[...], 1, 0)
    spread = jnp.where(slots[...] == column_slots[...], wide, 0.0).astype(jnp.bfloat16)
    result = ADAPTER_SCALE * dot(spread, ups[...], 1, 0)
    for addend in refs[:count]:
        result += addend[...].astype(jnp.float32)
    out[...] = result.astype(out.dtype)


def output_product(addends, compact, slots, column_slots, select, ups):
    rows, width = compact.shape[0], ups.shape[1]
    tile = rows // 2
    line = lambda i: (i, 0)
    operands = list(addends) + [compact, slots]
    specs = [pl.BlockSpec((tile, x.shape[1]), line) for x in operands]
    operands += [column_slots, select, ups]
    specs += [whole(x) for x in operands[-3:]]
    return call(
        functools.partial(output_body, len(addends)),
        (rows // tile,),
        specs,
        pl.BlockSpec((tile, width), line),
        jax.ShapeDtypeStruct((rows, width), jnp.bfloat16),
        operands,
        2 * rows * width * ups.shape[0],
    )


def total_body(planes, shares, width, last_width, value_width, *refs):
    out_down, out_up = refs[-2:]
    position = 0
    for ref in refs[:-2]:
        last = ref is refs[-3]
        columns = last_width if last else ref.shape[2]
        for share in range(shares):
            total = sum(ref[q * shares + share].astype(jnp.float32) for q in range(planes))
            start = share * width + position
            out_down[:, start : start + columns] = total[:, :columns].astype(jnp.bfloat16)
            if last:
                start = share * value_width
                out_up[:, start : start + value_width] = total[:, columns:].astype(jnp.bfloat16)
        position += columns


def total_product(arrived, planes, shares, width, last_width, value_width):
    lot = arrived[0].shape[1]
    shapes = [
        jax.ShapeDtypeStruct((lot, shares * columns), jnp.bfloat16)
        for columns in (width, value_width)
    ]
    return call(
        functools.partial(total_body, planes, shares, width, last_width, value_width),
        (1,),
        [whole(x) for x in arrived],
        [whole(x) for x in shapes],
        shapes,
        arrived,
        1000,
    )


def choose(ranks, rank):
    return (jnp.arange(rank, dtype=jnp.int32)[:, None] == ranks[None, :]).astype(jnp.bfloat16)


def shards(
    tokens,
    frozen_value_weight,
    adapter_down_weight,
    adapter_up_weight,
    cotangent,
    language_pair_index,
    language_pair_counts,
    adapter_owner_table,
):
    sides = lax.axis_size("adapter")
    shares = lax.axis_size("tensor")
    far, near = lax.axis_size("far"), lax.axis_size("near")
    planes = far * near
    side = lax.axis_index("adapter")
    share = lax.axis_index("tensor")
    plane = lax.axis_index(("far", "near"))
    close = lax.axis_index("near")
    rows, width = tokens.shape
    stored, rank, _ = adapter_down_weight.shape
    values = cotangent.shape[1]
    value_width = values // shares
    own = shares * stored
    piece = rank // planes
    lot = stored * piece
    steps = range(1, sides)

    quarter = lax.dynamic_slice_in_dim(adapter_down_weight, plane * piece, piece, 1)
    quarter = quarter.reshape(lot, shares * width)
    parcel = jnp.stack([quarter[:, s * width : (s + 1) * width] for s in range(shares)])
    parcel = jnp.broadcast_to(parcel[None], (sides,) + parcel.shape)
    parcel = parcel.reshape(sides * shares, lot, width)
    got = exchange(parcel, ("adapter", "tensor"))

    quarters = []
    for j in steps:
        block = lax.dynamic_slice(
            got, (((side - j) % sides) * shares, 0, 0), (shares, lot, width)
        ).reshape(own * piece, width)
        quarters.append([block] + [shift(block, "near", i) for i in range(1, near)])
    shared = [block for blocks in quarters for block in blocks]

    pairs = jnp.arange(adapter_owner_table.shape[0], dtype=jnp.int32)
    matches = language_pair_index[:, None] == pairs[None, :]
    slots = jnp.sum(jnp.where(matches, adapter_owner_table[None, :], 0), axis=1)
    row_counts = jnp.sum(jnp.where(matches, language_pair_counts[0][None, :], 0), axis=1)
    row_weight = 1.0 / row_counts.astype(jnp.float32)
    scaled = (cotangent.astype(jnp.float32) * row_weight[:, None]).astype(jnp.bfloat16)
    scaled_part = lax.dynamic_slice_in_dim(scaled, share * value_width, value_width, 1)

    tag_rows = -(-rows // value_width)
    tags = jnp.pad(slots, (0, tag_rows * value_width - rows)).reshape(tag_rows, value_width)
    tags = jnp.concatenate([tags // SPLIT, tags % SPLIT]).astype(jnp.bfloat16)
    tags = jnp.pad(tags, ((0, -2 * tag_rows % 16), (0, 0)))
    message = after(jnp.concatenate([scaled_part, tags]), parcel)
    scaled_of, slots_of = [scaled_part], [slots]
    for j in steps:
        answer = shift(message, "adapter", j)
        scaled_of.append(answer[:rows])
        numbers = answer[rows : rows + 2 * tag_rows].astype(jnp.int32)
        numbers = numbers[:tag_rows] * SPLIT + numbers[tag_rows:]
        slots_of.append(numbers.reshape(-1)[:rows])
    row_slots = jnp.stack(slots_of)
    slot_columns = row_slots.T

    def over_shares(matrix):
        columns = matrix.shape[1] // shares
        sent = [
            lax.dynamic_slice_in_dim(matrix, (share ^ k) * columns, columns, 1)
            for k in range(shares)
        ]
        return jnp.concatenate(
            [sent[0]] + [swap(sent[k], "tensor", k) for k in range(1, shares)]
        )

    own_ups = over_shares(adapter_up_weight.reshape(stored * rank, values))
    down_flat = after(adapter_down_weight.reshape(stored * rank, shares * width), own_ups)
    own_down = over_shares(down_flat)
    gated_ups = after(own_ups, own_down, *shared)

    pieces, position = [], 0
    for part in PIECES:
        piece_width = width // part
        others = tokens[:, position : position + piece_width]
        others = after(others, own_ups)
        pieces.append(
            (
                (position // piece_width, piece_width),
                [tokens] + [shift(others, "adapter", j) for j in steps],
            )
        )
        position += piece_width

    base_term = dot(tokens, frozen_value_weight, 1, 0).astype(jnp.bfloat16)

    column = jnp.arange(own * rank, dtype=jnp.int32)
    sent_slots = (side * shares + (share ^ (column // (stored * rank)))) * stored
    sent_slots += (column // rank) % stored
    sent_select = choose(column % rank, rank)
    part_local = (column % (own * piece)) // piece
    part_plane = column // (own * piece)
    part_plane = (part_plane % far) * near + part_plane // far
    part_ranks = part_plane * piece + column % piece
    part_slots = (side * own + part_local)[:, None]
    part_select = choose(part_ranks, rank).T

    back_part = fold_product(
        scaled_of,
        gated_ups,
        (0, value_width),
        sent_slots[None, :],
        slot_columns,
        rank,
        ADAPTER_SCALE,
        None,
        jnp.bfloat16,
    )
    back_part, base_term = lax.optimization_barrier((back_part, base_term))
    back_all = tensor_sum(back_part)
    back = back_all[:, :rank]
    for j in steps:
        back = back + shift(back_all[:, j * rank : (j + 1) * rank], "adapter", -j)


    base_share = scatter_columns(base_term)
    back_gate = back_all
    low_part = None
    parts_down = []
    for n, (block, lines) in enumerate(pieces):
        last = n == len(pieces) - 1

        def gradient():
            return weight_product(
                back_gate, row_slots, part_slots, part_select, lines, block, 1.0
            )

        if not last:
            parts_down.append(gradient())
            own_down = after(own_down, parts_down[-1])
        low_part = fold_product(
            lines,
            own_down,
            block,
            sent_slots[None, :],
            slot_columns,
            rank,
            1.0,
            low_part,
            jnp.bfloat16 if last else jnp.float32,
        )
        if last:
            low_part = tensor_sum(low_part, bits_below(shares)[:1])
        low_part, back_gate, base_share = lax.optimization_barrier(
            (low_part, back_gate, base_share)
        )
        if last:
            parts_down.append(gradient())
    bundle = rank // far
    by_rank = own_down.reshape(own, rank, width)
    rests = []
    for j in steps:
        for i in range(1, far):
            start = (plane // near + i) % far * bundle
            rest = lax.dynamic_slice_in_dim(by_rank, start, bundle, 1)
            rests.append(shift(rest.reshape(own * bundle, width), "adapter", j))

    def fold(part):
        half = part.shape[0] // near
        kept = lax.dynamic_slice_in_dim(part, close * half, half, 0)
        for j in range(1, near):
            away = lax.dynamic_slice_in_dim(part, ((close + j) % near) * half, half, 0)
            kept = add(kept, shift(away, "near", j))
        return kept

    def send(part):
        return exchange(part.reshape(far * shares, lot, part.shape[1]), ("far", "tensor"))

    parts_down = [fold(part) for part in parts_down]
    first = send(after(parts_down[0], *pieces[1][1][1:]))
    low_all = tensor_sum(low_part, bits_below(shares)[1:])
    up_part = weight_product(
        low_all, row_slots, part_slots, part_select, scaled_of, (0, value_width), ADAPTER_SCALE
    )
    last_width = parts_down[-1].shape[1]
    parts_down[-1] = jnp.concatenate([parts_down[-1], fold(up_part)], axis=1)
    parts_down[-1] = after(parts_down[-1], *rests)

    arrived = [first]
    for part in parts_down[1:]:
        arrived.append(send(after(part, arrived[-1])))
    grad_down, grad_up = total_product(arrived, far, shares, width, last_width, value_width)
    grad_down = grad_down.reshape(stored, piece, shares * width)
    grad_up = grad_up.reshape(stored, piece, values)

    addends = [base_share]
    for j in steps:
        theirs = output_product(
            [],
            low_all[:, j * rank : (j + 1) * rank],
            slots_of[j][:, None],
            sent_slots[None, :],
            sent_select,
            own_ups,
        )
        addends.append(shift(theirs, "adapter", -j))
    columns, selects, downs = [sent_slots[None, :]], [sent_select], [own_down]

    def block(weights, block_slots, block_ranks):
        columns.append(block_slots[None, :])
        selects.append(choose(block_ranks, rank))
        downs.append(weights)

    quarter_column = column[: own * piece]
    bundle_column = column[: own * bundle]
    for j in steps:
        away = (side - j) % sides
        for i, weights in enumerate(quarters[j - 1]):
            from_plane = plane - close + (close - i) % near
            block(
                weights,
                away * own + quarter_column // piece,
                from_plane * piece + quarter_column % piece,
            )
        for i in range(1, far):
            adapter = bundle_column // bundle
            block(
                rests[(j - 1) * (far - 1) + i - 1],
                (away * shares + (share ^ (adapter // stored))) * stored + adapter % stored,
                (plane // near + i) % far * bundle + bundle_column % bundle,
            )
    input_gradient = input_product(
        scaled,
        frozen_value_weight,
        back,
        slots[:, None],
        columns,
        selects,
        downs,
        max(LANES, 1024 // sides),
    )
    addends[0] = after(addends[0], input_gradient)
    mixed_out = output_product(
        addends, low_all[:, :rank], slots[:, None], sent_slots[None, :], sent_select, own_ups
    )
    return mixed_out, input_gradient, grad_down, grad_up


def solution(mesh):
    planes = mesh.shape["dp"]
    near = 2 if planes % 2 == 0 else 1
    split = Mesh(
        mesh.devices.reshape((planes // near, near) + mesh.devices.shape[1:]),
        ("far", "near") + tuple(mesh.axis_names[1:]),
    )
    dp = ("far", "near")
    lines = dp + ("adapter",)
    return jax.shard_map(
        shards,
        mesh=split,
        in_specs=(
            P(lines, "tensor"),
            P("tensor", None),
            P(("adapter", "tensor"), None, None),
            P(("adapter", "tensor"), None, None),
            P(lines, None),
            P(lines),
            P(lines, None),
            P(),
        ),
        out_specs=(
            P(lines, "tensor"),
            P(lines, "tensor"),
            P(("adapter", "tensor"), dp, None),
            P(("adapter", "tensor"), dp, None),
        ),
        check_vma=False,
    )
```

time: 277 us -> 209 us (0.75)
  waiting for transfers between devices: 126 us -> 62 us
  other arithmetic: 33.5 us -> 24.9 us
  local copies, waits for them, and re-layouts: 17.2 us -> 24.6 us
    ppermute x11 -> x12, waiting for transfers between devices: 73 us -> 24.8 us  [swap(): lax.ppermute(array, axis, [(i, i ^ bit) for i in range(lax.axis_size(axis...]
    ppermute x5 -> x10, waiting for transfers between devices: 47.9 us -> 37.2 us  [shift(): lax.ppermute(array, axis, [(i, (i + step) % size) for i in range(size)])]
    all_to_all x4 -> x3, starting transfers between devices: 22.2 us -> 13.5 us  [exchange(): return lax.all_to_all(pieces, axes, split_axis=0, concat_axis=0, tiled=True)]
    ppermute x5 -> x10, starting transfers between devices: 4.74 us -> 10.7 us  [shift(): lax.ppermute(array, axis, [(i, (i + step) % size) for i in range(size)])]
    concatenate x7 -> x4, other arithmetic: 12.4 us -> 6.69 us  [the longest x2 4.83 us: over_shares(): jnp.concatenate([sent[0]] + [swap(sent[k], 'tensor', k) for k in range(1,...]
    all_to_all x4 -> x3, waiting for transfers between devices: 5.46 us -> 0.01 us  [exchange(): return lax.all_to_all(pieces, axes, split_axis=0, concat_axis=0, tiled=True)]
    dynamic_slice x2 -> x6, local copies, waits for them, and re-layouts: 2.49 us -> 7.9 us  [the longest x3 3.31 us: fold(): away = lax.dynamic_slice_in_dim(part, (close + j) % near * half, half, 0)]
    unnamed x52 -> x46, local copies, waits for them, and re-layouts: 1.35 us -> 5.36 us
  transfers between devices with their start and end apart: 20 -> 25, of which waited for: 9 -> 8; matrix products, arithmetic and copies ran while one was open for 18% -> 24% of each run, Pallas kernels for 20% -> 25%
where the time goes in v3:
time: 209 us; the launch traced here: 208 us
  waiting for transfers between devices  62 us (30%)
  Pallas kernels  55.2 us (26%)
  starting transfers between devices  33.5 us (16%)
  other arithmetic  24.9 us (12%)
  local copies, waits for them, and re-layouts  24.6 us (12%)
  matrix products  6.82 us (3%)
    pallas_call x10, Pallas kernels, call(): pl.pallas_call(body, grid=grid, in_specs=in_specs, out_specs=out_spec, ou...  55.2 us
    ppermute x10, waiting for transfers between devices, shift(): lax.ppermute(array, axis, [(i, (i + step) % size) for i in range(size)])  37.2 us
    ppermute x12, waiting for transfers between devices, swap(): lax.ppermute(array, axis, [(i, i ^ bit) for i in range(lax.axis_size(axis...  24.8 us
    all_to_all x3, starting transfers between devices, exchange(): return lax.all_to_all(pieces, axes, split_axis=0, concat_axis=0, tiled=True)  13.5 us
    ppermute x10, starting transfers between devices, shift(): lax.ppermute(array, axis, [(i, (i + step) % size) for i in range(size)])  10.7 us
    ppermute x12, starting transfers between devices, swap(): lax.ppermute(array, axis, [(i, i ^ bit) for i in range(lax.axis_size(axis...  9.34 us
    convert_element_type x9, other arithmetic, add(): return (a.astype(jnp.float32) + b.astype(jnp.float32)).astype(jnp.bfloat16)  8.04 us
    dot_general x1, matrix products, dot(): lax.dot_general(a, b, (((ca,), (cb,)), ((), ())), preferred_element_type=...  6.82 us
  transfers between devices with their start and end apart: 25, of which 8 were waited for; matrix products, arithmetic and copies ran while one was open for 24% of the time, Pallas kernels for 25%

profile of v3, /device:TPU:0, one launch (start us, length us, event | category | flops | bytes accessed | tf_op | source)
XLA Modules:
  0.0 208.0 jit_solution(17003020811217827884)
XLA Ops:
  0.7 1.8 constant_dynamic-slice_fusion.16
  2.9 2.5 %collective-permute-start.1 = (bf16[192,256]{1,0:T(8,128)(2,1)}, bf16[192,256]{1,0:T(8,128)(2,1)}, u32[]{:S(2)}, u32[]{:S(2)}) collective-permute-start(bf16[192,256]{1,0:T(8,128)(2,1)} %get-tuple-element.62), channel_id=1, source_target_pairs={{0,2},{1,3},{2,0},{3,1},{4,6},{5,7},{6,4},{7,5},{8,10},{9,11},{10,... | collective-permute-start | bytes 294920 | tf_op jit(solution)/shard_map/ppermute | solution.py:29
  5.6 1.2 constant_dynamic-slice_fusion.7
  7.0 1.4 broadcast_in_dim.32
  8.3 4.4 %all-to-all-start = ((bf16[8,48,2048]{2,1,0:T(8,128)(2,1)}), bf16[8,48,2048]{2,1,0:T(8,128)(2,1)}, u32[]{:S(2)}, u32[]{:S(2)}) async-start(bf16[8,48,2048]{2,1,0:T(8,128)(2,1)} %bitcast.8), calls=%async_computation | async-start | bytes 3145728 | tf_op jit(solution)/shard_map/all_to_all | solution.py:20
  12.9 1.9 multiply_convert_fusion.refs_0_
  14.8 1.1 copy-done.2
  16.1 0.8 pad_maximum_fusion.4
  16.9 1.9 collective-permute-start.7
  18.9 2.1 %fusion.47 = (bf16[768,1024]{1,0:T(8,128)(2,1)}, bf16[768,1024]{1,0:T(8,128)(2,1)}) fusion(bf16[768,2048]{1,0:T(8,128)(2,1)S(1)} %copy-done), kind=kLoop, calls=%fused_computation.158 | loop fusion | bytes 6291456 | tf_op jit(solution)/shard_map/slice | solution.py:362
  21.0 6.8 %convolution_convert_fusion = bf16[768,1024]{1,0:T(8,128)(2,1)} fusion(bf16[768,2048]{1,0:T(8,128)(2,1)S(1)} %copy-done, bf16[2048,1024]{1,0:T(8,128)(2,1)} %refs_1_.1), kind=kOutput, calls=%fused_computation.2 | convolution fusion | flops 3222011904 | bytes 8912896 | tf_op jit(solution)/shard_map/dot_general | solution.py:66
  28.4 1.8 pad_maximum_fusion.5.refs_2_.refs_4_.refs_6_
  30.2 1.5 constant_dynamic-slice_fusion.12
  31.7 1.5 collective-permute-start.5
  33.9 1.2 constant_dynamic-slice_fusion.6
  35.0 6.9 %collective-permute-done.7 = bf16[784,256]{1,0:T(8,128)(2,1)} collective-permute-done((bf16[784,256]{1,0:T(8,128)(2,1)}, bf16[784,256]{1,0:T(8,128)(2,1)}, u32[]{:S(2)}, u32[]{:S(2)}) %collective-permute-start.7) | collective-permute-done | bytes 401440 | tf_op jit(solution)/shard_map/ppermute | solution.py:25
  41.9 1.8 collective-permute-start.8
  43.7 0.7 slice_convert_fusion
  45.0 1.0 copy.22.refs_4_
  46.0 1.8 slice.84.refs_1_.refs_5_
  47.8 4.6 %collective-permute-done.5 = bf16[192,2048]{1,0:T(8,128)(2,1)} collective-permute-done((bf16[192,2048]{1,0:T(8,128)(2,1)}, bf16[192,2048]{1,0:T(8,128)(2,1)}, u32[]{:S(2)}, u32[]{:S(2)}) %collective-permute-start.5) | collective-permute-done | bytes 786464 | tf_op jit(solution)/shard_map/ppermute | solution.py:29
  52.3 16.1 %collective-permute-done.6 = bf16[192,2048]{1,0:T(8,128)(2,1)} collective-permute-done((bf16[192,2048]{1,0:T(8,128)(2,1)}, bf16[192,2048]{1,0:T(8,128)(2,1)}, u32[]{:S(2)}, u32[]{:S(2)}) %collective-permute-start.6) | collective-permute-done | bytes 786464 | tf_op jit(solution)/shard_map/ppermute | solution.py:29
  68.4 3.1 %pad_maximum_fusion.refs_2_.refs_12_ = bf16[768,2048]{1,0:T(8,128)(2,1)} fusion(bf16[192,2048]{1,0:T(8,128)(2,1)} %collective-permute-done.6, bf16[192,2048]{1,0:T(8,128)(2,1)} %collective-permute-done.5, bf16[192,2048]{1,0:T(8,128)(2,1)} %collective-permute-done.4, bf16[192,2048]{1,0:T(8,128)(2,1)S(1)} %get-tuple-element.50), kind=kLoop, calls=%fused_computation | loop fusion | flops 12582912 | bytes 6291456 | tf_op jit(solution)/shard_map/concatenate | solution.py:350
  71.5 3.5 %shard_map.111 = bf16[768,128]{1,0:T(8,128)(2,1)} custom-call(bf16[768,256]{1,0:T(8,128)(2,1)} %copy-done.6, bf16[768,256]{1,0:T(8,128)(2,1)} %slice.84.refs_1_.refs_5_, bf16[768,256]{1,0:T(8,128)(2,1)} %pad_maximum_fusion.5.refs_2_.refs_4_.refs_6_, s32[1,768]{1,0:T(1,128)} %fusion.36.refs_3_.refs_4_.refs_2_, s32[768,2]{1,0:T(8,128)} %copy.22.refs_4_), custom_call_target="tpu_custom_call" | custom-call | flops 603979 | bytes 1188 | tf_op jit(solution)/shard_map/pallas_call | solution.py:71
  75.1 0.9 pad_maximum_fusion.3
  77.0 1.1 fusion.1.refs_2_
  78.2 0.8 fusion.7.refs_3_
  79.6 1.7 collective-permute-start.10
  81.3 2.0 add_convert_fusion.3
  83.7 3.5 %collective-permute-done.10 = bf16[768,128]{1,0:T(8,128)(2,1)S(1)} collective-permute-done((bf16[768,128]{1,0:T(8,128)(2,1)S(1)}, bf16[768,128]{1,0:T(8,128)(2,1)S(1)}, u32[]{:S(2)}, u32[]{:S(2)}) %collective-permute-start.10) | collective-permute-done | bytes 196640 | tf_op jit(solution)/shard_map/ppermute | solution.py:29
  87.2 0.7 add_convert_fusion.8.refs_0_
  87.9 1.2 copy-done.3
  89.2 6.1 %shard_map.112 = bf16[768,1024]{1,0:T(8,128)(2,1)} custom-call(bf16[768,128]{1,0:T(8,128)(2,1)} %add_convert_fusion.8.refs_0_, s32[2,768]{1,0:T(2,128)} %get-tuple-element.66.refs_1_, s32[768,1]{1,0:T(8,128)} %fusion.1.refs_2_, bf16[768,64]{1,0:T(8,128)(2,1)} %fusion.7.refs_3_, bf16[768,2048]{1,0:T(8,128)(2,1)} %refs_4_.3, bf16[768,1024]{1,0:T(8,128)(2,1)} %copy-done.3), custom_call_target="tpu_custom_call" | custom-call | flops 2415919 | bytes 5022 | tf_op jit(solution)/shard_map/pallas_call | solution.py:71
  95.3 1.2 constant_dynamic-slice_fusion.2
  96.5 1.8 collective-permute-start.19
  98.4 6.0 %shard_map.113.refs_5_ = f32[768,128]{1,0:T(8,128)} custom-call(bf16[768,2048]{1,0:T(8,128)(2,1)} %refs_4_.3, bf16[768,1024]{1,0:T(8,128)(2,1)} %copy-done.3, bf16[768,2048]{1,0:T(8,128)(2,1)} %pad_maximum_fusion.refs_2_.refs_12_, s32[1,768]{1,0:T(1,128)} %fusion.36.refs_3_.refs_4_.refs_2_, s32[768,2]{1,0:T(8,128)} %copy.22.refs_4_), custom_call_target="tpu_custom_call" | custom-call | flops 2415919 | bytes 7873 | tf_op jit(solution)/shard_map/pallas_call | solution.py:71
  104.4 2.0 add_convert_fusion.2.refs_0_
  106.4 7.0 %collective-permute-done.3.refs_1_.refs_5_ = bf16[768,1024]{1,0:T(8,128)(2,1)} collective-permute-done((bf16[768,1024]{1,0:T(8,128)(2,1)S(1)}, bf16[768,1024]{1,0:T(8,128)(2,1)}, u32[]{:S(2)}, u32[]{:S(2)}) %collective-permute-start.3) | collective-permute-done | bytes 1572896 | tf_op jit(solution)/shard_map/ppermute | solution.py:25
  113.4 6.1 %shard_map.114 = bf16[768,128]{1,0:T(8,128)(2,1)} custom-call(bf16[768,2048]{1,0:T(8,128)(2,1)} %refs_4_.3, bf16[768,1024]{1,0:T(8,128)(2,1)} %collective-permute-done.3.refs_1_.refs_5_, bf16[768,2048]{1,0:T(8,128)(2,1)} %pad_maximum_fusion.refs_2_.refs_12_, s32[1,768]{1,0:T(1,128)} %fusion.36.refs_3_.refs_4_.refs_2_, s32[768,2]{1,0:T(8,128)} %copy.22.refs_4_, ...), custom_call_target="tpu_custom_call" | custom-call | flops 2415919 | bytes 8266 | tf_op jit(solution)/shard_map/pallas_call | solution.py:71
  119.5 1.3 constant_dynamic-slice_fusion.3
  121.2 1.8 collective-permute-start.17
  123.0 1.2 add_convert_fusion.1
  124.2 4.1 %all-to-all-start.1 = ((bf16[8,48,1024]{2,1,0:T(8,128)(2,1)}), bf16[8,48,1024]{2,1,0:T(8,128)(2,1)S(1)}, u32[]{:S(2)}, u32[]{:S(2)}) async-start(bf16[8,48,1024]{2,1,0:T(8,128)(2,1)} %bitcast.14), calls=%async_computation.1 | async-start | bytes 1572864 | tf_op jit(solution)/shard_map/all_to_all | solution.py:20
  128.3 6.1 %shard_map.118 = bf16[768,1024]{1,0:T(8,128)(2,1)} custom-call(bf16[768,128]{1,0:T(8,128)(2,1)} %add_convert_fusion.8.refs_0_, s32[2,768]{1,0:T(2,128)} %get-tuple-element.66.refs_1_, s32[768,1]{1,0:T(8,128)} %fusion.1.refs_2_, bf16[768,64]{1,0:T(8,128)(2,1)} %fusion.7.refs_3_, bf16[768,2048]{1,0:T(8,128)(2,1)} %refs_4_.3, ...), custom_call_target="tpu_custom_call" | custom-call | flops 2415919 | bytes 5022 | tf_op jit(solution)/shard_map/pallas_call | solution.py:71
  134.4 1.2 constant_dynamic-slice_fusion.1
  135.6 1.7 collective-permute-start.20
  137.3 0.7 add_convert_fusion.6.refs_0_
  138.0 4.4 %shard_map.119 = bf16[768,256]{1,0:T(8,128)(2,1)} custom-call(bf16[768,128]{1,0:T(8,128)(2,1)} %add_convert_fusion.6.refs_0_, s32[2,768]{1,0:T(2,128)} %get-tuple-element.66.refs_1_, s32[768,1]{1,0:T(8,128)} %fusion.1.refs_2_, bf16[768,64]{1,0:T(8,128)(2,1)} %fusion.7.refs_3_, bf16[768,256]{1,0:T(8,128)(2,1)} %copy-done.6, ...), custom_call_target="tpu_custom_call" | custom-call | flops 603979 | bytes 1090 | tf_op jit(solution)/shard_map/pallas_call | solution.py:71
  142.4 0.9 constant_dynamic-slice_fusion
  143.9 23.3 %collective-permute-done.21 = bf16[384,256]{1,0:T(8,128)(2,1)S(1)} collective-permute-done((bf16[384,256]{1,0:T(8,128)(2,1)S(1)}, bf16[384,256]{1,0:T(8,128)(2,1)S(1)}, u32[]{:S(2)}, u32[]{:S(2)}) %collective-permute-start.21) | collective-permute-done | bytes 196640 | tf_op jit(solution)/shard_map/ppermute | solution.py:25
  167.2 1.0 add_convert_fusion.5
  168.5 1.0 pad_maximum_fusion.1
  169.5 5.0 %all-to-all-start.2 = ((bf16[8,48,1280]{2,1,0:T(8,128)(2,1)}), bf16[8,48,1280]{2,1,0:T(8,128)(2,1)S(1)}, u32[]{:S(2)}, u32[]{:S(2)}) async-start(bf16[8,48,1280]{2,1,0:T(8,128)(2,1)} %bitcast.15), calls=%async_computation.2 | async-start | bytes 1966080 | tf_op jit(solution)/shard_map/all_to_all | solution.py:20
  177.1 0.9 copy.30
  178.2 1.6 collective-permute-start.15
  179.7 0.8 fusion.48
  180.5 2.9 %shard_map.116 = bf16[768,256]{1,0:T(8,128)(2,1)} custom-call(bf16[768,64]{1,0:T(8,128)(2,1)} %get-tuple-element.65.refs_0_, s32[768,1]{1,0:T(8,128)} %bitcast.38, s32[1,768]{1,0:T(1,128)} %fusion.36.refs_3_.refs_4_.refs_2_, bf16[64,768]{1,0:T(8,128)(2,1)} %fusion.8.refs_8_.refs_3_.refs_5_, bf16[768,256]{1,0:T(8,128)(2,1)} %pad_maximum_fusion.5.refs_2_.refs_4_.refs_6_), custom_call_target="tpu_custom_call" | custom-call | flops 301989 | bytes 595 | tf_op jit(solution)/shard_map/pallas_call | solution.py:71
  183.9 0.9 broadcast_in_dim.36.refs_3_
  185.5 0.7 slice_add_fusion.refs_2_
  186.2 14.4 %shard_map.115 = bf16[768,2048]{1,0:T(8,128)(2,1)} custom-call(bf16[768,1024]{1,0:T(8,128)(2,1)} %copy-done.2, bf16[2048,1024]{1,0:T(8,128)(2,1)} %refs_1_.1, bf16[768,64]{1,0:T(8,128)(2,1)} %slice_add_fusion.refs_2_, s32[768,1]{1,0:T(8,128)} %broadcast_in_dim.36.refs_3_, s32[1,768]{1,0:T(1,128)} %fusion.36.refs_3_.refs_4_.refs_2_, s32[1,192]{1,0:T(1,128)} %bitcast.42, ...), custom_call_target="tpu_custom_call" | custom-call | flops 8053063 | bytes 12362 | tf_op jit(solution)/shard_map/pallas_call | solution.py:71
  200.6 0.7 copy-done.17
  201.4 3.1 %shard_map.117 = bf16[768,256]{1,0:T(8,128)(2,1)} custom-call(bf16[768,256]{1,0:T(8,128)(2,1)} %add_convert_fusion.2.refs_0_, bf16[768,256]{1,0:T(8,128)(2,1)} %copy-done.17, bf16[768,64]{1,0:T(8,128)(2,1)} %get-tuple-element.64.refs_2_, s32[768,1]{1,0:T(8,128)} %broadcast_in_dim.36.refs_3_, s32[1,768]{1,0:T(1,128)} %fusion.36.refs_3_.refs_4_.refs_2_, ...), custom_call_target="tpu_custom_call" | custom-call | flops 301989 | bytes 1382 | tf_op jit(solution)/shard_map/pallas_call | solution.py:71
  204.5 1.0 copy-done.9
  205.5 2.5 %shard_map.120 = (bf16[48,8192]{1,0:T(8,128)(2,1)}, bf16[48,1024]{1,0:T(8,128)(2,1)}) custom-call(bf16[8,48,1024]{2,1,0:T(8,128)(2,1)} %copy-done.11, bf16[8,48,1280]{2,1,0:T(8,128)(2,1)} %copy-done.9), custom_call_target="tpu_custom_call" | custom-call | flops 1 | bytes 1769 | tf_op jit(solution)/shard_map/pallas_call | solution.py:71
  (101 shorter events, 10.1 us)
Async XLA Ops:
  2.5 26.0 %collective-permute-start = (bf16[192,256]{1,0:T(8,128)(2,1)}, bf16[192,256]{1,0:T(8,128)(2,1)}, u32[]{:S(2)}, u32[]{:S(2)}) collective-permute-start(bf16[192,256]{1,0:T(8,128)(2,1)} %get-tuple-element.63), channel_id=1, source_target_pairs={{0,1},{1,0},{2,3},{3,2},{4,5},{5,4},{6,7},{7,6},{8,9},{9,8},{10,11... | collective-permute-start | bytes 294920 | tf_op jit(solution)/shard_map/ppermute | solution.py:29
  2.9 25.5 %collective-permute-start.1 = (bf16[192,256]{1,0:T(8,128)(2,1)}, bf16[192,256]{1,0:T(8,128)(2,1)}, u32[]{:S(2)}, u32[]{:S(2)}) collective-permute-start(bf16[192,256]{1,0:T(8,128)(2,1)} %get-tuple-element.62), channel_id=1, source_target_pairs={{0,2},{1,3},{2,0},{3,1},{4,6},{5,7},{6,4},{7,5},{8,10},{9,11},{10,... | collective-permute-start | bytes 294920 | tf_op jit(solution)/shard_map/ppermute | solution.py:29
  5.4 23.0 %collective-permute-start.2 = (bf16[192,256]{1,0:T(8,128)(2,1)}, bf16[192,256]{1,0:T(8,128)(2,1)}, u32[]{:S(2)}, u32[]{:S(2)}) collective-permute-start(bf16[192,256]{1,0:T(8,128)(2,1)} %get-tuple-element.61), channel_id=1, source_target_pairs={{0,3},{1,2},{2,1},{3,0},{4,7},{5,6},{6,5},{7,4},{8,11},{9,10},{10,... | collective-permute-start | bytes 294920 | tf_op jit(solution)/shard_map/ppermute | solution.py:29
  8.3 4.4 %copy-start.19 = (s32[768]{0:T(1024)S(1)}, s32[768]{0:T(1024)}, u32[]{:S(2)}) copy-start(s32[768]{0:T(1024)} %param.13) | copy-start | bytes 9220
  8.3 4.5 %copy-start.20 = (s32[24]{0:T(128)S(1)}, s32[24]{0:T(128)}, u32[]{:S(2)}) copy-start(s32[24]{0:T(128)} %param.15) | copy-start | bytes 292
  8.3 4.5 %copy-start.21 = (s32[1,24]{1,0:T(1,128)S(1)}, s32[1,24]{1,0:T(1,128)}, u32[]{:S(2)}) copy-start(s32[1,24]{1,0:T(1,128)} %param.14) | copy-start | bytes 292
  8.3 25.5 %all-to-all-start = ((bf16[8,48,2048]{2,1,0:T(8,128)(2,1)}), bf16[8,48,2048]{2,1,0:T(8,128)(2,1)}, u32[]{:S(2)}, u32[]{:S(2)}) async-start(bf16[8,48,2048]{2,1,0:T(8,128)(2,1)} %bitcast.8), calls=%async_computation | async-start | bytes 3145728 | tf_op jit(solution)/shard_map/all_to_all | solution.py:20
  12.9 5.9 %copy-start = (bf16[768,2048]{1,0:T(8,128)(2,1)S(1)}, bf16[768,2048]{1,0:T(8,128)(2,1)}, u32[]{:S(2)}) copy-start(bf16[768,2048]{1,0:T(8,128)(2,1)} %refs_4_.3) | copy-start | bytes 9437188
  14.8 1.2 copy-start.2
  16.0 5.0 %copy-start.6 = (bf16[768,256]{1,0:T(8,128)(2,1)}, bf16[768,256]{1,0:T(8,128)(2,1)S(1)}, u32[]{:S(2)}) copy-start(bf16[768,256]{1,0:T(8,128)(2,1)S(1)} %constant_dynamic-slice_fusion.8.refs_0_.refs_4_) | copy-start | bytes 1179652
  16.9 25.0 %collective-permute-start.7 = (bf16[784,256]{1,0:T(8,128)(2,1)}, bf16[784,256]{1,0:T(8,128)(2,1)}, u32[]{:S(2)}, u32[]{:S(2)}) collective-permute-start(bf16[784,256]{1,0:T(8,128)(2,1)} %pad_maximum_fusion.4), channel_id=1, source_target_pairs={{0,4},{4,0},{1,5},{5,1},{2,6},{6,2},{3,7},{7,3},{8,12},{12,8},{9,1... | collective-permute-start | bytes 1204232 | tf_op jit(solution)/shard_map/ppermute | solution.py:25
  21.0 7.4 %copy-start.18 = (bf16[192,256]{1,0:T(8,128)(2,1)S(1)}, bf16[192,256]{1,0:T(8,128)(2,1)}, u32[]{:S(2)}) copy-start(bf16[192,256]{1,0:T(8,128)(2,1)} %get-tuple-element.60) | copy-start | bytes 294916
  21.0 9.2 %copy-start.8 = (bf16[3,64,8192]{2,1,0:T(8,128)(2,1)S(1)}, bf16[3,64,8192]{2,1,0:T(8,128)(2,1)}, u32[]{:S(2)}) copy-start(bf16[3,64,8192]{2,1,0:T(8,128)(2,1)} %param.10) | copy-start | bytes 9437188
  31.7 16.1 %collective-permute-start.4 = (bf16[192,2048]{1,0:T(8,128)(2,1)}, bf16[192,2048]{1,0:T(8,128)(2,1)}, u32[]{:S(2)}, u32[]{:S(2)}) collective-permute-start(bf16[192,2048]{1,0:T(8,128)(2,1)} %get-tuple-element.53), channel_id=1, source_target_pairs={{0,1},{1,0},{2,3},{3,2},{4,5},{5,4},{6,7},{7,6},{8,9},{9,8},{10,11... | collective-permute-start | bytes 2359304 | tf_op jit(solution)/shard_map/ppermute | solution.py:29
  31.7 20.7 %collective-permute-start.5 = (bf16[192,2048]{1,0:T(8,128)(2,1)}, bf16[192,2048]{1,0:T(8,128)(2,1)}, u32[]{:S(2)}, u32[]{:S(2)}) collective-permute-start(bf16[192,2048]{1,0:T(8,128)(2,1)} %get-tuple-element.52), channel_id=1, source_target_pairs={{0,2},{1,3},{2,0},{3,1},{4,6},{5,7},{6,4},{7,5},{8,10},{9,11},{10,... | collective-permute-start | bytes 2359304 | tf_op jit(solution)/shard_map/ppermute | solution.py:29
  33.2 35.3 %collective-permute-start.6 = (bf16[192,2048]{1,0:T(8,128)(2,1)}, bf16[192,2048]{1,0:T(8,128)(2,1)}, u32[]{:S(2)}, u32[]{:S(2)}) collective-permute-start(bf16[192,2048]{1,0:T(8,128)(2,1)} %get-tuple-element.51), channel_id=1, source_target_pairs={{0,3},{1,2},{2,1},{3,0},{4,7},{5,6},{6,5},{7,4},{8,11},{9,10},{10,... | collective-permute-start | bytes 2359304 | tf_op jit(solution)/shard_map/ppermute | solution.py:29
  33.5 54.4 %collective-permute-start.11 = (bf16[768,1024]{1,0:T(8,128)(2,1)}, bf16[768,1024]{1,0:T(8,128)(2,1)S(1)}, u32[]{:S(2)}, u32[]{:S(2)}) collective-permute-start(bf16[768,1024]{1,0:T(8,128)(2,1)} %get-tuple-element.29), channel_id=1, source_target_pairs={{0,4},{4,0},{1,5},{5,1},{2,6},{6,2},{3,7},{7,3},{8,12},{12,8},{9,1... | collective-permute-start | bytes 4718600 | tf_op jit(solution)/shard_map/ppermute | solution.py:25
  35.0 36.4 %copy-start.10 = (bf16[4,48,2048]{2,1,0:T(8,128)(2,1)}, bf16[4,48,2048]{2,1,0:T(8,128)(2,1)S(1)}, u32[]{:S(2)}) copy-start(bf16[4,48,2048]{2,1,0:T(8,128)(2,1)S(1)} %constant_dynamic-slice_fusion.6) | copy-start | bytes 2359300
  41.9 29.5 %collective-permute-start.8 = (bf16[192,2048]{1,0:T(8,128)(2,1)S(1)}, bf16[192,2048]{1,0:T(8,128)(2,1)}, u32[]{:S(2)}, u32[]{:S(2)}) collective-permute-start(bf16[192,2048]{1,0:T(8,128)(2,1)S(1)} %bitcast.35), channel_id=1, source_target_pairs={{0,8},{8,0},{1,9},{9,1},{2,10},{10,2},{3,11},{11,3},{4,12},{12,4},... | collective-permute-start | bytes 2359304 | tf_op jit(solution)/shard_map/ppermute | solution.py:25
  71.5 3.5 %copy-start.14 = (bf16[768,1024]{1,0:T(8,128)(2,1)S(1)}, bf16[768,1024]{1,0:T(8,128)(2,1)}, u32[]{:S(2)}) copy-start(bf16[768,1024]{1,0:T(8,128)(2,1)} %convolution_convert_fusion) | copy-start | bytes 4718596
  74.9 1.7 copy-start.13
  75.0 3.2 %copy-start.15 = (bf16[768,128]{1,0:T(8,128)(2,1)S(1)}, bf16[768,128]{1,0:T(8,128)(2,1)}, u32[]{:S(2)}) copy-start(bf16[768,128]{1,0:T(8,128)(2,1)} %shard_map.111) | copy-start | bytes 589828
  76.0 5.3 %collective-permute-start.12 = (bf16[768,512]{1,0:T(8,128)(2,1)}, bf16[768,512]{1,0:T(8,128)(2,1)}, u32[]{:S(2)}, u32[]{:S(2)}) collective-permute-start(bf16[768,512]{1,0:T(8,128)(2,1)} %pad_maximum_fusion.3), channel_id=1, source_target_pairs={{0,1},{1,0},{2,3},{3,2},{4,5},{5,4},{6,7},{7,6},{8,9},{9,8},{10,11... | collective-permute-start | bytes 2359304 | tf_op jit(solution)/shard_map/ppermute | solution.py:29
  76.6 36.8 %collective-permute-start.3 = (bf16[768,1024]{1,0:T(8,128)(2,1)S(1)}, bf16[768,1024]{1,0:T(8,128)(2,1)}, u32[]{:S(2)}, u32[]{:S(2)}) collective-permute-start(bf16[768,1024]{1,0:T(8,128)(2,1)S(1)} %copy-done.13), channel_id=1, source_target_pairs={{0,4},{4,0},{1,5},{5,1},{2,6},{6,2},{3,7},{7,3},{8,12},{12,8},{9,1... | collective-permute-start | bytes 4718600 | tf_op jit(solution)/shard_map/ppermute | solution.py:25
  78.1 1.4 collective-permute-start.9
  79.6 7.6 %collective-permute-start.10 = (bf16[768,128]{1,0:T(8,128)(2,1)S(1)}, bf16[768,128]{1,0:T(8,128)(2,1)S(1)}, u32[]{:S(2)}, u32[]{:S(2)}) collective-permute-start(bf16[768,128]{1,0:T(8,128)(2,1)S(1)} %add_convert_fusion.9), channel_id=1, source_target_pairs={{0,2},{1,3},{2,0},{3,1},{4,6},{5,7},{6,4},{7,5},{8,10},{9,11},{10,... | collective-permute-start | bytes 589832 | tf_op jit(solution)/shard_map/ppermute | solution.py:29
  83.3 21.1 %collective-permute-start.13 = (bf16[768,256]{1,0:T(8,128)(2,1)}, bf16[768,256]{1,0:T(8,128)(2,1)S(1)}, u32[]{:S(2)}, u32[]{:S(2)}) collective-permute-start(bf16[768,256]{1,0:T(8,128)(2,1)} %add_convert_fusion.3), channel_id=1, source_target_pairs={{0,2},{1,3},{2,0},{3,1},{4,6},{5,7},{6,4},{7,5},{8,10},{9,11},{10,... | collective-permute-start | bytes 1179656 | tf_op jit(solution)/shard_map/ppermute | solution.py:29
  87.9 1.2 copy-start.3
  96.5 26.5 %collective-permute-start.19 = (bf16[384,1024]{1,0:T(8,128)(2,1)S(1)}, bf16[384,1024]{1,0:T(8,128)(2,1)S(1)}, u32[]{:S(2)}, u32[]{:S(2)}) collective-permute-start(bf16[384,1024]{1,0:T(8,128)(2,1)S(1)} %constant_dynamic-slice_fusion.2), channel_id=1, source_target_pairs={{0,8},{8,0},{1,9},{9,1},{2,10},{10,2},{3,11},{11,3},{4,12},{12,4},... | collective-permute-start | bytes 2359304 | tf_op jit(solution)/shard_map/ppermute | solution.py:25
  106.4 13.1 %copy-start.1 = (bf16[768,2048]{1,0:T(8,128)(2,1)S(1)}, bf16[768,2048]{1,0:T(8,128)(2,1)}, u32[]{:S(2)}) copy-start(bf16[768,2048]{1,0:T(8,128)(2,1)} %pad_maximum_fusion.refs_2_.refs_12_) | copy-start | bytes 9437188
  119.5 1.7 collective-permute-start.14
  119.5 1.6 copy-start.16
  119.5 3.5 %copy-start.4 = (bf16[768,1024]{1,0:T(8,128)(2,1)S(1)}, bf16[768,1024]{1,0:T(8,128)(2,1)}, u32[]{:S(2)}) copy-start(bf16[768,1024]{1,0:T(8,128)(2,1)} %shard_map.112) | copy-start | bytes 4718596
  120.9 48.6 %collective-permute-start.16 = (bf16[384,2048]{1,0:T(8,128)(2,1)}, bf16[384,2048]{1,0:T(8,128)(2,1)}, u32[]{:S(2)}, u32[]{:S(2)}) collective-permute-start(bf16[384,2048]{1,0:T(8,128)(2,1)} %bitcast.13), channel_id=1, source_target_pairs={{0,4},{4,0},{1,5},{5,1},{2,6},{6,2},{3,7},{7,3},{8,12},{12,8},{9,1... | collective-permute-start | bytes 4718600 | tf_op jit(solution)/shard_map/ppermute | solution.py:25
  121.2 16.1 %collective-permute-start.17 = (bf16[768,128]{1,0:T(8,128)(2,1)S(1)}, bf16[768,128]{1,0:T(8,128)(2,1)S(1)}, u32[]{:S(2)}, u32[]{:S(2)}) collective-permute-start(bf16[768,128]{1,0:T(8,128)(2,1)S(1)} %add_convert_fusion.7), channel_id=1, source_target_pairs={{0,2},{1,3},{2,0},{3,1},{4,6},{5,7},{6,4},{7,5},{8,10},{9,11},{10,... | collective-permute-start | bytes 589832 | tf_op jit(solution)/shard_map/ppermute | solution.py:29
  124.2 45.3 %all-to-all-start.1 = ((bf16[8,48,1024]{2,1,0:T(8,128)(2,1)}), bf16[8,48,1024]{2,1,0:T(8,128)(2,1)S(1)}, u32[]{:S(2)}, u32[]{:S(2)}) async-start(bf16[8,48,1024]{2,1,0:T(8,128)(2,1)} %bitcast.14), calls=%async_computation.1 | async-start | bytes 1572864 | tf_op jit(solution)/shard_map/all_to_all | solution.py:20
  135.6 32.5 %collective-permute-start.20 = (bf16[384,1024]{1,0:T(8,128)(2,1)S(1)}, bf16[384,1024]{1,0:T(8,128)(2,1)S(1)}, u32[]{:S(2)}, u32[]{:S(2)}) collective-permute-start(bf16[384,1024]{1,0:T(8,128)(2,1)S(1)} %constant_dynamic-slice_fusion.1), channel_id=1, source_target_pairs={{0,8},{8,0},{1,9},{9,1},{2,10},{10,2},{3,11},{11,3},{4,12},{12,4},... | collective-permute-start | bytes 2359304 | tf_op jit(solution)/shard_map/ppermute | solution.py:25
  138.0 30.1 %copy-start.5 = (bf16[768,1024]{1,0:T(8,128)(2,1)S(1)}, bf16[768,1024]{1,0:T(8,128)(2,1)}, u32[]{:S(2)}) copy-start(bf16[768,1024]{1,0:T(8,128)(2,1)} %shard_map.118) | copy-start | bytes 4718596
  143.4 23.8 %collective-permute-start.21 = (bf16[384,256]{1,0:T(8,128)(2,1)S(1)}, bf16[384,256]{1,0:T(8,128)(2,1)S(1)}, u32[]{:S(2)}, u32[]{:S(2)}) collective-permute-start(bf16[384,256]{1,0:T(8,128)(2,1)S(1)} %constant_dynamic-slice_fusion), channel_id=1, source_target_pairs={{0,8},{8,0},{1,9},{9,1},{2,10},{10,2},{3,11},{11,3},{4,12},{12,4},... | collective-permute-start | bytes 589832 | tf_op jit(solution)/shard_map/ppermute | solution.py:25
  169.5 8.6 %copy-start.7 = (bf16[768,128]{1,0:T(8,128)(2,1)S(1)}, bf16[768,128]{1,0:T(8,128)(2,1)}, u32[]{:S(2)}) copy-start(bf16[768,128]{1,0:T(8,128)(2,1)} %add_convert_fusion.8.refs_0_) | copy-start | bytes 589828
  169.5 10.2 %copy-start.12 = (bf16[768,128]{1,0:T(8,128)(2,1)S(1)}, bf16[768,128]{1,0:T(8,128)(2,1)}, u32[]{:S(2)}) copy-start(bf16[768,128]{1,0:T(8,128)(2,1)} %add_convert_fusion.6.refs_0_) | copy-start | bytes 589828
  169.5 11.0 %copy-start.11 = (bf16[8,48,1024]{2,1,0:T(8,128)(2,1)}, bf16[8,48,1024]{2,1,0:T(8,128)(2,1)S(1)}, u32[]{:S(2)}) copy-start(bf16[8,48,1024]{2,1,0:T(8,128)(2,1)S(1)} %all-to-all-done.1.refs_0_) | copy-start | bytes 2359300
  169.5 35.0 %all-to-all-start.2 = ((bf16[8,48,1280]{2,1,0:T(8,128)(2,1)}), bf16[8,48,1280]{2,1,0:T(8,128)(2,1)S(1)}, u32[]{:S(2)}, u32[]{:S(2)}) async-start(bf16[8,48,1280]{2,1,0:T(8,128)(2,1)} %bitcast.15), calls=%async_computation.2 | async-start | bytes 1966080 | tf_op jit(solution)/shard_map/all_to_all | solution.py:20
  178.2 7.4 %collective-permute-start.15 = (bf16[768,64]{1,0:T(8,128)(2,1)S(1)}, bf16[768,64]{1,0:T(8,128)(2,1)S(1)}, u32[]{:S(2)}, u32[]{:S(2)}) collective-permute-start(bf16[768,64]{1,0:T(8,128)(2,1)S(1)} %slice.91), channel_id=1, source_target_pairs={{0,4},{4,0},{1,5},{5,1},{2,6},{6,2},{3,7},{7,3},{8,12},{12,8},{9,1... | collective-permute-start | bytes 294920 | tf_op jit(solution)/shard_map/ppermute | solution.py:25
  183.4 17.2 %collective-permute-start.18 = (bf16[768,256]{1,0:T(8,128)(2,1)}, bf16[768,256]{1,0:T(8,128)(2,1)S(1)}, u32[]{:S(2)}, u32[]{:S(2)}) collective-permute-start(bf16[768,256]{1,0:T(8,128)(2,1)} %shard_map.116), channel_id=1, source_target_pairs={{0,4},{4,0},{1,5},{5,1},{2,6},{6,2},{3,7},{7,3},{8,12},{12,8},{9,1... | collective-permute-start | bytes 1179656 | tf_op jit(solution)/shard_map/ppermute | solution.py:25
  200.6 0.7 copy-start.17
  204.5 1.0 copy-start.9

commit v4 on v3

--- a/solution.py
+++ b/solution.py
@@ -9,7 +9,7 @@
 from jax.sharding import PartitionSpec as P
 
 ADAPTER_SCALE = 0.5
-PIECES = (2, 2)
+PIECES = (2, 4, 4)
 SPLIT = 128
 HINT = 1000
 LANES = 128
@@ -47,7 +47,7 @@
     return total
 
 
-def scatter_columns(term):
+def scatter_columns(term, gate=None):
     size = lax.axis_size("tensor")
     share = lax.axis_index("tensor")
     width = term.shape[1] // size
@@ -56,6 +56,8 @@
     ]
     for bit in bits_below(size):
         kept = [i for i in range(size) if i % (2 * bit) == 0]
+        if 2 * bit == size:
+            blocks = after(blocks, gate)
         got = swap(jnp.concatenate([blocks[i ^ bit] for i in kept], axis=1), "tensor", bit)
         for n, i in enumerate(kept):
             blocks[i] = add(blocks[i], got[:, n * width : (n + 1) * width])
@@ -172,6 +174,84 @@
     )
 
 
+def piece_body(count, rank, has_before, *refs):
+    compact, row_slots, part_slots, select, weight, column_slots, slots = refs[:7]
+    lines = refs[7 : 7 + count]
+    out_weight, out_low, spread, *fulls = refs[7 + count + has_before :]
+    step = pl.program_id(0)
+
+    @pl.when(step == 0)
+    def _():
+        for n in range(count):
+            wide = dot(select[...], compact[:, n * rank : (n + 1) * rank], 1, 1)
+            mine = part_slots[...] == row_slots[n : n + 1, :]
+            spread[n] = jnp.where(mine, wide, 0.0).astype(jnp.bfloat16)
+            if fulls:
+                fulls[n][...] = dot(lines[n][...], weight[...], 1, 1)
+
+    if fulls:
+
+        @pl.when(step > 0)
+        def _():
+            for n in range(count):
+                fulls[n][...] += dot(lines[n][...], weight[...], 1, 1)
+
+    @pl.when(step == pl.num_programs(0) - 1)
+    def _():
+        block = max(rank, LANES)
+        results = []
+        for n in range(count):
+            full = fulls[n][...] if fulls else dot(lines[n][...], weight[...], 1, 1)
+            full = jnp.where(slots[:, n : n + 1] == column_slots[...], full, 0.0)
+            total = full[:, :block]
+            for i in range(block, full.shape[1], block):
+                total += full[:, i : i + block]
+            results.append(sum(total[:, i : i + rank] for i in range(0, block, rank)))
+        result = jnp.concatenate(results, axis=1)
+        if has_before:
+            result += refs[7 + count][...]
+        out_low[...] = result.astype(out_low.dtype)
+
+    total = dot(spread[0], lines[0][...], 1, 0)
+    for n in range(1, count):
+        total += dot(spread[n], lines[n][...], 1, 0)
+    out_weight[...] = total.astype(out_weight.dtype)
+
+
+def piece_product(
+    compact, row_slots, part_slots, select, weight, column_slots, slots, lines, block, before, dtype
+):
+    count = len(lines)
+    rows = row_slots.shape[1]
+    columns, rank = select.shape
+    offset, width = block
+    tile = min(width, 512)
+    per = width // tile
+    here = lambda i: (0, offset * per + i)
+    small = [compact, row_slots, part_slots, select, column_slots, slots]
+    specs = [whole(x) for x in small[:4]] + [pl.BlockSpec((columns, tile), here)]
+    specs += [whole(x) for x in small[4:]]
+    for line in lines:
+        skip = 0 if line.shape[1] == width else offset * per
+        specs.append(pl.BlockSpec((rows, tile), functools.partial(lambda s, i: (0, s + i), skip)))
+    operands = small[:4] + [weight] + small[4:] + list(lines)
+    if before is not None:
+        specs.append(whole(before))
+        operands.append(before)
+    low = jax.ShapeDtypeStruct((rows, count * rank), dtype)
+    return call(
+        functools.partial(piece_body, count, rank, before is not None),
+        (per,),
+        specs,
+        [pl.BlockSpec((columns, tile), lambda i: (0, i)), whole(low)],
+        [jax.ShapeDtypeStruct((columns, width), jnp.bfloat16), low],
+        operands,
+        4 * count * rows * columns * width,
+        [pltpu.VMEM((count, columns, rows), jnp.bfloat16)]
+        + [pltpu.VMEM((rows, columns), jnp.float32)] * (count if per > 1 else 0),
+    )
+
+
 def input_body(count, *refs):
     scaled, frozen, compact, slots = refs[:4]
     columns, selects, downs = (refs[4 + i * count : 4 + (i + 1) * count] for i in range(3))
@@ -181,7 +261,7 @@
     def _():
         for n in range(count):
             wide = dot(compact[...], selects[n][...], 1, 0)
-            mine = slots[...] == columns[n][...]
+            mine = slots[:, :1] == columns[n][...]
             spreads[n][...] = jnp.where(mine, wide, 0.0).astype(jnp.bfloat16)
 
     total = dot(scaled[...], frozen[...], 1, 1)
@@ -209,18 +289,19 @@
     )
 
 
-def output_body(count, *refs):
+def output_body(count, which, rank, *refs):
     compact, slots, column_slots, select, ups = refs[count : count + 5]
     out = refs[-1]
-    wide = dot(compact[...], select[...], 1, 0)
-    spread = jnp.where(slots[...] == column_slots[...], wide, 0.0).astype(jnp.bfloat16)
+    wide = dot(compact[:, which * rank : (which + 1) * rank], select[...], 1, 0)
+    mine = slots[:, which : which + 1] == column_slots[...]
+    spread = jnp.where(mine, wide, 0.0).astype(jnp.bfloat16)
     result = ADAPTER_SCALE * dot(spread, ups[...], 1, 0)
     for addend in refs[:count]:
         result += addend[...].astype(jnp.float32)
     out[...] = result.astype(out.dtype)
 
 
-def output_product(addends, compact, slots, column_slots, select, ups):
+def output_product(addends, which, compact, slots, column_slots, select, ups):
     rows, width = compact.shape[0], ups.shape[1]
     tile = rows // 2
     line = lambda i: (i, 0)
@@ -229,7 +310,7 @@
     operands += [column_slots, select, ups]
     specs += [whole(x) for x in operands[-3:]]
     return call(
-        functools.partial(output_body, len(addends)),
+        functools.partial(output_body, len(addends), which, select.shape[0]),
         (rows // tile,),
         specs,
         pl.BlockSpec((tile, width), line),
@@ -239,14 +320,16 @@
     )
 
 
-def total_body(planes, shares, width, last_width, value_width, *refs):
+def total_body(shares, width, last_width, value_width, *refs):
     out_down, out_up = refs[-2:]
     position = 0
     for ref in refs[:-2]:
         last = ref is refs[-3]
         columns = last_width if last else ref.shape[2]
         for share in range(shares):
-            total = sum(ref[q * shares + share].astype(jnp.float32) for q in range(planes))
+            total = sum(
+                ref[source].astype(jnp.float32) for source in range(share, ref.shape[0], shares)
+            )
             start = share * width + position
             out_down[:, start : start + columns] = total[:, :columns].astype(jnp.bfloat16)
             if last:
@@ -255,14 +338,14 @@
         position += columns
 
 
-def total_product(arrived, planes, shares, width, last_width, value_width):
+def total_product(arrived, shares, width, last_width, value_width):
     lot = arrived[0].shape[1]
     shapes = [
         jax.ShapeDtypeStruct((lot, shares * columns), jnp.bfloat16)
         for columns in (width, value_width)
     ]
     return call(
-        functools.partial(total_body, planes, shares, width, last_width, value_width),
+        functools.partial(total_body, shares, width, last_width, value_width),
         (1,),
         [whole(x) for x in arrived],
         [whole(x) for x in shapes],
@@ -317,6 +400,7 @@
         ).reshape(own * piece, width)
         quarters.append([block] + [shift(block, "near", i) for i in range(1, near)])
     shared = [block for blocks in quarters for block in blocks]
+    spread_far = [[shift(q[0], "far", i) for i in range(1, far)] for q in quarters]
 
     pairs = jnp.arange(adapter_owner_table.shape[0], dtype=jnp.int32)
     matches = language_pair_index[:, None] == pairs[None, :]
@@ -354,7 +438,7 @@
     own_ups = over_shares(adapter_up_weight.reshape(stored * rank, values))
     down_flat = after(adapter_down_weight.reshape(stored * rank, shares * width), own_ups)
     own_down = over_shares(down_flat)
-    gated_ups = after(own_ups, own_down, *shared)
+    gated_ups = after(own_ups, own_down, *shared, *[b for blocks in spread_far for b in blocks])
 
     pieces, position = [], 0
     for part in PIECES:
@@ -382,6 +466,29 @@
     part_slots = (side * own + part_local)[:, None]
     part_select = choose(part_ranks, rank).T
 
+    columns, selects = [sent_slots[None, :]], [sent_select]
+    quarter_column = column[: own * piece]
+    adapter = quarter_column // piece
+    per = (far - 1) * (near - 1)
+    for j in steps:
+        away = (side - j) % sides
+        mine = plane // near
+        stored_order = away * own + adapter
+        sent_order = (away * shares + (share ^ (adapter // stored))) * stored + adapter % stored
+        blocks = [(stored_order, mine * near + (close - i) % near) for i in range(near)]
+        blocks += [(stored_order, (mine - i) % far * near + close) for i in range(1, far)]
+        blocks += [
+            (sent_order, (mine + i) % far * near + (close + k) % near)
+            for i in range(1, far)
+            for k in range(1, near)
+        ]
+        for block_slots, from_plane in blocks:
+            columns.append(block_slots[None, :])
+            selects.append(choose(from_plane * piece + quarter_column % piece, rank))
+    tables = (part_slots, part_select, sent_slots, sent_select, columns, selects, slot_columns)
+    gated_ups, tables = lax.optimization_barrier((gated_ups, tables))
+    part_slots, part_select, sent_slots, sent_select, columns, selects, slot_columns = tables
+
     back_part = fold_product(
         scaled_of,
         gated_ups,
@@ -395,78 +502,74 @@
     )
     back_part, base_term = lax.optimization_barrier((back_part, base_term))
     back_all = tensor_sum(back_part)
-    back = back_all[:, :rank]
-    for j in steps:
-        back = back + shift(back_all[:, j * rank : (j + 1) * rank], "adapter", -j)
-
-
-    base_share = scatter_columns(base_term)
+    replies = [shift(back_all[:, j * rank : (j + 1) * rank], "adapter", -j) for j in steps]
+
+
     back_gate = back_all
-    low_part = None
+    groups = [slice(g, min(g + 2, sides)) for g in range(0, sides, 2)]
+    lows = [None] * len(groups)
     parts_down = []
     for n, (block, lines) in enumerate(pieces):
         last = n == len(pieces) - 1
-
-        def gradient():
-            return weight_product(
-                back_gate, row_slots, part_slots, part_select, lines, block, 1.0
+        parts = []
+        for g, group in enumerate(groups):
+            part, lows[g] = piece_product(
+                back_gate[:, group.start * rank : group.stop * rank],
+                row_slots[group],
+                part_slots,
+                part_select,
+                own_down,
+                sent_slots[None, :],
+                slot_columns[:, group],
+                lines[group],
+                block,
+                lows[g],
+                jnp.bfloat16 if last else jnp.float32,
             )
-
-        if not last:
-            parts_down.append(gradient())
-            own_down = after(own_down, parts_down[-1])
-        low_part = fold_product(
-            lines,
-            own_down,
-            block,
-            sent_slots[None, :],
-            slot_columns,
-            rank,
-            1.0,
-            low_part,
-            jnp.bfloat16 if last else jnp.float32,
-        )
+            parts.append(part)
+        parts_down.append(functools.reduce(add, parts))
         if last:
-            low_part = tensor_sum(low_part, bits_below(shares)[:1])
-        low_part, back_gate, base_share = lax.optimization_barrier(
-            (low_part, back_gate, base_share)
-        )
-        if last:
-            parts_down.append(gradient())
-    bundle = rank // far
+            low_part = tensor_sum(jnp.concatenate(lows, axis=1), bits_below(shares)[:1])
+        lows, back_gate = lax.optimization_barrier((lows, back_gate))
     by_rank = own_down.reshape(own, rank, width)
     rests = []
     for j in steps:
         for i in range(1, far):
-            start = (plane // near + i) % far * bundle
-            rest = lax.dynamic_slice_in_dim(by_rank, start, bundle, 1)
-            rests.append(shift(rest.reshape(own * bundle, width), "adapter", j))
-
-    def fold(part):
+            for k in range(1, near):
+                start = ((plane // near + i) % far * near + (close + k) % near) * piece
+                rest = lax.dynamic_slice_in_dim(by_rank, start, piece, 1)
+                rests.append(shift(rest.reshape(own * piece, width), "adapter", j))
+
+    def fold_start(part):
         half = part.shape[0] // near
-        kept = lax.dynamic_slice_in_dim(part, close * half, half, 0)
-        for j in range(1, near):
-            away = lax.dynamic_slice_in_dim(part, ((close + j) % near) * half, half, 0)
-            kept = add(kept, shift(away, "near", j))
-        return kept
-
-    def send(part):
-        return exchange(part.reshape(far * shares, lot, part.shape[1]), ("far", "tensor"))
-
-    parts_down = [fold(part) for part in parts_down]
-    first = send(after(parts_down[0], *pieces[1][1][1:]))
+        pieces_of = [
+            lax.dynamic_slice_in_dim(part, ((close + j) % near) * half, half, 0)
+            for j in range(near)
+        ]
+        return [pieces_of[0]] + [shift(pieces_of[j], "near", j) for j in range(1, near)]
+
+    def fold_end(parts):
+        return functools.reduce(add, parts)
+
+    def send(part, axes):
+        size = lax.axis_size(axes)
+        return exchange(part.reshape(size, lot, part.shape[1]), axes)
+
+    first = send(parts_down[0], ("near", "far", "tensor"))
+    started = [fold_start(part) for part in parts_down[1:]]
     low_all = tensor_sum(low_part, bits_below(shares)[1:])
+    base_share = scatter_columns(base_term, low_all)
     up_part = weight_product(
         low_all, row_slots, part_slots, part_select, scaled_of, (0, value_width), ADAPTER_SCALE
     )
-    last_width = parts_down[-1].shape[1]
-    parts_down[-1] = jnp.concatenate([parts_down[-1], fold(up_part)], axis=1)
-    parts_down[-1] = after(parts_down[-1], *rests)
-
-    arrived = [first]
-    for part in parts_down[1:]:
-        arrived.append(send(after(part, arrived[-1])))
-    grad_down, grad_up = total_product(arrived, far, shares, width, last_width, value_width)
+    last_width = sum(part.shape[1] for part in parts_down[1:])
+    up_start = fold_start(up_part)
+    up_start, started, replies = lax.optimization_barrier((up_start, started, replies))
+    back = sum(replies, back_all[:, :rank])
+    folded = jnp.concatenate([fold_end(parts) for parts in started + [up_start]], axis=1)
+    second = send(after(folded, first, base_share, *rests), ("far", "tensor"))
+    arrived = [first, second]
+    grad_down, grad_up = total_product(arrived, shares, width, last_width, value_width)
     grad_down = grad_down.reshape(stored, piece, shares * width)
     grad_up = grad_up.reshape(stored, piece, values)
 
@@ -474,43 +577,22 @@
     for j in steps:
         theirs = output_product(
             [],
-            low_all[:, j * rank : (j + 1) * rank],
-            slots_of[j][:, None],
+            j,
+            low_all,
+            slot_columns,
             sent_slots[None, :],
             sent_select,
             own_ups,
         )
         addends.append(shift(theirs, "adapter", -j))
-    columns, selects, downs = [sent_slots[None, :]], [sent_select], [own_down]
-
-    def block(weights, block_slots, block_ranks):
-        columns.append(block_slots[None, :])
-        selects.append(choose(block_ranks, rank))
-        downs.append(weights)
-
-    quarter_column = column[: own * piece]
-    bundle_column = column[: own * bundle]
-    for j in steps:
-        away = (side - j) % sides
-        for i, weights in enumerate(quarters[j - 1]):
-            from_plane = plane - close + (close - i) % near
-            block(
-                weights,
-                away * own + quarter_column // piece,
-                from_plane * piece + quarter_column % piece,
-            )
-        for i in range(1, far):
-            adapter = bundle_column // bundle
-            block(
-                rests[(j - 1) * (far - 1) + i - 1],
-                (away * shares + (share ^ (adapter // stored))) * stored + adapter % stored,
-                (plane // near + i) % far * bundle + bundle_column % bundle,
-            )
+    downs = [own_down] + [block for n in range(len(steps)) for block in (
+        quarters[n] + spread_far[n] + rests[n * per : (n + 1) * per]
+    )]
     input_gradient = input_product(
         scaled,
         frozen_value_weight,
         back,
-        slots[:, None],
+        slot_columns,
         columns,
         selects,
         downs,
@@ -518,7 +600,7 @@
     )
     addends[0] = after(addends[0], input_gradient)
     mixed_out = output_product(
-        addends, low_all[:, :rank], slots[:, None], sent_slots[None, :], sent_select, own_ups
+        addends, 0, low_all, slot_columns, sent_slots[None, :], sent_select, own_ups
     )
     return mixed_out, input_gradient, grad_down, grad_up
 

time: 209 us -> 199 us (0.952)
  waiting for transfers between devices: 62 us -> 55.3 us
  other arithmetic: 24.9 us -> 20.1 us
  starting transfers between devices: 33.5 us -> 36.5 us
    ppermute x10 -> x12, waiting for transfers between devices: 37.2 us -> 20.7 us  [shift(): lax.ppermute(array, axis, [(i, (i + step) % size) for i in range(size)])]
    ppermute x12, waiting for transfers between devices: 24.8 us -> 32.7 us  [swap(): lax.ppermute(array, axis, [(i, i ^ bit) for i in range(lax.axis_size(axis...]
    convert_element_type x9, other arithmetic: 8.04 us -> 2.94 us  [add(): return (a.astype(jnp.float32) + b.astype(jnp.float32)).astype(jnp.bfloat16)]
    ppermute x10 -> x12, starting transfers between devices: 10.7 us -> 14.5 us  [shift(): lax.ppermute(array, axis, [(i, (i + step) % size) for i in range(size)])]
    dynamic_slice x2, local copies, waits for them, and re-layouts: 3.27 us -> 5.39 us  [over_shares(): lax.dynamic_slice_in_dim(matrix, (share ^ k) * columns, columns, 1)]
    pallas_call x10 -> x9, Pallas kernels: 55.2 us -> 53.7 us  [call(): pl.pallas_call(body, grid=grid, in_specs=in_specs, out_specs=out_spec, ou...]
    unnamed x46 -> x37, local copies, waits for them, and re-layouts: 5.36 us -> 4.71 us
  transfers between devices with their start and end apart: 25 -> 27, of which waited for: 8 -> 12; matrix products, arithmetic and copies ran while one was open for 24% -> 23% of each run, Pallas kernels for 25% -> 26%
where the time goes in v4:
time: 199 us; the launch traced here: 198 us
  waiting for transfers between devices  55.3 us (28%)
  Pallas kernels  53.7 us (27%)
  starting transfers between devices  36.5 us (18%)
  local copies, waits for them, and re-layouts  24.8 us (12%)
  other arithmetic  20.1 us (10%)
  matrix products  6.66 us (3%)
    pallas_call x9, Pallas kernels, call(): pl.pallas_call(body, grid=grid, in_specs=in_specs, out_specs=out_spec, ou...  53.7 us
    ppermute x12, waiting for transfers between devices, swap(): lax.ppermute(array, axis, [(i, i ^ bit) for i in range(lax.axis_size(axis...  32.7 us
    ppermute x12, waiting for transfers between devices, shift(): lax.ppermute(array, axis, [(i, (i + step) % size) for i in range(size)])  20.7 us
    ppermute x12, starting transfers between devices, shift(): lax.ppermute(array, axis, [(i, (i + step) % size) for i in range(size)])  14.5 us
    all_to_all x3, starting transfers between devices, exchange(): return lax.all_to_all(pieces, axes, split_axis=0, concat_axis=0, tiled=True)  13 us
    ppermute x12, starting transfers between devices, swap(): lax.ppermute(array, axis, [(i, i ^ bit) for i in range(lax.axis_size(axis...  8.96 us
    dot_general x1, matrix products, dot(): lax.dot_general(a, b, (((ca,), (cb,)), ((), ())), preferred_element_type=...  6.66 us
    dynamic_slice x2, local copies, waits for them, and re-layouts, over_shares(): lax.dynamic_slice_in_dim(matrix, (share ^ k) * columns, columns, 1)  5.39 us
  transfers between devices with their start and end apart: 27, of which 12 were waited for; matrix products, arithmetic and copies ran while one was open for 23% of the time, Pallas kernels for 26%

profile of v4, /device:TPU:0, one launch (start us, length us, event | category | flops | bytes accessed | tf_op | source)
XLA Modules:
  0.0 198.2 jit_solution(8290411701889948494)
XLA Ops:
  0.7 1.8 constant_dynamic-slice_fusion.17
  2.9 2.5 %collective-permute-start.2 = (bf16[192,256]{1,0:T(8,128)(2,1)}, bf16[192,256]{1,0:T(8,128)(2,1)}, u32[]{:S(2)}, u32[]{:S(2)}) collective-permute-start(bf16[192,256]{1,0:T(8,128)(2,1)} %get-tuple-element.126), channel_id=1, source_target_pairs={{0,2},{1,3},{2,0},{3,1},{4,6},{5,7},{6,4},{7,5},{8,10},{9,11},{10,... | collective-permute-start | bytes 294920 | tf_op jit(solution)/shard_map/ppermute | solution.py:29
  5.6 1.2 constant_dynamic-slice_fusion.18
  7.0 1.3 broadcast_in_dim.32
  8.3 4.3 %all-to-all-start = ((bf16[8,48,2048]{2,1,0:T(8,128)(2,1)}), bf16[8,48,2048]{2,1,0:T(8,128)(2,1)}, u32[]{:S(2)}, u32[]{:S(2)}) async-start(bf16[8,48,2048]{2,1,0:T(8,128)(2,1)} %bitcast.6), calls=%async_computation | async-start | bytes 3145728 | tf_op jit(solution)/shard_map/all_to_all | solution.py:20
  12.8 1.9 multiply_convert_fusion.refs_0_
  14.7 1.1 copy-done.1
  15.9 0.8 pad_maximum_fusion.4
  16.8 1.9 collective-permute-start
  20.7 6.7 %convolution_convert_fusion = bf16[768,1024]{1,0:T(8,128)(2,1)} fusion(bf16[768,2048]{1,0:T(8,128)(2,1)S(1)} %copy-done, bf16[2048,1024]{1,0:T(8,128)(2,1)} %refs_1_.1), kind=kOutput, calls=%fused_computation.2 | convolution fusion | flops 3222011904 | bytes 8912896 | tf_op jit(solution)/shard_map/dot_general | solution.py:68
  28.0 0.9 fusion.7.refs_3_
  29.4 1.8 pad_maximum_fusion.5.refs_2_.refs_4_.refs_6_
  31.3 3.6 %constant_dynamic-slice_fusion.13 = (bf16[192,2048]{1,0:T(8,128)(2,1)}, bf16[192,2048]{1,0:T(8,128)(2,1)}, bf16[192,2048]{1,0:T(8,128)(2,1)}, bf16[192,2048]{1,0:T(8,128)(2,1)}) fusion(bf16[192,8192]{1,0:T(8,128)(2,1)} %bitcast.37, s32[]{:T(128)S(6)} %select_n.260, s32[]{:T(128)S(6)} %select_n.263, s32[]{:T(128)S(6)} %select_n.262, s32[]{:T(128)S(6)} %select_n.261), kind=kLoop, calls=%fused_computation.102 | loop fusion | bytes 6291472 | tf_op jit(solution)/shard_map/dynamic_slice | solution.py:431
  35.5 1.3 slice.71
  36.8 1.1 fusion.1.refs_2_
  37.9 1.5 collective-permute-start.5
  39.8 2.1 %constant_dynamic-slice_fusion.9 = bf16[4,48,2048]{2,1,0:T(8,128)(2,1)} fusion(bf16[8,48,2048]{2,1,0:T(8,128)(2,1)} %all-to-all-done, s32[]{:T(128)S(6)} %select_n.265), kind=kLoop, calls=%fused_computation.98 | loop fusion | bytes 1572868 | tf_op jit(solution)/shard_map/dynamic_slice | solution.py:398
  41.9 1.8 collective-permute-start.7
  43.6 2.6 %collective-permute-start.8 = (bf16[192,2048]{1,0:T(8,128)(2,1)}, bf16[192,2048]{1,0:T(8,128)(2,1)}, u32[]{:S(2)}, u32[]{:S(2)}) collective-permute-start(bf16[192,2048]{1,0:T(8,128)(2,1)} %bitcast.9.refs_15_), channel_id=1, source_target_pairs={{0,16},{16,0},{1,17},{17,1},{2,18},{18,2},{3,19},{19,3},{4,20},{20... | collective-permute-start | bytes 2359304 | tf_op jit(solution)/shard_map/ppermute | solution.py:25
  47.2 0.9 copy.23
  48.2 1.8 slice.80.refs_1_.refs_5_
  50.0 8.6 %collective-permute-done.5 = bf16[192,2048]{1,0:T(8,128)(2,1)} collective-permute-done((bf16[192,2048]{1,0:T(8,128)(2,1)}, bf16[192,2048]{1,0:T(8,128)(2,1)}, u32[]{:S(2)}, u32[]{:S(2)}) %collective-permute-start.5) | collective-permute-done | bytes 786464 | tf_op jit(solution)/shard_map/ppermute | solution.py:29
  58.6 16.1 %collective-permute-done.6 = bf16[192,2048]{1,0:T(8,128)(2,1)} collective-permute-done((bf16[192,2048]{1,0:T(8,128)(2,1)}, bf16[192,2048]{1,0:T(8,128)(2,1)}, u32[]{:S(2)}, u32[]{:S(2)}) %collective-permute-start.6) | collective-permute-done | bytes 786464 | tf_op jit(solution)/shard_map/ppermute | solution.py:29
  74.6 3.2 %pad_maximum_fusion.refs_4_.refs_14_ = bf16[768,2048]{1,0:T(8,128)(2,1)} fusion(bf16[192,2048]{1,0:T(8,128)(2,1)} %collective-permute-done.6, bf16[192,2048]{1,0:T(8,128)(2,1)} %collective-permute-done.5, bf16[192,2048]{1,0:T(8,128)(2,1)} %collective-permute-done.4, bf16[192,2048]{1,0:T(8,128)(2,1)} %get-tuple-element.106), kind=kLoop, calls=%fused_computation | loop fusion | flops 12582912 | bytes 6291456 | tf_op jit(solution)/shard_map/concatenate | solution.py:434
  77.8 0.8 collective-permute-done.7.refs_16_
  78.6 2.6 %collective-permute-done.8.refs_17_ = bf16[192,2048]{1,0:T(8,128)(2,1)} collective-permute-done((bf16[192,2048]{1,0:T(8,128)(2,1)}, bf16[192,2048]{1,0:T(8,128)(2,1)}, u32[]{:S(2)}, u32[]{:S(2)}) %collective-permute-start.8) | collective-permute-done | bytes 786464 | tf_op jit(solution)/shard_map/ppermute | solution.py:25
  81.8 3.3 %shard_map.111 = bf16[768,128]{1,0:T(8,128)(2,1)} custom-call(bf16[768,256]{1,0:T(8,128)(2,1)} %copy-done.4, bf16[768,256]{1,0:T(8,128)(2,1)} %slice.80.refs_1_.refs_5_, bf16[768,256]{1,0:T(8,128)(2,1)} %pad_maximum_fusion.5.refs_2_.refs_4_.refs_6_, s32[1,768]{1,0:T(1,128)} %broadcast_in_dim.35.refs_3_.refs_5_.refs_2_.refs_4_, s32[768,2]{1,0:T(8,128)} %bitcast.30), custom_call_target="tpu_custom_call" | custom-call | flops 603979 | bytes 1188 | tf_op jit(solution)/shard_map/pallas_call | solution.py:73
  85.1 1.4 fusion.51
  86.7 1.8 collective-permute-start.14
  88.6 1.5 collective-permute-start.11
  90.1 5.3 %collective-permute-done.11 = bf16[768,128]{1,0:T(8,128)(2,1)S(1)} collective-permute-done((bf16[768,128]{1,0:T(8,128)(2,1)S(1)}, bf16[768,128]{1,0:T(8,128)(2,1)S(1)}, u32[]{:S(2)}, u32[]{:S(2)}) %collective-permute-start.11) | collective-permute-done | bytes 196640 | tf_op jit(solution)/shard_map/ppermute | solution.py:29
  95.4 0.7 add_convert_fusion.8.refs_0_
  96.1 10.1 %shard_map.112 = (bf16[768,1024]{1,0:T(8,128)(2,1)}, f32[768,128]{1,0:T(8,128)}) custom-call(bf16[768,128]{1,0:T(8,128)(2,1)} %add_convert_fusion.8.refs_0_, s32[2,768]{1,0:T(2,128)} %copy-done.13, s32[768,1]{1,0:T(8,128)} %fusion.1.refs_2_, bf16[768,64]{1,0:T(8,128)(2,1)} %fusion.7.refs_3_, bf16[768,2048]{1,0:T(8,128)(2,1)} %pad_maximum_fusion.refs_4_.refs_14_, ...), custom_call_target="tpu_custom_call" | custom-call | flops 4831838 | bytes 8177 | tf_op jit(solution)/shard_map/pallas_call | solution.py:73
  106.2 4.8 %all-to-all-start.1 = ((bf16[16,48,1024]{2,1,0:T(8,128)(2,1)}), bf16[16,48,1024]{2,1,0:T(8,128)(2,1)S(1)}, u32[]{:S(2)}, u32[]{:S(2)}) async-start(bf16[16,48,1024]{2,1,0:T(8,128)(2,1)} %bitcast.39), calls=%async_computation.1 | async-start | bytes 3145728 | tf_op jit(solution)/shard_map/all_to_all | solution.py:20
  111.0 1.2 constant_dynamic-slice_fusion
  112.9 0.9 copy-done.11
  113.8 6.3 %shard_map.113 = (bf16[768,512]{1,0:T(8,128)(2,1)}, f32[768,128]{1,0:T(8,128)}) custom-call(bf16[768,128]{1,0:T(8,128)(2,1)} %add_convert_fusion.8.refs_0_, s32[2,768]{1,0:T(2,128)} %copy-done.13, s32[768,1]{1,0:T(8,128)} %fusion.1.refs_2_, bf16[768,64]{1,0:T(8,128)(2,1)} %fusion.7.refs_3_, bf16[768,2048]{1,0:T(8,128)(2,1)} %pad_maximum_fusion.refs_4_.refs_14_, ...), custom_call_target="tpu_custom_call" | custom-call | flops 2415919 | bytes 7784 | tf_op jit(solution)/shard_map/pallas_call | solution.py:73
  120.1 3.8 %collective-permute-done.14.refs_8_ = bf16[768,512]{1,0:T(8,128)(2,1)S(1)} collective-permute-done((bf16[768,512]{1,0:T(8,128)(2,1)}, bf16[768,512]{1,0:T(8,128)(2,1)S(1)}, u32[]{:S(2)}, u32[]{:S(2)}) %collective-permute-start.14) | collective-permute-done | bytes 786464 | tf_op jit(solution)/shard_map/ppermute | solution.py:25
  123.9 0.9 copy-done.10
  124.8 6.3 %shard_map.114 = (bf16[768,512]{1,0:T(8,128)(2,1)}, bf16[768,128]{1,0:T(8,128)(2,1)}) custom-call(bf16[768,128]{1,0:T(8,128)(2,1)} %add_convert_fusion.8.refs_0_, s32[2,768]{1,0:T(2,128)} %copy-done.13, s32[768,1]{1,0:T(8,128)} %fusion.1.refs_2_, bf16[768,64]{1,0:T(8,128)(2,1)} %fusion.7.refs_3_, bf16[768,2048]{1,0:T(8,128)(2,1)} %pad_maximum_fusion.refs_4_.refs_14_, ...), custom_call_target="tpu_custom_call" | custom-call | flops 2415919 | bytes 7784 | tf_op jit(solution)/shard_map/pallas_call | solution.py:73
  131.9 0.9 collective-permute-done.15
  132.8 1.5 collective-permute-start.16
  134.4 0.8 slice.87
  135.7 0.8 constant_dynamic-slice_fusion.3
  136.5 1.6 collective-permute-start.19
  138.1 1.8 collective-permute-done.16
  140.4 0.7 add_convert_fusion.6.refs_0_.refs_2_
  141.2 4.3 %shard_map.115 = bf16[768,256]{1,0:T(8,128)(2,1)} custom-call(bf16[768,128]{1,0:T(8,128)(2,1)} %add_convert_fusion.6.refs_0_.refs_2_, s32[2,768]{1,0:T(2,128)} %copy-done.13, s32[768,1]{1,0:T(8,128)} %fusion.1.refs_2_, bf16[768,64]{1,0:T(8,128)(2,1)} %fusion.7.refs_3_, bf16[768,256]{1,0:T(8,128)(2,1)} %copy-done.4, bf16[768,256]{1,0:T(8,128)(2,1)} %slice.80.refs_1_.refs_5_), custom_call_target="tpu_custom_call" | custom-call | flops 603979 | bytes 1090 | tf_op jit(solution)/shard_map/pallas_call | solution.py:73
  145.5 1.0 constant_dynamic-slice_fusion.5
  146.5 2.4 %collective-permute-start.18 = (bf16[384,256]{1,0:T(8,128)(2,1)S(1)}, bf16[384,256]{1,0:T(8,128)(2,1)S(1)}, u32[]{:S(2)}, u32[]{:S(2)}) collective-permute-start(bf16[384,256]{1,0:T(8,128)(2,1)S(1)} %get-tuple-element.122), channel_id=1, source_target_pairs={{0,8},{8,0},{1,9},{9,1},{2,10},{10,2},{3,11},{11,3},{4,12},{12,4},... | collective-permute-start | bytes 589832 | tf_op jit(solution)/shard_map/ppermute | solution.py:25
  149.5 2.0 collective-permute-done.20
  151.5 8.4 %collective-permute-done.19 = bf16[384,512]{1,0:T(8,128)(2,1)S(1)} collective-permute-done((bf16[384,512]{1,0:T(8,128)(2,1)}, bf16[384,512]{1,0:T(8,128)(2,1)S(1)}, u32[]{:S(2)}, u32[]{:S(2)}) %collective-permute-start.19) | collective-permute-done | bytes 393248 | tf_op jit(solution)/shard_map/ppermute | solution.py:25
  159.9 3.1 %collective-permute-done.18 = bf16[384,256]{1,0:T(8,128)(2,1)S(1)} collective-permute-done((bf16[384,256]{1,0:T(8,128)(2,1)S(1)}, bf16[384,256]{1,0:T(8,128)(2,1)S(1)}, u32[]{:S(2)}, u32[]{:S(2)}) %collective-permute-start.18) | collective-permute-done | bytes 196640 | tf_op jit(solution)/shard_map/ppermute | solution.py:25
  163.2 1.1 pad_maximum_fusion.1
  164.3 0.8 add_convert_fusion.2.refs_0_
  165.2 3.9 %all-to-all-start.2 = ((bf16[8,48,1280]{2,1,0:T(8,128)(2,1)}), bf16[8,48,1280]{2,1,0:T(8,128)(2,1)S(1)}, u32[]{:S(2)}, u32[]{:S(2)}) async-start(bf16[8,48,1280]{2,1,0:T(8,128)(2,1)} %bitcast.16), calls=%async_computation.2 | async-start | bytes 1966080 | tf_op jit(solution)/shard_map/all_to_all | solution.py:20
  169.1 3.0 %shard_map.117 = bf16[768,256]{1,0:T(8,128)(2,1)} custom-call(bf16[768,128]{1,0:T(8,128)(2,1)} %add_convert_fusion.6.refs_0_.refs_2_, s32[768,2]{1,0:T(8,128)} %bitcast.34, s32[1,768]{1,0:T(1,128)} %broadcast_in_dim.35.refs_3_.refs_5_.refs_2_.refs_4_, bf16[64,768]{1,0:T(8,128)(2,1)} %fusion.8.refs_9_.refs_3_.refs_5_, ...), custom_call_target="tpu_custom_call" | custom-call | flops 301989 | bytes 697 | tf_op jit(solution)/shard_map/pallas_call | solution.py:73
  172.5 1.6 slice_add_fusion.refs_2_
  174.2 14.4 %shard_map.116 = bf16[768,2048]{1,0:T(8,128)(2,1)} custom-call(bf16[768,1024]{1,0:T(8,128)(2,1)} %copy-done.1, bf16[2048,1024]{1,0:T(8,128)(2,1)} %refs_1_.1, bf16[768,64]{1,0:T(8,128)(2,1)} %slice_add_fusion.refs_2_, s32[768,2]{1,0:T(8,128)} %bitcast.35, s32[1,768]{1,0:T(1,128)} %fusion.45.refs_4_, s32[1,192]{1,0:T(1,128)} %bitcast.42, s32[1,192]{1,0:T(1,128)} %bitcast.43, ...), custom_call_target="tpu_custom_call" | custom-call | flops 8053063 | bytes 12365 | tf_op jit(solution)/shard_map/pallas_call | solution.py:73
  188.6 0.7 copy-done.12
  189.3 3.1 %shard_map.118 = bf16[768,256]{1,0:T(8,128)(2,1)} custom-call(bf16[768,256]{1,0:T(8,128)(2,1)} %add_convert_fusion.2.refs_0_, bf16[768,256]{1,0:T(8,128)(2,1)} %copy-done.12, bf16[768,128]{1,0:T(8,128)(2,1)} %add_convert_fusion.6.refs_0_.refs_2_, s32[768,2]{1,0:T(8,128)} %bitcast.36, s32[1,768]{1,0:T(1,128)} %broadcast_in_dim.35.refs_3_.refs_5_.refs_2_.refs_4_, ...), custom_call_target="tpu_custom_call" | custom-call | flops 301989 | bytes 1483 | tf_op jit(solution)/shard_map/pallas_call | solution.py:73
  192.4 1.9 all-to-all-done.2.refs_1_
  194.3 1.0 copy-done.5
  195.3 2.9 %shard_map.119 = (bf16[48,8192]{1,0:T(8,128)(2,1)}, bf16[48,1024]{1,0:T(8,128)(2,1)}) custom-call(bf16[16,48,1024]{2,1,0:T(8,128)(2,1)} %copy-done.3, bf16[8,48,1280]{2,1,0:T(8,128)(2,1)} %copy-done.5), custom_call_target="tpu_custom_call" | custom-call | flops 1 | bytes 2555 | tf_op jit(solution)/shard_map/pallas_call | solution.py:73
  (93 shorter events, 10.8 us)
Async XLA Ops:
  2.4 27.0 %collective-permute-start.1 = (bf16[192,256]{1,0:T(8,128)(2,1)}, bf16[192,256]{1,0:T(8,128)(2,1)}, u32[]{:S(2)}, u32[]{:S(2)}) collective-permute-start(bf16[192,256]{1,0:T(8,128)(2,1)} %get-tuple-element.127), channel_id=1, source_target_pairs={{0,1},{1,0},{2,3},{3,2},{4,5},{5,4},{6,7},{7,6},{8,9},{9,8},{10,11... | collective-permute-start | bytes 294920 | tf_op jit(solution)/shard_map/ppermute | solution.py:29
  2.9 26.5 %collective-permute-start.2 = (bf16[192,256]{1,0:T(8,128)(2,1)}, bf16[192,256]{1,0:T(8,128)(2,1)}, u32[]{:S(2)}, u32[]{:S(2)}) collective-permute-start(bf16[192,256]{1,0:T(8,128)(2,1)} %get-tuple-element.126), channel_id=1, source_target_pairs={{0,2},{1,3},{2,0},{3,1},{4,6},{5,7},{6,4},{7,5},{8,10},{9,11},{10,... | collective-permute-start | bytes 294920 | tf_op jit(solution)/shard_map/ppermute | solution.py:29
  5.4 24.0 %collective-permute-start.3 = (bf16[192,256]{1,0:T(8,128)(2,1)}, bf16[192,256]{1,0:T(8,128)(2,1)}, u32[]{:S(2)}, u32[]{:S(2)}) collective-permute-start(bf16[192,256]{1,0:T(8,128)(2,1)} %get-tuple-element.125), channel_id=1, source_target_pairs={{0,3},{1,2},{2,1},{3,0},{4,7},{5,6},{6,5},{7,4},{8,11},{9,10},{10,... | collective-permute-start | bytes 294920 | tf_op jit(solution)/shard_map/ppermute | solution.py:29
  6.9 5.7 %copy-start.15 = (s32[768]{0:T(1024)S(1)}, s32[768]{0:T(1024)}, u32[]{:S(2)}) copy-start(s32[768]{0:T(1024)} %param.13) | copy-start | bytes 9220
  7.0 5.7 %copy-start.16 = (s32[24]{0:T(128)S(1)}, s32[24]{0:T(128)}, u32[]{:S(2)}) copy-start(s32[24]{0:T(128)} %param.15) | copy-start | bytes 292
  7.0 5.7 %copy-start.17 = (s32[1,24]{1,0:T(1,128)S(1)}, s32[1,24]{1,0:T(1,128)}, u32[]{:S(2)}) copy-start(s32[1,24]{1,0:T(1,128)} %param.14) | copy-start | bytes 292
  8.3 31.5 %all-to-all-start = ((bf16[8,48,2048]{2,1,0:T(8,128)(2,1)}), bf16[8,48,2048]{2,1,0:T(8,128)(2,1)}, u32[]{:S(2)}, u32[]{:S(2)}) async-start(bf16[8,48,2048]{2,1,0:T(8,128)(2,1)} %bitcast.6), calls=%async_computation | async-start | bytes 3145728 | tf_op jit(solution)/shard_map/all_to_all | solution.py:20
  12.6 8.0 %copy-start = (bf16[768,2048]{1,0:T(8,128)(2,1)S(1)}, bf16[768,2048]{1,0:T(8,128)(2,1)}, u32[]{:S(2)}) copy-start(bf16[768,2048]{1,0:T(8,128)(2,1)} %refs_7_.5) | copy-start | bytes 9437188
  14.7 1.1 copy-start.1
  15.9 11.5 %copy-start.4 = (bf16[768,256]{1,0:T(8,128)(2,1)}, bf16[768,256]{1,0:T(8,128)(2,1)S(1)}, u32[]{:S(2)}) copy-start(bf16[768,256]{1,0:T(8,128)(2,1)S(1)} %constant_dynamic-slice_fusion.19.refs_0_.refs_4_) | copy-start | bytes 1179652
  16.8 26.9 %collective-permute-start = (bf16[784,256]{1,0:T(8,128)(2,1)}, bf16[784,256]{1,0:T(8,128)(2,1)}, u32[]{:S(2)}, u32[]{:S(2)}) collective-permute-start(bf16[784,256]{1,0:T(8,128)(2,1)} %pad_maximum_fusion.4), channel_id=1, source_target_pairs={{0,4},{4,0},{1,5},{5,1},{2,6},{6,2},{3,7},{7,3},{8,12},{12,8},{9,1... | collective-permute-start | bytes 1204232 | tf_op jit(solution)/shard_map/ppermute | solution.py:25
  34.9 12.0 %collective-permute-start.4 = (bf16[192,2048]{1,0:T(8,128)(2,1)}, bf16[192,2048]{1,0:T(8,128)(2,1)}, u32[]{:S(2)}, u32[]{:S(2)}) collective-permute-start(bf16[192,2048]{1,0:T(8,128)(2,1)} %get-tuple-element.109), channel_id=1, source_target_pairs={{0,1},{1,0},{2,3},{3,2},{4,5},{5,4},{6,7},{7,6},{8,9},{9,8},{10,11... | collective-permute-start | bytes 2359304 | tf_op jit(solution)/shard_map/ppermute | solution.py:29
  37.9 20.7 %collective-permute-start.5 = (bf16[192,2048]{1,0:T(8,128)(2,1)}, bf16[192,2048]{1,0:T(8,128)(2,1)}, u32[]{:S(2)}, u32[]{:S(2)}) collective-permute-start(bf16[192,2048]{1,0:T(8,128)(2,1)} %get-tuple-element.108), channel_id=1, source_target_pairs={{0,2},{1,3},{2,0},{3,1},{4,6},{5,7},{6,4},{7,5},{8,10},{9,11},{10,... | collective-permute-start | bytes 2359304 | tf_op jit(solution)/shard_map/ppermute | solution.py:29
  39.4 35.3 %collective-permute-start.6 = (bf16[192,2048]{1,0:T(8,128)(2,1)}, bf16[192,2048]{1,0:T(8,128)(2,1)}, u32[]{:S(2)}, u32[]{:S(2)}) collective-permute-start(bf16[192,2048]{1,0:T(8,128)(2,1)} %get-tuple-element.107), channel_id=1, source_target_pairs={{0,3},{1,2},{2,1},{3,0},{4,7},{5,6},{6,5},{7,4},{8,11},{9,10},{10,... | collective-permute-start | bytes 2359304 | tf_op jit(solution)/shard_map/ppermute | solution.py:29
  41.9 36.8 %collective-permute-start.7 = (bf16[192,2048]{1,0:T(8,128)(2,1)}, bf16[192,2048]{1,0:T(8,128)(2,1)}, u32[]{:S(2)}, u32[]{:S(2)}) collective-permute-start(bf16[192,2048]{1,0:T(8,128)(2,1)} %bitcast.9.refs_15_), channel_id=1, source_target_pairs={{0,8},{8,0},{1,9},{9,1},{2,10},{10,2},{3,11},{11,3},{4,12},{12,4},... | collective-permute-start | bytes 2359304 | tf_op jit(solution)/shard_map/ppermute | solution.py:25
  43.6 37.6 %collective-permute-start.8 = (bf16[192,2048]{1,0:T(8,128)(2,1)}, bf16[192,2048]{1,0:T(8,128)(2,1)}, u32[]{:S(2)}, u32[]{:S(2)}) collective-permute-start(bf16[192,2048]{1,0:T(8,128)(2,1)} %bitcast.9.refs_15_), channel_id=1, source_target_pairs={{0,16},{16,0},{1,17},{17,1},{2,18},{18,2},{3,19},{19,3},{4,20},{20... | collective-permute-start | bytes 2359304 | tf_op jit(solution)/shard_map/ppermute | solution.py:25
  46.9 49.2 %collective-permute-start.12 = (bf16[768,1024]{1,0:T(8,128)(2,1)}, bf16[768,1024]{1,0:T(8,128)(2,1)}, u32[]{:S(2)}, u32[]{:S(2)}) collective-permute-start(bf16[768,1024]{1,0:T(8,128)(2,1)} %slice.71), channel_id=1, source_target_pairs={{0,4},{4,0},{1,5},{5,1},{2,6},{6,2},{3,7},{7,3},{8,12},{12,8},{9,1... | collective-permute-start | bytes 4718600 | tf_op jit(solution)/shard_map/ppermute | solution.py:25
  47.2 30.6 %copy-start.13 = (s32[2,768]{1,0:T(2,128)}, s32[2,768]{1,0:T(2,128)S(1)}, u32[]{:S(2)}) copy-start(s32[2,768]{1,0:T(2,128)S(1)} %pad_add_fusion.refs_1_) | copy-start | bytes 18436
  85.1 3.4 %copy-start.9 = (bf16[768,128]{1,0:T(8,128)(2,1)S(1)}, bf16[768,128]{1,0:T(8,128)(2,1)}, u32[]{:S(2)}) copy-start(bf16[768,128]{1,0:T(8,128)(2,1)} %shard_map.111) | copy-start | bytes 589828
  85.1 3.4 %collective-permute-start.10 = (bf16[768,128]{1,0:T(8,128)(2,1)}, bf16[768,128]{1,0:T(8,128)(2,1)S(1)}, u32[]{:S(2)}, u32[]{:S(2)}) collective-permute-start(bf16[768,128]{1,0:T(8,128)(2,1)} %shard_map.111), channel_id=1, source_target_pairs={{0,1},{1,0},{2,3},{3,2},{4,5},{5,4},{6,7},{7,6},{8,9},{9,8},{10,11... | collective-permute-start | bytes 589832 | tf_op jit(solution)/shard_map/ppermute | solution.py:29
  86.5 26.4 %collective-permute-start.13 = (bf16[768,512]{1,0:T(8,128)(2,1)}, bf16[768,512]{1,0:T(8,128)(2,1)S(1)}, u32[]{:S(2)}, u32[]{:S(2)}) collective-permute-start(bf16[768,512]{1,0:T(8,128)(2,1)} %get-tuple-element.64), channel_id=1, source_target_pairs={{0,4},{4,0},{1,5},{5,1},{2,6},{6,2},{3,7},{7,3},{8,12},{12,8},{9,1... | collective-permute-start | bytes 2359304 | tf_op jit(solution)/shard_map/ppermute | solution.py:25
  86.7 37.2 %collective-permute-start.14 = (bf16[768,512]{1,0:T(8,128)(2,1)}, bf16[768,512]{1,0:T(8,128)(2,1)S(1)}, u32[]{:S(2)}, u32[]{:S(2)}) collective-permute-start(bf16[768,512]{1,0:T(8,128)(2,1)} %get-tuple-element.68), channel_id=1, source_target_pairs={{0,4},{4,0},{1,5},{5,1},{2,6},{6,2},{3,7},{7,3},{8,12},{12,8},{9,1... | collective-permute-start | bytes 2359304 | tf_op jit(solution)/shard_map/ppermute | solution.py:25
  88.6 6.8 %collective-permute-start.11 = (bf16[768,128]{1,0:T(8,128)(2,1)S(1)}, bf16[768,128]{1,0:T(8,128)(2,1)S(1)}, u32[]{:S(2)}, u32[]{:S(2)}) collective-permute-start(bf16[768,128]{1,0:T(8,128)(2,1)S(1)} %add_convert_fusion.9), channel_id=1, source_target_pairs={{0,2},{1,3},{2,0},{3,1},{4,6},{5,7},{6,4},{7,5},{8,10},{9,11},{10,... | collective-permute-start | bytes 589832 | tf_op jit(solution)/shard_map/ppermute | solution.py:29
  106.2 58.9 %all-to-all-start.1 = ((bf16[16,48,1024]{2,1,0:T(8,128)(2,1)}), bf16[16,48,1024]{2,1,0:T(8,128)(2,1)S(1)}, u32[]{:S(2)}, u32[]{:S(2)}) async-start(bf16[16,48,1024]{2,1,0:T(8,128)(2,1)} %bitcast.39), calls=%async_computation.1 | async-start | bytes 3145728 | tf_op jit(solution)/shard_map/all_to_all | solution.py:20
  112.3 52.9 %collective-permute-start.22 = (bf16[192,2048]{1,0:T(8,128)(2,1)S(1)}, bf16[192,2048]{1,0:T(8,128)(2,1)}, u32[]{:S(2)}, u32[]{:S(2)}) collective-permute-start(bf16[192,2048]{1,0:T(8,128)(2,1)S(1)} %bitcast.40), channel_id=1, source_target_pairs={{0,4},{4,0},{1,5},{5,1},{2,6},{6,2},{3,7},{7,3},{8,12},{12,8},{9,1... | collective-permute-start | bytes 2359304 | tf_op jit(solution)/shard_map/ppermute | solution.py:25
  112.9 0.9 copy-start.11
  120.1 11.0 %copy-start.6 = (bf16[768,1024]{1,0:T(8,128)(2,1)S(1)}, bf16[768,1024]{1,0:T(8,128)(2,1)}, u32[]{:S(2)}) copy-start(bf16[768,1024]{1,0:T(8,128)(2,1)} %convolution_convert_fusion) | copy-start | bytes 4718596
  123.9 0.9 copy-start.10
  131.0 1.7 copy-start.14
  131.0 3.3 %copy-start.8 = (bf16[768,512]{1,0:T(8,128)(2,1)S(1)}, bf16[768,512]{1,0:T(8,128)(2,1)}, u32[]{:S(2)}) copy-start(bf16[768,512]{1,0:T(8,128)(2,1)} %get-tuple-element.74) | copy-start | bytes 2359300
  131.0 3.4 %copy-start.2 = (bf16[768,128]{1,0:T(8,128)(2,1)S(1)}, bf16[768,128]{1,0:T(8,128)(2,1)}, u32[]{:S(2)}) copy-start(bf16[768,128]{1,0:T(8,128)(2,1)} %add_convert_fusion.8.refs_0_) | copy-start | bytes 589828
  131.0 4.6 %copy-start.7 = (bf16[768,512]{1,0:T(8,128)(2,1)S(1)}, bf16[768,512]{1,0:T(8,128)(2,1)}, u32[]{:S(2)}) copy-start(bf16[768,512]{1,0:T(8,128)(2,1)} %get-tuple-element.73) | copy-start | bytes 2359300
  131.1 1.7 collective-permute-start.15
  131.3 15.2 %collective-permute-start.9 = (bf16[768,512]{1,0:T(8,128)(2,1)S(1)}, bf16[768,512]{1,0:T(8,128)(2,1)S(1)}, u32[]{:S(2)}, u32[]{:S(2)}) collective-permute-start(bf16[768,512]{1,0:T(8,128)(2,1)S(1)} %pad_maximum_fusion.3), channel_id=1, source_target_pairs={{0,1},{1,0},{2,3},{3,2},{4,5},{5,4},{6,7},{7,6},{8,9},{9,8},{10,11... | collective-permute-start | bytes 2359304 | tf_op jit(solution)/shard_map/ppermute | solution.py:29
  132.8 7.1 %collective-permute-start.16 = (bf16[768,128]{1,0:T(8,128)(2,1)S(1)}, bf16[768,128]{1,0:T(8,128)(2,1)S(1)}, u32[]{:S(2)}, u32[]{:S(2)}) collective-permute-start(bf16[768,128]{1,0:T(8,128)(2,1)S(1)} %add_convert_fusion.7), channel_id=1, source_target_pairs={{0,2},{1,3},{2,0},{3,1},{4,6},{5,7},{6,4},{7,5},{8,10},{9,11},{10,... | collective-permute-start | bytes 589832 | tf_op jit(solution)/shard_map/ppermute | solution.py:29
  135.2 16.2 %collective-permute-start.20 = (bf16[384,512]{1,0:T(8,128)(2,1)S(1)}, bf16[384,512]{1,0:T(8,128)(2,1)S(1)}, u32[]{:S(2)}, u32[]{:S(2)}) collective-permute-start(bf16[384,512]{1,0:T(8,128)(2,1)S(1)} %get-tuple-element.114), channel_id=1, source_target_pairs={{0,8},{8,0},{1,9},{9,1},{2,10},{10,2},{3,11},{11,3},{4,12},{12,4},... | collective-permute-start | bytes 1179656 | tf_op jit(solution)/shard_map/ppermute | solution.py:25
  136.5 23.4 %collective-permute-start.19 = (bf16[384,512]{1,0:T(8,128)(2,1)}, bf16[384,512]{1,0:T(8,128)(2,1)S(1)}, u32[]{:S(2)}, u32[]{:S(2)}) collective-permute-start(bf16[384,512]{1,0:T(8,128)(2,1)} %get-tuple-element.116), channel_id=1, source_target_pairs={{0,8},{8,0},{1,9},{9,1},{2,10},{10,2},{3,11},{11,3},{4,12},{12,4},... | collective-permute-start | bytes 1179656 | tf_op jit(solution)/shard_map/ppermute | solution.py:25
  139.9 9.3 %collective-permute-start.21 = (bf16[768,64]{1,0:T(8,128)(2,1)}, bf16[768,64]{1,0:T(8,128)(2,1)}, u32[]{:S(2)}, u32[]{:S(2)}) collective-permute-start(bf16[768,64]{1,0:T(8,128)(2,1)} %slice.87), channel_id=1, source_target_pairs={{0,4},{4,0},{1,5},{5,1},{2,6},{6,2},{3,7},{7,3},{8,12},{12,8},{9,1... | collective-permute-start | bytes 294920 | tf_op jit(solution)/shard_map/ppermute | solution.py:25
  146.5 16.4 %collective-permute-start.18 = (bf16[384,256]{1,0:T(8,128)(2,1)S(1)}, bf16[384,256]{1,0:T(8,128)(2,1)S(1)}, u32[]{:S(2)}, u32[]{:S(2)}) collective-permute-start(bf16[384,256]{1,0:T(8,128)(2,1)S(1)} %get-tuple-element.122), channel_id=1, source_target_pairs={{0,8},{8,0},{1,9},{9,1},{2,10},{10,2},{3,11},{11,3},{4,12},{12,4},... | collective-permute-start | bytes 589832 | tf_op jit(solution)/shard_map/ppermute | solution.py:25
  149.2 15.1 %collective-permute-start.17 = (bf16[768,256]{1,0:T(8,128)(2,1)S(1)}, bf16[768,256]{1,0:T(8,128)(2,1)S(1)}, u32[]{:S(2)}, u32[]{:S(2)}) collective-permute-start(bf16[768,256]{1,0:T(8,128)(2,1)S(1)} %get-tuple-element.72), channel_id=1, source_target_pairs={{0,2},{1,3},{2,0},{3,1},{4,6},{5,7},{6,4},{7,5},{8,10},{9,11},{10,... | collective-permute-start | bytes 1179656 | tf_op jit(solution)/shard_map/ppermute | solution.py:29
  165.2 23.4 %copy-start.3 = (bf16[16,48,1024]{2,1,0:T(8,128)(2,1)}, bf16[16,48,1024]{2,1,0:T(8,128)(2,1)S(1)}, u32[]{:S(2)}) copy-start(bf16[16,48,1024]{2,1,0:T(8,128)(2,1)S(1)} %all-to-all-done.1.refs_0_) | copy-start | bytes 4718596
  165.2 29.1 %all-to-all-start.2 = ((bf16[8,48,1280]{2,1,0:T(8,128)(2,1)}), bf16[8,48,1280]{2,1,0:T(8,128)(2,1)S(1)}, u32[]{:S(2)}, u32[]{:S(2)}) async-start(bf16[8,48,1280]{2,1,0:T(8,128)(2,1)} %bitcast.16), calls=%async_computation.2 | async-start | bytes 1966080 | tf_op jit(solution)/shard_map/all_to_all | solution.py:20
  172.1 16.4 %collective-permute-start.23 = (bf16[768,256]{1,0:T(8,128)(2,1)}, bf16[768,256]{1,0:T(8,128)(2,1)S(1)}, u32[]{:S(2)}, u32[]{:S(2)}) collective-permute-start(bf16[768,256]{1,0:T(8,128)(2,1)} %shard_map.117), channel_id=1, source_target_pairs={{0,4},{4,0},{1,5},{5,1},{2,6},{6,2},{3,7},{7,3},{8,12},{12,8},{9,1... | collective-permute-start | bytes 1179656 | tf_op jit(solution)/shard_map/ppermute | solution.py:25
  188.5 0.7 copy-start.12
  194.3 1.0 copy-start.5

commit v5 on v4

--- a/solution.py
+++ b/solution.py
@@ -438,7 +438,7 @@
     own_ups = over_shares(adapter_up_weight.reshape(stored * rank, values))
     down_flat = after(adapter_down_weight.reshape(stored * rank, shares * width), own_ups)
     own_down = over_shares(down_flat)
-    gated_ups = after(own_ups, own_down, *shared, *[b for blocks in spread_far for b in blocks])
+    gated_ups = after(own_ups, got)
 
     pieces, position = [], 0
     for part in PIECES:
@@ -501,6 +501,8 @@
         jnp.bfloat16,
     )
     back_part, base_term = lax.optimization_barrier((back_part, base_term))
+    far_blocks = [block for blocks in spread_far for block in blocks]
+    back_part = after(back_part, own_down, *shared, *far_blocks, *pieces[0][1][1:])
     back_all = tensor_sum(back_part)
     replies = [shift(back_all[:, j * rank : (j + 1) * rank], "adapter", -j) for j in steps]
 

time: 199 us -> 197 us (0.990)
  waiting for transfers between devices: 55.3 us -> 45.2 us
  starting transfers between devices: 36.5 us -> 44.4 us
    ppermute x12, waiting for transfers between devices: 20.7 us -> 11.8 us  [shift(): lax.ppermute(array, axis, [(i, (i + step) % size) for i in range(size)])]
    ppermute x12, starting transfers between devices: 14.5 us -> 18.1 us  [shift(): lax.ppermute(array, axis, [(i, (i + step) % size) for i in range(size)])]
    ppermute x12, starting transfers between devices: 8.96 us -> 11.6 us  [swap(): lax.ppermute(array, axis, [(i, i ^ bit) for i in range(lax.axis_size(axis...]
    unnamed x37 -> x39, local copies, waits for them, and re-layouts: 4.71 us -> 4.77 us
  transfers between devices with their start and end apart: 27 -> 27, of which waited for: 12 -> 9; matrix products, arithmetic and copies ran while one was open for 23% -> 23% of each run, Pallas kernels for 26% -> 26%
where the time goes in v5:
time: 197 us; the launch traced here: 196 us
  Pallas kernels  53.7 us (27%)
  waiting for transfers between devices  45.2 us (23%)
  starting transfers between devices  44.4 us (23%)
  local copies, waits for them, and re-layouts  24.9 us (13%)
  other arithmetic  20 us (10%)
  matrix products  6.66 us (3%)
    pallas_call x9, Pallas kernels, call(): pl.pallas_call(body, grid=grid, in_specs=in_specs, out_specs=out_spec, ou...  53.7 us
    ppermute x12, waiting for transfers between devices, swap(): lax.ppermute(array, axis, [(i, i ^ bit) for i in range(lax.axis_size(axis...  32.6 us
    ppermute x12, starting transfers between devices, shift(): lax.ppermute(array, axis, [(i, (i + step) % size) for i in range(size)])  18.1 us
    all_to_all x3, starting transfers between devices, exchange(): return lax.all_to_all(pieces, axes, split_axis=0, concat_axis=0, tiled=True)  14.7 us
    ppermute x12, waiting for transfers between devices, shift(): lax.ppermute(array, axis, [(i, (i + step) % size) for i in range(size)])  11.8 us
    ppermute x12, starting transfers between devices, swap(): lax.ppermute(array, axis, [(i, i ^ bit) for i in range(lax.axis_size(axis...  11.6 us
    dot_general x1, matrix products, dot(): lax.dot_general(a, b, (((ca,), (cb,)), ((), ())), preferred_element_type=...  6.66 us
    dynamic_slice x2, local copies, waits for them, and re-layouts, over_shares(): lax.dynamic_slice_in_dim(matrix, (share ^ k) * columns, columns, 1)  5.42 us
  transfers between devices with their start and end apart: 27, of which 9 were waited for; matrix products, arithmetic and copies ran while one was open for 23% of the time, Pallas kernels for 26%

profile of v5, /device:TPU:0, one launch (start us, length us, event | category | flops | bytes accessed | tf_op | source)
XLA Modules:
  0.0 196.0 jit_solution(5466520668177705133)
XLA Ops:
  0.7 1.8 constant_dynamic-slice_fusion.17
  2.9 2.5 %collective-permute-start.2 = (bf16[192,256]{1,0:T(8,128)(2,1)}, bf16[192,256]{1,0:T(8,128)(2,1)}, u32[]{:S(2)}, u32[]{:S(2)}) collective-permute-start(bf16[192,256]{1,0:T(8,128)(2,1)} %get-tuple-element.128), channel_id=1, source_target_pairs={{0,2},{1,3},{2,0},{3,1},{4,6},{5,7},{6,4},{7,5},{8,10},{9,11},{10,... | collective-permute-start | bytes 294920 | tf_op jit(solution)/shard_map/ppermute | solution.py:29
  5.6 1.2 constant_dynamic-slice_fusion.18
  7.0 1.4 broadcast_in_dim.32
  8.3 4.3 %all-to-all-start = ((bf16[8,48,2048]{2,1,0:T(8,128)(2,1)}), bf16[8,48,2048]{2,1,0:T(8,128)(2,1)}, u32[]{:S(2)}, u32[]{:S(2)}) async-start(bf16[8,48,2048]{2,1,0:T(8,128)(2,1)} %bitcast.6), calls=%async_computation | async-start | bytes 3145728 | tf_op jit(solution)/shard_map/all_to_all | solution.py:20
  12.8 1.9 multiply_convert_fusion.refs_0_
  14.7 1.1 copy-done.1
  16.0 0.8 pad_maximum_fusion.4
  16.8 1.9 collective-permute-start
  20.7 6.7 %convolution_convert_fusion = bf16[768,1024]{1,0:T(8,128)(2,1)} fusion(bf16[768,2048]{1,0:T(8,128)(2,1)S(1)} %copy-done, bf16[2048,1024]{1,0:T(8,128)(2,1)} %refs_1_.1), kind=kOutput, calls=%fused_computation.2 | convolution fusion | flops 3222011904 | bytes 8912896 | tf_op jit(solution)/shard_map/dot_general | solution.py:68
  28.5 1.3 slice.71
  29.9 1.8 pad_maximum_fusion.5.refs_2_.refs_4_.refs_6_
  31.7 3.6 %constant_dynamic-slice_fusion.11 = (bf16[192,2048]{1,0:T(8,128)(2,1)}, bf16[192,2048]{1,0:T(8,128)(2,1)}, bf16[192,2048]{1,0:T(8,128)(2,1)}, bf16[192,2048]{1,0:T(8,128)(2,1)}) fusion(bf16[192,8192]{1,0:T(8,128)(2,1)} %bitcast.37, s32[]{:T(128)S(6)} %select_n.283, s32[]{:T(128)S(6)} %select_n.286, s32[]{:T(128)S(6)} %select_n.285, s32[]{:T(128)S(6)} %select_n.284), kind=kLoop, calls=%fused_computation.100 | loop fusion | bytes 6291472 | tf_op jit(solution)/shard_map/dynamic_slice | solution.py:431
  35.6 0.9 fusion.7.refs_3_
  37.0 1.1 fusion.1.refs_2_
  38.2 1.8 collective-permute-start.6
  40.0 2.1 %constant_dynamic-slice_fusion.7 = bf16[4,48,2048]{2,1,0:T(8,128)(2,1)} fusion(bf16[8,48,2048]{2,1,0:T(8,128)(2,1)} %all-to-all-done, s32[]{:T(128)S(6)} %select_n.287), kind=kLoop, calls=%fused_computation.96 | loop fusion | bytes 1572868 | tf_op jit(solution)/shard_map/dynamic_slice | solution.py:398
  42.1 1.8 collective-permute-start.8
  43.8 2.6 %collective-permute-start.9 = (bf16[192,2048]{1,0:T(8,128)(2,1)}, bf16[192,2048]{1,0:T(8,128)(2,1)}, u32[]{:S(2)}, u32[]{:S(2)}) collective-permute-start(bf16[192,2048]{1,0:T(8,128)(2,1)} %bitcast.12.refs_15_), channel_id=1, source_target_pairs={{0,16},{16,0},{1,17},{17,1},{2,18},{18,2},{3,19},{19,3},{4,20},{20... | collective-permute-start | bytes 2359304 | tf_op jit(solution)/shard_map/ppermute | solution.py:25
  47.2 0.9 copy.23
  48.1 1.8 slice.80.refs_1_.refs_5_
  49.9 9.0 %collective-permute-done.6 = bf16[192,2048]{1,0:T(8,128)(2,1)} collective-permute-done((bf16[192,2048]{1,0:T(8,128)(2,1)}, bf16[192,2048]{1,0:T(8,128)(2,1)}, u32[]{:S(2)}, u32[]{:S(2)}) %collective-permute-start.6) | collective-permute-done | bytes 786464 | tf_op jit(solution)/shard_map/ppermute | solution.py:29
  58.8 15.6 %collective-permute-done.7 = bf16[192,2048]{1,0:T(8,128)(2,1)} collective-permute-done((bf16[192,2048]{1,0:T(8,128)(2,1)}, bf16[192,2048]{1,0:T(8,128)(2,1)}, u32[]{:S(2)}, u32[]{:S(2)}) %collective-permute-start.7) | collective-permute-done | bytes 786464 | tf_op jit(solution)/shard_map/ppermute | solution.py:29
  74.5 3.2 %pad_maximum_fusion.refs_4_.refs_14_ = bf16[768,2048]{1,0:T(8,128)(2,1)} fusion(bf16[192,2048]{1,0:T(8,128)(2,1)} %collective-permute-done.7, bf16[192,2048]{1,0:T(8,128)(2,1)} %collective-permute-done.6, bf16[192,2048]{1,0:T(8,128)(2,1)} %collective-permute-done.5, bf16[192,2048]{1,0:T(8,128)(2,1)} %get-tuple-element.108), kind=kLoop, calls=%fused_computation | loop fusion | flops 12582912 | bytes 6291456 | tf_op jit(solution)/shard_map/concatenate | solution.py:434
  78.3 3.3 %shard_map.111 = bf16[768,128]{1,0:T(8,128)(2,1)} custom-call(bf16[768,256]{1,0:T(8,128)(2,1)} %copy-done.4, bf16[768,256]{1,0:T(8,128)(2,1)} %slice.80.refs_1_.refs_5_, bf16[768,256]{1,0:T(8,128)(2,1)} %pad_maximum_fusion.5.refs_2_.refs_4_.refs_6_, s32[1,768]{1,0:T(1,128)} %broadcast_in_dim.35.refs_3_.refs_5_.refs_2_.refs_4_, s32[768,2]{1,0:T(8,128)} %bitcast.30), custom_call_target="tpu_custom_call" | custom-call | flops 603979 | bytes 1188 | tf_op jit(solution)/shard_map/pallas_call | solution.py:73
  81.6 0.8 collective-permute-start.11
  82.4 1.3 fusion.51
  83.7 1.7 collective-permute-start.13
  85.8 1.8 collective-permute-start.12
  87.6 4.6 %collective-permute-done.12 = bf16[768,128]{1,0:T(8,128)(2,1)S(1)} collective-permute-done((bf16[768,128]{1,0:T(8,128)(2,1)S(1)}, bf16[768,128]{1,0:T(8,128)(2,1)S(1)}, u32[]{:S(2)}, u32[]{:S(2)}) %collective-permute-start.12) | collective-permute-done | bytes 196640 | tf_op jit(solution)/shard_map/ppermute | solution.py:29
  92.1 0.7 add_convert_fusion.8.refs_0_
  92.9 10.2 %shard_map.112 = (bf16[768,1024]{1,0:T(8,128)(2,1)}, f32[768,128]{1,0:T(8,128)}) custom-call(bf16[768,128]{1,0:T(8,128)(2,1)} %add_convert_fusion.8.refs_0_, s32[2,768]{1,0:T(2,128)} %copy-done.14, s32[768,1]{1,0:T(8,128)} %fusion.1.refs_2_, bf16[768,64]{1,0:T(8,128)(2,1)} %fusion.7.refs_3_, bf16[768,2048]{1,0:T(8,128)(2,1)} %pad_maximum_fusion.refs_4_.refs_14_, ...), custom_call_target="tpu_custom_call" | custom-call | flops 4831838 | bytes 8177 | tf_op jit(solution)/shard_map/pallas_call | solution.py:73
  103.1 6.3 %all-to-all-start.1 = ((bf16[16,48,1024]{2,1,0:T(8,128)(2,1)}), bf16[16,48,1024]{2,1,0:T(8,128)(2,1)S(1)}, u32[]{:S(2)}, u32[]{:S(2)}) async-start(bf16[16,48,1024]{2,1,0:T(8,128)(2,1)} %bitcast.39), calls=%async_computation.1 | async-start | bytes 3145728 | tf_op jit(solution)/shard_map/all_to_all | solution.py:20
  109.4 1.2 constant_dynamic-slice_fusion
  110.6 1.6 collective-permute-start.22
  112.2 0.9 copy-done.11
  113.1 6.3 %shard_map.113 = (bf16[768,512]{1,0:T(8,128)(2,1)}, f32[768,128]{1,0:T(8,128)}) custom-call(bf16[768,128]{1,0:T(8,128)(2,1)} %add_convert_fusion.8.refs_0_, s32[2,768]{1,0:T(2,128)} %copy-done.14, s32[768,1]{1,0:T(8,128)} %fusion.1.refs_2_, bf16[768,64]{1,0:T(8,128)(2,1)} %fusion.7.refs_3_, bf16[768,2048]{1,0:T(8,128)(2,1)} %pad_maximum_fusion.refs_4_.refs_14_, ...), custom_call_target="tpu_custom_call" | custom-call | flops 2415919 | bytes 7784 | tf_op jit(solution)/shard_map/pallas_call | solution.py:73
  119.4 1.8 collective-permute-done.14.refs_8_
  121.2 0.9 copy-done.10
  122.1 6.3 %shard_map.114 = (bf16[768,512]{1,0:T(8,128)(2,1)}, bf16[768,128]{1,0:T(8,128)(2,1)}) custom-call(bf16[768,128]{1,0:T(8,128)(2,1)} %add_convert_fusion.8.refs_0_, s32[2,768]{1,0:T(2,128)} %copy-done.14, s32[768,1]{1,0:T(8,128)} %fusion.1.refs_2_, bf16[768,64]{1,0:T(8,128)(2,1)} %fusion.7.refs_3_, bf16[768,2048]{1,0:T(8,128)(2,1)} %pad_maximum_fusion.refs_4_.refs_14_, ...), custom_call_target="tpu_custom_call" | custom-call | flops 2415919 | bytes 7784 | tf_op jit(solution)/shard_map/pallas_call | solution.py:73
  129.2 0.9 collective-permute-done.15
  130.2 1.8 collective-permute-start.16
  132.0 0.8 slice.87
  132.8 1.8 collective-permute-start.20
  134.6 0.8 constant_dynamic-slice_fusion.3
  135.6 2.5 %collective-permute-done.16 = bf16[768,128]{1,0:T(8,128)(2,1)S(1)} collective-permute-done((bf16[768,128]{1,0:T(8,128)(2,1)S(1)}, bf16[768,128]{1,0:T(8,128)(2,1)S(1)}, u32[]{:S(2)}, u32[]{:S(2)}) %collective-permute-start.16) | collective-permute-done | bytes 196640 | tf_op jit(solution)/shard_map/ppermute | solution.py:29
  138.2 1.5 collective-permute-start.21
  140.4 4.3 %shard_map.115 = bf16[768,256]{1,0:T(8,128)(2,1)} custom-call(bf16[768,128]{1,0:T(8,128)(2,1)} %add_convert_fusion.6.refs_0_.refs_2_, s32[2,768]{1,0:T(2,128)} %copy-done.14, s32[768,1]{1,0:T(8,128)} %fusion.1.refs_2_, bf16[768,64]{1,0:T(8,128)(2,1)} %fusion.7.refs_3_, bf16[768,256]{1,0:T(8,128)(2,1)} %copy-done.4, bf16[768,256]{1,0:T(8,128)(2,1)} %slice.80.refs_1_.refs_5_), custom_call_target="tpu_custom_call" | custom-call | flops 603979 | bytes 1090 | tf_op jit(solution)/shard_map/pallas_call | solution.py:73
  144.7 1.0 constant_dynamic-slice_fusion.5
  145.7 2.9 %collective-permute-start.18 = (bf16[384,256]{1,0:T(8,128)(2,1)S(1)}, bf16[384,256]{1,0:T(8,128)(2,1)S(1)}, u32[]{:S(2)}, u32[]{:S(2)}) collective-permute-start(bf16[384,256]{1,0:T(8,128)(2,1)S(1)} %get-tuple-element.124), channel_id=1, source_target_pairs={{0,8},{8,0},{1,9},{9,1},{2,10},{10,2},{3,11},{11,3},{4,12},{12,4},... | collective-permute-start | bytes 589832 | tf_op jit(solution)/shard_map/ppermute | solution.py:25
  149.0 1.8 collective-permute-start.17
  150.7 6.7 %collective-permute-done.19 = bf16[384,512]{1,0:T(8,128)(2,1)S(1)} collective-permute-done((bf16[384,512]{1,0:T(8,128)(2,1)}, bf16[384,512]{1,0:T(8,128)(2,1)S(1)}, u32[]{:S(2)}, u32[]{:S(2)}) %collective-permute-start.19) | collective-permute-done | bytes 393248 | tf_op jit(solution)/shard_map/ppermute | solution.py:25
  157.4 3.2 %collective-permute-done.18 = bf16[384,256]{1,0:T(8,128)(2,1)S(1)} collective-permute-done((bf16[384,256]{1,0:T(8,128)(2,1)S(1)}, bf16[384,256]{1,0:T(8,128)(2,1)S(1)}, u32[]{:S(2)}, u32[]{:S(2)}) %collective-permute-start.18) | collective-permute-done | bytes 196640 | tf_op jit(solution)/shard_map/ppermute | solution.py:25
  161.0 1.1 pad_maximum_fusion.1
  162.0 0.8 add_convert_fusion.2.refs_0_
  162.9 4.1 %all-to-all-start.2 = ((bf16[8,48,1280]{2,1,0:T(8,128)(2,1)}), bf16[8,48,1280]{2,1,0:T(8,128)(2,1)S(1)}, u32[]{:S(2)}, u32[]{:S(2)}) async-start(bf16[8,48,1280]{2,1,0:T(8,128)(2,1)} %bitcast.16), calls=%async_computation.2 | async-start | bytes 1966080 | tf_op jit(solution)/shard_map/all_to_all | solution.py:20
  166.9 3.0 %shard_map.117 = bf16[768,256]{1,0:T(8,128)(2,1)} custom-call(bf16[768,128]{1,0:T(8,128)(2,1)} %add_convert_fusion.6.refs_0_.refs_2_, s32[768,2]{1,0:T(8,128)} %bitcast.34, s32[1,768]{1,0:T(1,128)} %broadcast_in_dim.35.refs_3_.refs_5_.refs_2_.refs_4_, bf16[64,768]{1,0:T(8,128)(2,1)} %fusion.8.refs_9_.refs_3_.refs_5_, ...), custom_call_target="tpu_custom_call" | custom-call | flops 301989 | bytes 697 | tf_op jit(solution)/shard_map/pallas_call | solution.py:73
  169.9 1.5 collective-permute-start.23
  171.4 1.6 slice_add_fusion.refs_2_
  173.1 14.4 %shard_map.116 = bf16[768,2048]{1,0:T(8,128)(2,1)} custom-call(bf16[768,1024]{1,0:T(8,128)(2,1)} %copy-done.1, bf16[2048,1024]{1,0:T(8,128)(2,1)} %refs_1_.1, bf16[768,64]{1,0:T(8,128)(2,1)} %slice_add_fusion.refs_2_, s32[768,2]{1,0:T(8,128)} %bitcast.35, s32[1,768]{1,0:T(1,128)} %fusion.45.refs_4_, s32[1,192]{1,0:T(1,128)} %bitcast.42, s32[1,192]{1,0:T(1,128)} %bitcast.43, ...), custom_call_target="tpu_custom_call" | custom-call | flops 8053063 | bytes 12365 | tf_op jit(solution)/shard_map/pallas_call | solution.py:73
  188.2 3.1 %shard_map.118 = bf16[768,256]{1,0:T(8,128)(2,1)} custom-call(bf16[768,256]{1,0:T(8,128)(2,1)} %add_convert_fusion.2.refs_0_, bf16[768,256]{1,0:T(8,128)(2,1)} %copy-done.12, bf16[768,128]{1,0:T(8,128)(2,1)} %add_convert_fusion.6.refs_0_.refs_2_, s32[768,2]{1,0:T(8,128)} %bitcast.36, s32[1,768]{1,0:T(1,128)} %broadcast_in_dim.35.refs_3_.refs_5_.refs_2_.refs_4_, ...), custom_call_target="tpu_custom_call" | custom-call | flops 301989 | bytes 1483 | tf_op jit(solution)/shard_map/pallas_call | solution.py:73
  191.3 0.8 all-to-all-done.2.refs_1_
  192.1 1.0 copy-done.5
  193.1 2.9 %shard_map.119 = (bf16[48,8192]{1,0:T(8,128)(2,1)}, bf16[48,1024]{1,0:T(8,128)(2,1)}) custom-call(bf16[16,48,1024]{2,1,0:T(8,128)(2,1)} %copy-done.3, bf16[8,48,1280]{2,1,0:T(8,128)(2,1)} %copy-done.5), custom_call_target="tpu_custom_call" | custom-call | flops 1 | bytes 2555 | tf_op jit(solution)/shard_map/pallas_call | solution.py:73
  (95 shorter events, 9.9 us)
Async XLA Ops:
  2.4 27.4 %collective-permute-start.1 = (bf16[192,256]{1,0:T(8,128)(2,1)}, bf16[192,256]{1,0:T(8,128)(2,1)}, u32[]{:S(2)}, u32[]{:S(2)}) collective-permute-start(bf16[192,256]{1,0:T(8,128)(2,1)} %get-tuple-element.129), channel_id=1, source_target_pairs={{0,1},{1,0},{2,3},{3,2},{4,5},{5,4},{6,7},{7,6},{8,9},{9,8},{10,11... | collective-permute-start | bytes 294920 | tf_op jit(solution)/shard_map/ppermute | solution.py:29
  2.9 27.0 %collective-permute-start.2 = (bf16[192,256]{1,0:T(8,128)(2,1)}, bf16[192,256]{1,0:T(8,128)(2,1)}, u32[]{:S(2)}, u32[]{:S(2)}) collective-permute-start(bf16[192,256]{1,0:T(8,128)(2,1)} %get-tuple-element.128), channel_id=1, source_target_pairs={{0,2},{1,3},{2,0},{3,1},{4,6},{5,7},{6,4},{7,5},{8,10},{9,11},{10,... | collective-permute-start | bytes 294920 | tf_op jit(solution)/shard_map/ppermute | solution.py:29
  5.4 24.4 %collective-permute-start.3 = (bf16[192,256]{1,0:T(8,128)(2,1)}, bf16[192,256]{1,0:T(8,128)(2,1)}, u32[]{:S(2)}, u32[]{:S(2)}) collective-permute-start(bf16[192,256]{1,0:T(8,128)(2,1)} %get-tuple-element.127), channel_id=1, source_target_pairs={{0,3},{1,2},{2,1},{3,0},{4,7},{5,6},{6,5},{7,4},{8,11},{9,10},{10,... | collective-permute-start | bytes 294920 | tf_op jit(solution)/shard_map/ppermute | solution.py:29
  6.9 5.7 %copy-start.16 = (s32[768]{0:T(1024)S(1)}, s32[768]{0:T(1024)}, u32[]{:S(2)}) copy-start(s32[768]{0:T(1024)} %param.13) | copy-start | bytes 9220
  7.0 5.7 %copy-start.17 = (s32[24]{0:T(128)S(1)}, s32[24]{0:T(128)}, u32[]{:S(2)}) copy-start(s32[24]{0:T(128)} %param.15) | copy-start | bytes 292
  7.0 5.7 %copy-start.18 = (s32[1,24]{1,0:T(1,128)S(1)}, s32[1,24]{1,0:T(1,128)}, u32[]{:S(2)}) copy-start(s32[1,24]{1,0:T(1,128)} %param.14) | copy-start | bytes 292
  8.3 31.6 %all-to-all-start = ((bf16[8,48,2048]{2,1,0:T(8,128)(2,1)}), bf16[8,48,2048]{2,1,0:T(8,128)(2,1)}, u32[]{:S(2)}, u32[]{:S(2)}) async-start(bf16[8,48,2048]{2,1,0:T(8,128)(2,1)} %bitcast.6), calls=%async_computation | async-start | bytes 3145728 | tf_op jit(solution)/shard_map/all_to_all | solution.py:20
  12.6 8.0 %copy-start = (bf16[768,2048]{1,0:T(8,128)(2,1)S(1)}, bf16[768,2048]{1,0:T(8,128)(2,1)}, u32[]{:S(2)}) copy-start(bf16[768,2048]{1,0:T(8,128)(2,1)} %refs_7_.5) | copy-start | bytes 9437188
  14.7 1.2 copy-start.1
  15.9 11.4 %copy-start.4 = (bf16[768,256]{1,0:T(8,128)(2,1)}, bf16[768,256]{1,0:T(8,128)(2,1)S(1)}, u32[]{:S(2)}) copy-start(bf16[768,256]{1,0:T(8,128)(2,1)S(1)} %constant_dynamic-slice_fusion.19.refs_0_.refs_4_) | copy-start | bytes 1179652
  16.8 25.3 %collective-permute-start = (bf16[784,256]{1,0:T(8,128)(2,1)}, bf16[784,256]{1,0:T(8,128)(2,1)}, u32[]{:S(2)}, u32[]{:S(2)}) collective-permute-start(bf16[784,256]{1,0:T(8,128)(2,1)} %pad_maximum_fusion.4), channel_id=1, source_target_pairs={{0,4},{4,0},{1,5},{5,1},{2,6},{6,2},{3,7},{7,3},{8,12},{12,8},{9,1... | collective-permute-start | bytes 1204232 | tf_op jit(solution)/shard_map/ppermute | solution.py:25
  27.3 2.5 %copy-start.13 = (bf16[192,256]{1,0:T(8,128)(2,1)S(1)}, bf16[192,256]{1,0:T(8,128)(2,1)}, u32[]{:S(2)}) copy-start(bf16[192,256]{1,0:T(8,128)(2,1)} %get-tuple-element.126) | copy-start | bytes 294916
  35.3 8.6 %collective-permute-start.5 = (bf16[192,2048]{1,0:T(8,128)(2,1)}, bf16[192,2048]{1,0:T(8,128)(2,1)}, u32[]{:S(2)}, u32[]{:S(2)}) collective-permute-start(bf16[192,2048]{1,0:T(8,128)(2,1)} %get-tuple-element.111), channel_id=1, source_target_pairs={{0,1},{1,0},{2,3},{3,2},{4,5},{5,4},{6,7},{7,6},{8,9},{9,8},{10,11... | collective-permute-start | bytes 2359304 | tf_op jit(solution)/shard_map/ppermute | solution.py:29
  35.3 46.3 %collective-permute-start.10 = (bf16[768,1024]{1,0:T(8,128)(2,1)}, bf16[768,1024]{1,0:T(8,128)(2,1)}, u32[]{:S(2)}, u32[]{:S(2)}) collective-permute-start(bf16[768,1024]{1,0:T(8,128)(2,1)} %slice.71), channel_id=1, source_target_pairs={{0,4},{4,0},{1,5},{5,1},{2,6},{6,2},{3,7},{7,3},{8,12},{12,8},{9,1... | collective-permute-start | bytes 4718600 | tf_op jit(solution)/shard_map/ppermute | solution.py:25
  38.2 20.7 %collective-permute-start.6 = (bf16[192,2048]{1,0:T(8,128)(2,1)}, bf16[192,2048]{1,0:T(8,128)(2,1)}, u32[]{:S(2)}, u32[]{:S(2)}) collective-permute-start(bf16[192,2048]{1,0:T(8,128)(2,1)} %get-tuple-element.110), channel_id=1, source_target_pairs={{0,2},{1,3},{2,0},{3,1},{4,6},{5,7},{6,4},{7,5},{8,10},{9,11},{10,... | collective-permute-start | bytes 2359304 | tf_op jit(solution)/shard_map/ppermute | solution.py:29
  40.0 34.5 %collective-permute-start.7 = (bf16[192,2048]{1,0:T(8,128)(2,1)}, bf16[192,2048]{1,0:T(8,128)(2,1)}, u32[]{:S(2)}, u32[]{:S(2)}) collective-permute-start(bf16[192,2048]{1,0:T(8,128)(2,1)} %get-tuple-element.109), channel_id=1, source_target_pairs={{0,3},{1,2},{2,1},{3,0},{4,7},{5,6},{6,5},{7,4},{8,11},{9,10},{10,... | collective-permute-start | bytes 2359304 | tf_op jit(solution)/shard_map/ppermute | solution.py:29
  42.1 39.5 %collective-permute-start.8 = (bf16[192,2048]{1,0:T(8,128)(2,1)}, bf16[192,2048]{1,0:T(8,128)(2,1)}, u32[]{:S(2)}, u32[]{:S(2)}) collective-permute-start(bf16[192,2048]{1,0:T(8,128)(2,1)} %bitcast.12.refs_15_), channel_id=1, source_target_pairs={{0,8},{8,0},{1,9},{9,1},{2,10},{10,2},{3,11},{11,3},{4,12},{12,4},... | collective-permute-start | bytes 2359304 | tf_op jit(solution)/shard_map/ppermute | solution.py:25
  43.8 37.8 %collective-permute-start.9 = (bf16[192,2048]{1,0:T(8,128)(2,1)}, bf16[192,2048]{1,0:T(8,128)(2,1)}, u32[]{:S(2)}, u32[]{:S(2)}) collective-permute-start(bf16[192,2048]{1,0:T(8,128)(2,1)} %bitcast.12.refs_15_), channel_id=1, source_target_pairs={{0,16},{16,0},{1,17},{17,1},{2,18},{18,2},{3,19},{19,3},{4,20},{20... | collective-permute-start | bytes 2359304 | tf_op jit(solution)/shard_map/ppermute | solution.py:25
  47.1 30.5 %copy-start.14 = (s32[2,768]{1,0:T(2,128)}, s32[2,768]{1,0:T(2,128)S(1)}, u32[]{:S(2)}) copy-start(s32[2,768]{1,0:T(2,128)S(1)} %pad_add_fusion.refs_1_) | copy-start | bytes 18436
  81.6 4.2 %copy-start.9 = (bf16[768,128]{1,0:T(8,128)(2,1)S(1)}, bf16[768,128]{1,0:T(8,128)(2,1)}, u32[]{:S(2)}) copy-start(bf16[768,128]{1,0:T(8,128)(2,1)} %shard_map.111) | copy-start | bytes 589828
  81.6 4.1 %collective-permute-start.11 = (bf16[768,128]{1,0:T(8,128)(2,1)}, bf16[768,128]{1,0:T(8,128)(2,1)S(1)}, u32[]{:S(2)}, u32[]{:S(2)}) collective-permute-start(bf16[768,128]{1,0:T(8,128)(2,1)} %shard_map.111), channel_id=1, source_target_pairs={{0,1},{1,0},{2,3},{3,2},{4,5},{5,4},{6,7},{7,6},{8,9},{9,8},{10,11... | collective-permute-start | bytes 589832 | tf_op jit(solution)/shard_map/ppermute | solution.py:29
  83.7 28.5 %collective-permute-start.13 = (bf16[768,512]{1,0:T(8,128)(2,1)}, bf16[768,512]{1,0:T(8,128)(2,1)S(1)}, u32[]{:S(2)}, u32[]{:S(2)}) collective-permute-start(bf16[768,512]{1,0:T(8,128)(2,1)} %get-tuple-element.66), channel_id=1, source_target_pairs={{0,4},{4,0},{1,5},{5,1},{2,6},{6,2},{3,7},{7,3},{8,12},{12,8},{9,1... | collective-permute-start | bytes 2359304 | tf_op jit(solution)/shard_map/ppermute | solution.py:25
  85.4 35.7 %collective-permute-start.14 = (bf16[768,512]{1,0:T(8,128)(2,1)}, bf16[768,512]{1,0:T(8,128)(2,1)S(1)}, u32[]{:S(2)}, u32[]{:S(2)}) collective-permute-start(bf16[768,512]{1,0:T(8,128)(2,1)} %get-tuple-element.70), channel_id=1, source_target_pairs={{0,4},{4,0},{1,5},{5,1},{2,6},{6,2},{3,7},{7,3},{8,12},{12,8},{9,1... | collective-permute-start | bytes 2359304 | tf_op jit(solution)/shard_map/ppermute | solution.py:25
  85.8 6.3 %collective-permute-start.12 = (bf16[768,128]{1,0:T(8,128)(2,1)S(1)}, bf16[768,128]{1,0:T(8,128)(2,1)S(1)}, u32[]{:S(2)}, u32[]{:S(2)}) collective-permute-start(bf16[768,128]{1,0:T(8,128)(2,1)S(1)} %add_convert_fusion.9), channel_id=1, source_target_pairs={{0,2},{1,3},{2,0},{3,1},{4,6},{5,7},{6,4},{7,5},{8,10},{9,11},{10,... | collective-permute-start | bytes 589832 | tf_op jit(solution)/shard_map/ppermute | solution.py:29
  103.1 59.8 %all-to-all-start.1 = ((bf16[16,48,1024]{2,1,0:T(8,128)(2,1)}), bf16[16,48,1024]{2,1,0:T(8,128)(2,1)S(1)}, u32[]{:S(2)}, u32[]{:S(2)}) async-start(bf16[16,48,1024]{2,1,0:T(8,128)(2,1)} %bitcast.39), calls=%async_computation.1 | async-start | bytes 3145728 | tf_op jit(solution)/shard_map/all_to_all | solution.py:20
  110.6 52.2 %collective-permute-start.22 = (bf16[192,2048]{1,0:T(8,128)(2,1)S(1)}, bf16[192,2048]{1,0:T(8,128)(2,1)}, u32[]{:S(2)}, u32[]{:S(2)}) collective-permute-start(bf16[192,2048]{1,0:T(8,128)(2,1)S(1)} %bitcast.40), channel_id=1, source_target_pairs={{0,4},{4,0},{1,5},{5,1},{2,6},{6,2},{3,7},{7,3},{8,12},{12,8},{9,1... | collective-permute-start | bytes 2359304 | tf_op jit(solution)/shard_map/ppermute | solution.py:25
  112.2 0.9 copy-start.11
  119.4 9.1 %copy-start.6 = (bf16[768,1024]{1,0:T(8,128)(2,1)S(1)}, bf16[768,1024]{1,0:T(8,128)(2,1)}, u32[]{:S(2)}) copy-start(bf16[768,1024]{1,0:T(8,128)(2,1)} %convolution_convert_fusion) | copy-start | bytes 4718596
  121.2 0.9 copy-start.10
  128.4 1.7 copy-start.15
  128.4 3.6 %copy-start.8 = (bf16[768,512]{1,0:T(8,128)(2,1)S(1)}, bf16[768,512]{1,0:T(8,128)(2,1)}, u32[]{:S(2)}) copy-start(bf16[768,512]{1,0:T(8,128)(2,1)} %get-tuple-element.76) | copy-start | bytes 2359300
  128.4 3.6 %copy-start.2 = (bf16[768,128]{1,0:T(8,128)(2,1)S(1)}, bf16[768,128]{1,0:T(8,128)(2,1)}, u32[]{:S(2)}) copy-start(bf16[768,128]{1,0:T(8,128)(2,1)} %add_convert_fusion.8.refs_0_) | copy-start | bytes 589828
  128.4 6.2 %copy-start.7 = (bf16[768,512]{1,0:T(8,128)(2,1)S(1)}, bf16[768,512]{1,0:T(8,128)(2,1)}, u32[]{:S(2)}) copy-start(bf16[768,512]{1,0:T(8,128)(2,1)} %get-tuple-element.75) | copy-start | bytes 2359300
  128.4 1.7 collective-permute-start.15
  128.7 17.1 %collective-permute-start.4 = (bf16[768,512]{1,0:T(8,128)(2,1)S(1)}, bf16[768,512]{1,0:T(8,128)(2,1)S(1)}, u32[]{:S(2)}, u32[]{:S(2)}) collective-permute-start(bf16[768,512]{1,0:T(8,128)(2,1)S(1)} %pad_maximum_fusion.3), channel_id=1, source_target_pairs={{0,1},{1,0},{2,3},{3,2},{4,5},{5,4},{6,7},{7,6},{8,9},{9,8},{10,11... | collective-permute-start | bytes 2359304 | tf_op jit(solution)/shard_map/ppermute | solution.py:29
  130.2 8.0 %collective-permute-start.16 = (bf16[768,128]{1,0:T(8,128)(2,1)S(1)}, bf16[768,128]{1,0:T(8,128)(2,1)S(1)}, u32[]{:S(2)}, u32[]{:S(2)}) collective-permute-start(bf16[768,128]{1,0:T(8,128)(2,1)S(1)} %add_convert_fusion.7), channel_id=1, source_target_pairs={{0,2},{1,3},{2,0},{3,1},{4,6},{5,7},{6,4},{7,5},{8,10},{9,11},{10,... | collective-permute-start | bytes 589832 | tf_op jit(solution)/shard_map/ppermute | solution.py:29
  132.8 17.9 %collective-permute-start.20 = (bf16[384,512]{1,0:T(8,128)(2,1)S(1)}, bf16[384,512]{1,0:T(8,128)(2,1)S(1)}, u32[]{:S(2)}, u32[]{:S(2)}) collective-permute-start(bf16[384,512]{1,0:T(8,128)(2,1)S(1)} %get-tuple-element.116), channel_id=1, source_target_pairs={{0,8},{8,0},{1,9},{9,1},{2,10},{10,2},{3,11},{11,3},{4,12},{12,4},... | collective-permute-start | bytes 1179656 | tf_op jit(solution)/shard_map/ppermute | solution.py:25
  135.4 22.1 %collective-permute-start.19 = (bf16[384,512]{1,0:T(8,128)(2,1)}, bf16[384,512]{1,0:T(8,128)(2,1)S(1)}, u32[]{:S(2)}, u32[]{:S(2)}) collective-permute-start(bf16[384,512]{1,0:T(8,128)(2,1)} %get-tuple-element.118), channel_id=1, source_target_pairs={{0,8},{8,0},{1,9},{9,1},{2,10},{10,2},{3,11},{11,3},{4,12},{12,4},... | collective-permute-start | bytes 1179656 | tf_op jit(solution)/shard_map/ppermute | solution.py:25
  138.2 10.8 %collective-permute-start.21 = (bf16[768,64]{1,0:T(8,128)(2,1)}, bf16[768,64]{1,0:T(8,128)(2,1)}, u32[]{:S(2)}, u32[]{:S(2)}) collective-permute-start(bf16[768,64]{1,0:T(8,128)(2,1)} %slice.87), channel_id=1, source_target_pairs={{0,4},{4,0},{1,5},{5,1},{2,6},{6,2},{3,7},{7,3},{8,12},{12,8},{9,1... | collective-permute-start | bytes 294920 | tf_op jit(solution)/shard_map/ppermute | solution.py:25
  145.7 15.0 %collective-permute-start.18 = (bf16[384,256]{1,0:T(8,128)(2,1)S(1)}, bf16[384,256]{1,0:T(8,128)(2,1)S(1)}, u32[]{:S(2)}, u32[]{:S(2)}) collective-permute-start(bf16[384,256]{1,0:T(8,128)(2,1)S(1)} %get-tuple-element.124), channel_id=1, source_target_pairs={{0,8},{8,0},{1,9},{9,1},{2,10},{10,2},{3,11},{11,3},{4,12},{12,4},... | collective-permute-start | bytes 589832 | tf_op jit(solution)/shard_map/ppermute | solution.py:25
  149.0 13.0 %collective-permute-start.17 = (bf16[768,256]{1,0:T(8,128)(2,1)S(1)}, bf16[768,256]{1,0:T(8,128)(2,1)S(1)}, u32[]{:S(2)}, u32[]{:S(2)}) collective-permute-start(bf16[768,256]{1,0:T(8,128)(2,1)S(1)} %get-tuple-element.74), channel_id=1, source_target_pairs={{0,2},{1,3},{2,0},{3,1},{4,6},{5,7},{6,4},{7,5},{8,10},{9,11},{10,... | collective-permute-start | bytes 1179656 | tf_op jit(solution)/shard_map/ppermute | solution.py:29
  162.9 24.6 %copy-start.3 = (bf16[16,48,1024]{2,1,0:T(8,128)(2,1)}, bf16[16,48,1024]{2,1,0:T(8,128)(2,1)S(1)}, u32[]{:S(2)}) copy-start(bf16[16,48,1024]{2,1,0:T(8,128)(2,1)S(1)} %all-to-all-done.1.refs_0_) | copy-start | bytes 4718596
  162.9 29.2 %all-to-all-start.2 = ((bf16[8,48,1280]{2,1,0:T(8,128)(2,1)}), bf16[8,48,1280]{2,1,0:T(8,128)(2,1)S(1)}, u32[]{:S(2)}, u32[]{:S(2)}) async-start(bf16[8,48,1280]{2,1,0:T(8,128)(2,1)} %bitcast.16), calls=%async_computation.2 | async-start | bytes 1966080 | tf_op jit(solution)/shard_map/all_to_all | solution.py:20
  169.9 17.5 %collective-permute-start.23 = (bf16[768,256]{1,0:T(8,128)(2,1)}, bf16[768,256]{1,0:T(8,128)(2,1)S(1)}, u32[]{:S(2)}, u32[]{:S(2)}) collective-permute-start(bf16[768,256]{1,0:T(8,128)(2,1)} %shard_map.117), channel_id=1, source_target_pairs={{0,4},{4,0},{1,5},{5,1},{2,6},{6,2},{3,7},{7,3},{8,12},{12,8},{9,1... | collective-permute-start | bytes 1179656 | tf_op jit(solution)/shard_map/ppermute | solution.py:25
  187.5 0.7 copy-start.12
  192.1 1.0 copy-start.5

commit v6 on v5

--- a/solution.py
+++ b/solution.py
@@ -531,7 +531,7 @@
             parts.append(part)
         parts_down.append(functools.reduce(add, parts))
         if last:
-            low_part = tensor_sum(jnp.concatenate(lows, axis=1), bits_below(shares)[:1])
+            low_part = tensor_sum(jnp.concatenate(lows, axis=1), bits_below(shares)[1:])
         lows, back_gate = lax.optimization_barrier((lows, back_gate))
     by_rank = own_down.reshape(own, rank, width)
     rests = []
@@ -559,7 +559,7 @@
 
     first = send(parts_down[0], ("near", "far", "tensor"))
     started = [fold_start(part) for part in parts_down[1:]]
-    low_all = tensor_sum(low_part, bits_below(shares)[1:])
+    low_all = tensor_sum(low_part, bits_below(shares)[:1])
     base_share = scatter_columns(base_term, low_all)
     up_part = weight_product(
         low_all, row_slots, part_slots, part_select, scaled_of, (0, value_width), ADAPTER_SCALE

time: 197 us -> 203 us (1.030)
  waiting for transfers between devices: 45.2 us -> 53 us
  starting transfers between devices: 44.4 us -> 42.2 us
    ppermute x12, waiting for transfers between devices: 11.8 us -> 17.5 us  [shift(): lax.ppermute(array, axis, [(i, (i + step) % size) for i in range(size)])]
    ppermute x12, waiting for transfers between devices: 32.6 us -> 35.5 us  [swap(): lax.ppermute(array, axis, [(i, i ^ bit) for i in range(lax.axis_size(axis...]
    ppermute x12, starting transfers between devices: 11.6 us -> 9.49 us  [swap(): lax.ppermute(array, axis, [(i, i ^ bit) for i in range(lax.axis_size(axis...]
  transfers between devices with their start and end apart: 27 -> 27, of which waited for: 9 -> 8; matrix products, arithmetic and copies ran while one was open for 23% -> 22% of each run, Pallas kernels for 26% -> 25%
where the time goes in v6:
time: 203 us; the launch traced here: 202 us
  Pallas kernels  53.7 us (26%)
  waiting for transfers between devices  53 us (26%)
  starting transfers between devices  42.2 us (21%)
  local copies, waits for them, and re-layouts  24.9 us (12%)
  other arithmetic  20 us (10%)
  matrix products  6.66 us (3%)
    pallas_call x9, Pallas kernels, call(): pl.pallas_call(body, grid=grid, in_specs=in_specs, out_specs=out_spec, ou...  53.7 us
    ppermute x12, waiting for transfers between devices, swap(): lax.ppermute(array, axis, [(i, i ^ bit) for i in range(lax.axis_size(axis...  35.5 us
    ppermute x12, starting transfers between devices, shift(): lax.ppermute(array, axis, [(i, (i + step) % size) for i in range(size)])  18.4 us
    ppermute x12, waiting for transfers between devices, shift(): lax.ppermute(array, axis, [(i, (i + step) % size) for i in range(size)])  17.5 us
    all_to_all x3, starting transfers between devices, exchange(): return lax.all_to_all(pieces, axes, split_axis=0, concat_axis=0, tiled=True)  14.4 us
    ppermute x12, starting transfers between devices, swap(): lax.ppermute(array, axis, [(i, i ^ bit) for i in range(lax.axis_size(axis...  9.49 us
    dot_general x1, matrix products, dot(): lax.dot_general(a, b, (((ca,), (cb,)), ((), ())), preferred_element_type=...  6.66 us
    dynamic_slice x2, local copies, waits for them, and re-layouts, over_shares(): lax.dynamic_slice_in_dim(matrix, (share ^ k) * columns, columns, 1)  5.42 us
  transfers between devices with their start and end apart: 27, of which 8 were waited for; matrix products, arithmetic and copies ran while one was open for 22% of the time, Pallas kernels for 25%

profile of v6, /device:TPU:0, one launch (start us, length us, event | category | flops | bytes accessed | tf_op | source)
XLA Modules:
  0.0 201.7 jit_solution(4529213494465536825)
XLA Ops:
  0.7 1.8 constant_dynamic-slice_fusion.17
  2.9 2.5 %collective-permute-start.2 = (bf16[192,256]{1,0:T(8,128)(2,1)}, bf16[192,256]{1,0:T(8,128)(2,1)}, u32[]{:S(2)}, u32[]{:S(2)}) collective-permute-start(bf16[192,256]{1,0:T(8,128)(2,1)} %get-tuple-element.128), channel_id=1, source_target_pairs={{0,2},{1,3},{2,0},{3,1},{4,6},{5,7},{6,4},{7,5},{8,10},{9,11},{10,... | collective-permute-start | bytes 294920 | tf_op jit(solution)/shard_map/ppermute | solution.py:29
  5.6 1.2 constant_dynamic-slice_fusion.18
  7.0 1.4 broadcast_in_dim.32
  8.3 4.3 %all-to-all-start = ((bf16[8,48,2048]{2,1,0:T(8,128)(2,1)}), bf16[8,48,2048]{2,1,0:T(8,128)(2,1)}, u32[]{:S(2)}, u32[]{:S(2)}) async-start(bf16[8,48,2048]{2,1,0:T(8,128)(2,1)} %bitcast.6), calls=%async_computation | async-start | bytes 3145728 | tf_op jit(solution)/shard_map/all_to_all | solution.py:20
  12.8 1.9 multiply_convert_fusion.refs_0_
  14.7 1.1 copy-done.1
  16.0 0.8 pad_maximum_fusion.4
  16.8 1.9 collective-permute-start
  20.7 6.7 %convolution_convert_fusion = bf16[768,1024]{1,0:T(8,128)(2,1)} fusion(bf16[768,2048]{1,0:T(8,128)(2,1)S(1)} %copy-done, bf16[2048,1024]{1,0:T(8,128)(2,1)} %refs_1_.1), kind=kOutput, calls=%fused_computation.2 | convolution fusion | flops 3222011904 | bytes 8912896 | tf_op jit(solution)/shard_map/dot_general | solution.py:68
  28.5 1.3 slice.71
  29.9 1.8 pad_maximum_fusion.5.refs_2_.refs_4_.refs_6_
  31.7 3.6 %constant_dynamic-slice_fusion.11 = (bf16[192,2048]{1,0:T(8,128)(2,1)}, bf16[192,2048]{1,0:T(8,128)(2,1)}, bf16[192,2048]{1,0:T(8,128)(2,1)}, bf16[192,2048]{1,0:T(8,128)(2,1)}) fusion(bf16[192,8192]{1,0:T(8,128)(2,1)} %bitcast.37, s32[]{:T(128)S(6)} %select_n.283, s32[]{:T(128)S(6)} %select_n.286, s32[]{:T(128)S(6)} %select_n.285, s32[]{:T(128)S(6)} %select_n.284), kind=kLoop, calls=%fused_computation.100 | loop fusion | bytes 6291472 | tf_op jit(solution)/shard_map/dynamic_slice | solution.py:431
  35.6 0.9 fusion.7.refs_3_
  37.0 1.1 fusion.1.refs_2_
  38.2 1.8 collective-permute-start.6
  40.0 2.1 %constant_dynamic-slice_fusion.7 = bf16[4,48,2048]{2,1,0:T(8,128)(2,1)} fusion(bf16[8,48,2048]{2,1,0:T(8,128)(2,1)} %all-to-all-done, s32[]{:T(128)S(6)} %select_n.287), kind=kLoop, calls=%fused_computation.96 | loop fusion | bytes 1572868 | tf_op jit(solution)/shard_map/dynamic_slice | solution.py:398
  42.1 1.8 collective-permute-start.8
  43.8 2.6 %collective-permute-start.9 = (bf16[192,2048]{1,0:T(8,128)(2,1)}, bf16[192,2048]{1,0:T(8,128)(2,1)}, u32[]{:S(2)}, u32[]{:S(2)}) collective-permute-start(bf16[192,2048]{1,0:T(8,128)(2,1)} %bitcast.12.refs_15_), channel_id=1, source_target_pairs={{0,16},{16,0},{1,17},{17,1},{2,18},{18,2},{3,19},{19,3},{4,20},{20... | collective-permute-start | bytes 2359304 | tf_op jit(solution)/shard_map/ppermute | solution.py:25
  47.2 0.9 copy.23
  48.1 1.8 slice.80.refs_1_.refs_5_
  49.9 9.0 %collective-permute-done.6 = bf16[192,2048]{1,0:T(8,128)(2,1)} collective-permute-done((bf16[192,2048]{1,0:T(8,128)(2,1)}, bf16[192,2048]{1,0:T(8,128)(2,1)}, u32[]{:S(2)}, u32[]{:S(2)}) %collective-permute-start.6) | collective-permute-done | bytes 786464 | tf_op jit(solution)/shard_map/ppermute | solution.py:29
  58.8 15.6 %collective-permute-done.7 = bf16[192,2048]{1,0:T(8,128)(2,1)} collective-permute-done((bf16[192,2048]{1,0:T(8,128)(2,1)}, bf16[192,2048]{1,0:T(8,128)(2,1)}, u32[]{:S(2)}, u32[]{:S(2)}) %collective-permute-start.7) | collective-permute-done | bytes 786464 | tf_op jit(solution)/shard_map/ppermute | solution.py:29
  74.5 3.2 %pad_maximum_fusion.refs_4_.refs_14_ = bf16[768,2048]{1,0:T(8,128)(2,1)} fusion(bf16[192,2048]{1,0:T(8,128)(2,1)} %collective-permute-done.7, bf16[192,2048]{1,0:T(8,128)(2,1)} %collective-permute-done.6, bf16[192,2048]{1,0:T(8,128)(2,1)} %collective-permute-done.5, bf16[192,2048]{1,0:T(8,128)(2,1)} %get-tuple-element.108), kind=kLoop, calls=%fused_computation | loop fusion | flops 12582912 | bytes 6291456 | tf_op jit(solution)/shard_map/concatenate | solution.py:434
  78.3 3.3 %shard_map.111 = bf16[768,128]{1,0:T(8,128)(2,1)} custom-call(bf16[768,256]{1,0:T(8,128)(2,1)} %copy-done.4, bf16[768,256]{1,0:T(8,128)(2,1)} %slice.80.refs_1_.refs_5_, bf16[768,256]{1,0:T(8,128)(2,1)} %pad_maximum_fusion.5.refs_2_.refs_4_.refs_6_, s32[1,768]{1,0:T(1,128)} %broadcast_in_dim.35.refs_3_.refs_5_.refs_2_.refs_4_, s32[768,2]{1,0:T(8,128)} %bitcast.30), custom_call_target="tpu_custom_call" | custom-call | flops 603979 | bytes 1188 | tf_op jit(solution)/shard_map/pallas_call | solution.py:73
  81.6 0.8 collective-permute-start.11
  82.4 1.3 fusion.51
  83.7 1.7 collective-permute-start.13
  85.8 1.8 collective-permute-start.12
  87.6 4.6 %collective-permute-done.12 = bf16[768,128]{1,0:T(8,128)(2,1)S(1)} collective-permute-done((bf16[768,128]{1,0:T(8,128)(2,1)S(1)}, bf16[768,128]{1,0:T(8,128)(2,1)S(1)}, u32[]{:S(2)}, u32[]{:S(2)}) %collective-permute-start.12) | collective-permute-done | bytes 196640 | tf_op jit(solution)/shard_map/ppermute | solution.py:29
  92.1 0.7 add_convert_fusion.8.refs_0_
  92.9 10.2 %shard_map.112 = (bf16[768,1024]{1,0:T(8,128)(2,1)}, f32[768,128]{1,0:T(8,128)}) custom-call(bf16[768,128]{1,0:T(8,128)(2,1)} %add_convert_fusion.8.refs_0_, s32[2,768]{1,0:T(2,128)} %copy-done.14, s32[768,1]{1,0:T(8,128)} %fusion.1.refs_2_, bf16[768,64]{1,0:T(8,128)(2,1)} %fusion.7.refs_3_, bf16[768,2048]{1,0:T(8,128)(2,1)} %pad_maximum_fusion.refs_4_.refs_14_, ...), custom_call_target="tpu_custom_call" | custom-call | flops 4831838 | bytes 8177 | tf_op jit(solution)/shard_map/pallas_call | solution.py:73
  103.1 6.3 %all-to-all-start.1 = ((bf16[16,48,1024]{2,1,0:T(8,128)(2,1)}), bf16[16,48,1024]{2,1,0:T(8,128)(2,1)S(1)}, u32[]{:S(2)}, u32[]{:S(2)}) async-start(bf16[16,48,1024]{2,1,0:T(8,128)(2,1)} %bitcast.39), calls=%async_computation.1 | async-start | bytes 3145728 | tf_op jit(solution)/shard_map/all_to_all | solution.py:20
  109.4 1.2 constant_dynamic-slice_fusion
  110.6 1.6 collective-permute-start.22
  112.2 0.9 copy-done.11
  113.1 6.3 %shard_map.113 = (bf16[768,512]{1,0:T(8,128)(2,1)}, f32[768,128]{1,0:T(8,128)}) custom-call(bf16[768,128]{1,0:T(8,128)(2,1)} %add_convert_fusion.8.refs_0_, s32[2,768]{1,0:T(2,128)} %copy-done.14, s32[768,1]{1,0:T(8,128)} %fusion.1.refs_2_, bf16[768,64]{1,0:T(8,128)(2,1)} %fusion.7.refs_3_, bf16[768,2048]{1,0:T(8,128)(2,1)} %pad_maximum_fusion.refs_4_.refs_14_, ...), custom_call_target="tpu_custom_call" | custom-call | flops 2415919 | bytes 7784 | tf_op jit(solution)/shard_map/pallas_call | solution.py:73
  119.4 1.8 collective-permute-done.14.refs_8_
  121.2 0.9 copy-done.10
  122.1 6.3 %shard_map.114 = (bf16[768,512]{1,0:T(8,128)(2,1)}, bf16[768,128]{1,0:T(8,128)(2,1)}) custom-call(bf16[768,128]{1,0:T(8,128)(2,1)} %add_convert_fusion.8.refs_0_, s32[2,768]{1,0:T(2,128)} %copy-done.14, s32[768,1]{1,0:T(8,128)} %fusion.1.refs_2_, bf16[768,64]{1,0:T(8,128)(2,1)} %fusion.7.refs_3_, bf16[768,2048]{1,0:T(8,128)(2,1)} %pad_maximum_fusion.refs_4_.refs_14_, ...), custom_call_target="tpu_custom_call" | custom-call | flops 2415919 | bytes 7784 | tf_op jit(solution)/shard_map/pallas_call | solution.py:73
  128.4 1.8 collective-permute-start.15
  130.4 6.3 %collective-permute-done.15 = bf16[768,128]{1,0:T(8,128)(2,1)S(1)} collective-permute-done((bf16[768,128]{1,0:T(8,128)(2,1)}, bf16[768,128]{1,0:T(8,128)(2,1)S(1)}, u32[]{:S(2)}, u32[]{:S(2)}) %collective-permute-start.15) | collective-permute-done | bytes 196640 | tf_op jit(solution)/shard_map/ppermute | solution.py:29
  136.9 0.8 slice.87
  137.7 3.0 %collective-permute-start.20 = (bf16[384,512]{1,0:T(8,128)(2,1)S(1)}, bf16[384,512]{1,0:T(8,128)(2,1)S(1)}, u32[]{:S(2)}, u32[]{:S(2)}) collective-permute-start(bf16[384,512]{1,0:T(8,128)(2,1)S(1)} %get-tuple-element.116), channel_id=1, source_target_pairs={{0,8},{8,0},{1,9},{9,1},{2,10},{10,2},{3,11},{11,3},{4,12},{12,4},... | collective-permute-start | bytes 1179656 | tf_op jit(solution)/shard_map/ppermute | solution.py:25
  140.8 0.8 constant_dynamic-slice_fusion.3
  141.6 1.6 collective-permute-start.21
  143.1 0.7 add_convert_fusion.6.refs_0_.refs_2_
  143.9 4.3 %shard_map.115 = bf16[768,256]{1,0:T(8,128)(2,1)} custom-call(bf16[768,128]{1,0:T(8,128)(2,1)} %add_convert_fusion.6.refs_0_.refs_2_, s32[2,768]{1,0:T(2,128)} %copy-done.14, s32[768,1]{1,0:T(8,128)} %fusion.1.refs_2_, bf16[768,64]{1,0:T(8,128)(2,1)} %fusion.7.refs_3_, bf16[768,256]{1,0:T(8,128)(2,1)} %copy-done.4, bf16[768,256]{1,0:T(8,128)(2,1)} %slice.80.refs_1_.refs_5_), custom_call_target="tpu_custom_call" | custom-call | flops 603979 | bytes 1090 | tf_op jit(solution)/shard_map/pallas_call | solution.py:73
  148.2 1.0 constant_dynamic-slice_fusion.5
  149.2 2.1 %collective-permute-start.18 = (bf16[384,256]{1,0:T(8,128)(2,1)S(1)}, bf16[384,256]{1,0:T(8,128)(2,1)S(1)}, u32[]{:S(2)}, u32[]{:S(2)}) collective-permute-start(bf16[384,256]{1,0:T(8,128)(2,1)S(1)} %get-tuple-element.124), channel_id=1, source_target_pairs={{0,8},{8,0},{1,9},{9,1},{2,10},{10,2},{3,11},{11,3},{4,12},{12,4},... | collective-permute-start | bytes 589832 | tf_op jit(solution)/shard_map/ppermute | solution.py:25
  151.7 3.2 %collective-permute-done.20 = bf16[384,512]{1,0:T(8,128)(2,1)S(1)} collective-permute-done((bf16[384,512]{1,0:T(8,128)(2,1)S(1)}, bf16[384,512]{1,0:T(8,128)(2,1)S(1)}, u32[]{:S(2)}, u32[]{:S(2)}) %collective-permute-start.20) | collective-permute-done | bytes 393248 | tf_op jit(solution)/shard_map/ppermute | solution.py:25
  154.9 8.4 %collective-permute-done.19 = bf16[384,512]{1,0:T(8,128)(2,1)S(1)} collective-permute-done((bf16[384,512]{1,0:T(8,128)(2,1)}, bf16[384,512]{1,0:T(8,128)(2,1)S(1)}, u32[]{:S(2)}, u32[]{:S(2)}) %collective-permute-start.19) | collective-permute-done | bytes 393248 | tf_op jit(solution)/shard_map/ppermute | solution.py:25
  163.4 4.0 %collective-permute-done.18 = bf16[384,256]{1,0:T(8,128)(2,1)S(1)} collective-permute-done((bf16[384,256]{1,0:T(8,128)(2,1)S(1)}, bf16[384,256]{1,0:T(8,128)(2,1)S(1)}, u32[]{:S(2)}, u32[]{:S(2)}) %collective-permute-start.18) | collective-permute-done | bytes 196640 | tf_op jit(solution)/shard_map/ppermute | solution.py:25
  167.6 1.1 pad_maximum_fusion.1
  168.7 0.8 add_convert_fusion.2.refs_0_
  169.6 3.8 %all-to-all-start.2 = ((bf16[8,48,1280]{2,1,0:T(8,128)(2,1)}), bf16[8,48,1280]{2,1,0:T(8,128)(2,1)S(1)}, u32[]{:S(2)}, u32[]{:S(2)}) async-start(bf16[8,48,1280]{2,1,0:T(8,128)(2,1)} %bitcast.16), calls=%async_computation.2 | async-start | bytes 1966080 | tf_op jit(solution)/shard_map/all_to_all | solution.py:20
  173.4 3.0 %shard_map.117 = bf16[768,256]{1,0:T(8,128)(2,1)} custom-call(bf16[768,128]{1,0:T(8,128)(2,1)} %add_convert_fusion.6.refs_0_.refs_2_, s32[768,2]{1,0:T(8,128)} %bitcast.34, s32[1,768]{1,0:T(1,128)} %broadcast_in_dim.35.refs_3_.refs_5_.refs_2_.refs_4_, bf16[64,768]{1,0:T(8,128)(2,1)} %fusion.8.refs_9_.refs_3_.refs_5_, ...), custom_call_target="tpu_custom_call" | custom-call | flops 301989 | bytes 697 | tf_op jit(solution)/shard_map/pallas_call | solution.py:73
  176.4 1.6 collective-permute-start.23
  177.9 1.6 slice_add_fusion.refs_2_
  179.6 14.4 %shard_map.116 = bf16[768,2048]{1,0:T(8,128)(2,1)} custom-call(bf16[768,1024]{1,0:T(8,128)(2,1)} %copy-done.1, bf16[2048,1024]{1,0:T(8,128)(2,1)} %refs_1_.1, bf16[768,64]{1,0:T(8,128)(2,1)} %slice_add_fusion.refs_2_, s32[768,2]{1,0:T(8,128)} %bitcast.35, s32[1,768]{1,0:T(1,128)} %fusion.45.refs_4_, s32[1,192]{1,0:T(1,128)} %bitcast.42, s32[1,192]{1,0:T(1,128)} %bitcast.43, ...), custom_call_target="tpu_custom_call" | custom-call | flops 8053063 | bytes 12365 | tf_op jit(solution)/shard_map/pallas_call | solution.py:73
  194.0 0.7 copy-done.12
  194.7 3.1 %shard_map.118 = bf16[768,256]{1,0:T(8,128)(2,1)} custom-call(bf16[768,256]{1,0:T(8,128)(2,1)} %add_convert_fusion.2.refs_0_, bf16[768,256]{1,0:T(8,128)(2,1)} %copy-done.12, bf16[768,128]{1,0:T(8,128)(2,1)} %add_convert_fusion.6.refs_0_.refs_2_, s32[768,2]{1,0:T(8,128)} %bitcast.36, s32[1,768]{1,0:T(1,128)} %broadcast_in_dim.35.refs_3_.refs_5_.refs_2_.refs_4_, ...), custom_call_target="tpu_custom_call" | custom-call | flops 301989 | bytes 1483 | tf_op jit(solution)/shard_map/pallas_call | solution.py:73
  197.8 1.0 copy-done.5
  198.8 2.9 %shard_map.119 = (bf16[48,8192]{1,0:T(8,128)(2,1)}, bf16[48,1024]{1,0:T(8,128)(2,1)}) custom-call(bf16[16,48,1024]{2,1,0:T(8,128)(2,1)} %copy-done.3, bf16[8,48,1280]{2,1,0:T(8,128)(2,1)} %copy-done.5), custom_call_target="tpu_custom_call" | custom-call | flops 1 | bytes 2555 | tf_op jit(solution)/shard_map/pallas_call | solution.py:73
  (95 shorter events, 7.8 us)
Async XLA Ops:
  2.4 27.4 %collective-permute-start.1 = (bf16[192,256]{1,0:T(8,128)(2,1)}, bf16[192,256]{1,0:T(8,128)(2,1)}, u32[]{:S(2)}, u32[]{:S(2)}) collective-permute-start(bf16[192,256]{1,0:T(8,128)(2,1)} %get-tuple-element.129), channel_id=1, source_target_pairs={{0,1},{1,0},{2,3},{3,2},{4,5},{5,4},{6,7},{7,6},{8,9},{9,8},{10,11... | collective-permute-start | bytes 294920 | tf_op jit(solution)/shard_map/ppermute | solution.py:29
  2.9 27.0 %collective-permute-start.2 = (bf16[192,256]{1,0:T(8,128)(2,1)}, bf16[192,256]{1,0:T(8,128)(2,1)}, u32[]{:S(2)}, u32[]{:S(2)}) collective-permute-start(bf16[192,256]{1,0:T(8,128)(2,1)} %get-tuple-element.128), channel_id=1, source_target_pairs={{0,2},{1,3},{2,0},{3,1},{4,6},{5,7},{6,4},{7,5},{8,10},{9,11},{10,... | collective-permute-start | bytes 294920 | tf_op jit(solution)/shard_map/ppermute | solution.py:29
  5.4 24.4 %collective-permute-start.3 = (bf16[192,256]{1,0:T(8,128)(2,1)}, bf16[192,256]{1,0:T(8,128)(2,1)}, u32[]{:S(2)}, u32[]{:S(2)}) collective-permute-start(bf16[192,256]{1,0:T(8,128)(2,1)} %get-tuple-element.127), channel_id=1, source_target_pairs={{0,3},{1,2},{2,1},{3,0},{4,7},{5,6},{6,5},{7,4},{8,11},{9,10},{10,... | collective-permute-start | bytes 294920 | tf_op jit(solution)/shard_map/ppermute | solution.py:29
  6.9 5.7 %copy-start.16 = (s32[768]{0:T(1024)S(1)}, s32[768]{0:T(1024)}, u32[]{:S(2)}) copy-start(s32[768]{0:T(1024)} %param.13) | copy-start | bytes 9220
  7.0 5.7 %copy-start.17 = (s32[24]{0:T(128)S(1)}, s32[24]{0:T(128)}, u32[]{:S(2)}) copy-start(s32[24]{0:T(128)} %param.15) | copy-start | bytes 292
  7.0 5.7 %copy-start.18 = (s32[1,24]{1,0:T(1,128)S(1)}, s32[1,24]{1,0:T(1,128)}, u32[]{:S(2)}) copy-start(s32[1,24]{1,0:T(1,128)} %param.14) | copy-start | bytes 292
  8.3 31.6 %all-to-all-start = ((bf16[8,48,2048]{2,1,0:T(8,128)(2,1)}), bf16[8,48,2048]{2,1,0:T(8,128)(2,1)}, u32[]{:S(2)}, u32[]{:S(2)}) async-start(bf16[8,48,2048]{2,1,0:T(8,128)(2,1)} %bitcast.6), calls=%async_computation | async-start | bytes 3145728 | tf_op jit(solution)/shard_map/all_to_all | solution.py:20
  12.6 8.0 %copy-start = (bf16[768,2048]{1,0:T(8,128)(2,1)S(1)}, bf16[768,2048]{1,0:T(8,128)(2,1)}, u32[]{:S(2)}) copy-start(bf16[768,2048]{1,0:T(8,128)(2,1)} %refs_7_.5) | copy-start | bytes 9437188
  14.7 1.2 copy-start.1
  15.9 11.4 %copy-start.4 = (bf16[768,256]{1,0:T(8,128)(2,1)}, bf16[768,256]{1,0:T(8,128)(2,1)S(1)}, u32[]{:S(2)}) copy-start(bf16[768,256]{1,0:T(8,128)(2,1)S(1)} %constant_dynamic-slice_fusion.19.refs_0_.refs_4_) | copy-start | bytes 1179652
  16.8 25.3 %collective-permute-start = (bf16[784,256]{1,0:T(8,128)(2,1)}, bf16[784,256]{1,0:T(8,128)(2,1)}, u32[]{:S(2)}, u32[]{:S(2)}) collective-permute-start(bf16[784,256]{1,0:T(8,128)(2,1)} %pad_maximum_fusion.4), channel_id=1, source_target_pairs={{0,4},{4,0},{1,5},{5,1},{2,6},{6,2},{3,7},{7,3},{8,12},{12,8},{9,1... | collective-permute-start | bytes 1204232 | tf_op jit(solution)/shard_map/ppermute | solution.py:25
  27.3 2.5 %copy-start.13 = (bf16[192,256]{1,0:T(8,128)(2,1)S(1)}, bf16[192,256]{1,0:T(8,128)(2,1)}, u32[]{:S(2)}) copy-start(bf16[192,256]{1,0:T(8,128)(2,1)} %get-tuple-element.126) | copy-start | bytes 294916
  35.3 8.6 %collective-permute-start.5 = (bf16[192,2048]{1,0:T(8,128)(2,1)}, bf16[192,2048]{1,0:T(8,128)(2,1)}, u32[]{:S(2)}, u32[]{:S(2)}) collective-permute-start(bf16[192,2048]{1,0:T(8,128)(2,1)} %get-tuple-element.111), channel_id=1, source_target_pairs={{0,1},{1,0},{2,3},{3,2},{4,5},{5,4},{6,7},{7,6},{8,9},{9,8},{10,11... | collective-permute-start | bytes 2359304 | tf_op jit(solution)/shard_map/ppermute | solution.py:29
  35.3 46.3 %collective-permute-start.10 = (bf16[768,1024]{1,0:T(8,128)(2,1)}, bf16[768,1024]{1,0:T(8,128)(2,1)}, u32[]{:S(2)}, u32[]{:S(2)}) collective-permute-start(bf16[768,1024]{1,0:T(8,128)(2,1)} %slice.71), channel_id=1, source_target_pairs={{0,4},{4,0},{1,5},{5,1},{2,6},{6,2},{3,7},{7,3},{8,12},{12,8},{9,1... | collective-permute-start | bytes 4718600 | tf_op jit(solution)/shard_map/ppermute | solution.py:25
  38.2 20.7 %collective-permute-start.6 = (bf16[192,2048]{1,0:T(8,128)(2,1)}, bf16[192,2048]{1,0:T(8,128)(2,1)}, u32[]{:S(2)}, u32[]{:S(2)}) collective-permute-start(bf16[192,2048]{1,0:T(8,128)(2,1)} %get-tuple-element.110), channel_id=1, source_target_pairs={{0,2},{1,3},{2,0},{3,1},{4,6},{5,7},{6,4},{7,5},{8,10},{9,11},{10,... | collective-permute-start | bytes 2359304 | tf_op jit(solution)/shard_map/ppermute | solution.py:29
  40.0 34.5 %collective-permute-start.7 = (bf16[192,2048]{1,0:T(8,128)(2,1)}, bf16[192,2048]{1,0:T(8,128)(2,1)}, u32[]{:S(2)}, u32[]{:S(2)}) collective-permute-start(bf16[192,2048]{1,0:T(8,128)(2,1)} %get-tuple-element.109), channel_id=1, source_target_pairs={{0,3},{1,2},{2,1},{3,0},{4,7},{5,6},{6,5},{7,4},{8,11},{9,10},{10,... | collective-permute-start | bytes 2359304 | tf_op jit(solution)/shard_map/ppermute | solution.py:29
  42.1 39.5 %collective-permute-start.8 = (bf16[192,2048]{1,0:T(8,128)(2,1)}, bf16[192,2048]{1,0:T(8,128)(2,1)}, u32[]{:S(2)}, u32[]{:S(2)}) collective-permute-start(bf16[192,2048]{1,0:T(8,128)(2,1)} %bitcast.12.refs_15_), channel_id=1, source_target_pairs={{0,8},{8,0},{1,9},{9,1},{2,10},{10,2},{3,11},{11,3},{4,12},{12,4},... | collective-permute-start | bytes 2359304 | tf_op jit(solution)/shard_map/ppermute | solution.py:25
  43.8 37.8 %collective-permute-start.9 = (bf16[192,2048]{1,0:T(8,128)(2,1)}, bf16[192,2048]{1,0:T(8,128)(2,1)}, u32[]{:S(2)}, u32[]{:S(2)}) collective-permute-start(bf16[192,2048]{1,0:T(8,128)(2,1)} %bitcast.12.refs_15_), channel_id=1, source_target_pairs={{0,16},{16,0},{1,17},{17,1},{2,18},{18,2},{3,19},{19,3},{4,20},{20... | collective-permute-start | bytes 2359304 | tf_op jit(solution)/shard_map/ppermute | solution.py:25
  47.1 30.5 %copy-start.14 = (s32[2,768]{1,0:T(2,128)}, s32[2,768]{1,0:T(2,128)S(1)}, u32[]{:S(2)}) copy-start(s32[2,768]{1,0:T(2,128)S(1)} %pad_add_fusion.refs_1_) | copy-start | bytes 18436
  81.6 4.2 %copy-start.9 = (bf16[768,128]{1,0:T(8,128)(2,1)S(1)}, bf16[768,128]{1,0:T(8,128)(2,1)}, u32[]{:S(2)}) copy-start(bf16[768,128]{1,0:T(8,128)(2,1)} %shard_map.111) | copy-start | bytes 589828
  81.6 4.1 %collective-permute-start.11 = (bf16[768,128]{1,0:T(8,128)(2,1)}, bf16[768,128]{1,0:T(8,128)(2,1)S(1)}, u32[]{:S(2)}, u32[]{:S(2)}) collective-permute-start(bf16[768,128]{1,0:T(8,128)(2,1)} %shard_map.111), channel_id=1, source_target_pairs={{0,1},{1,0},{2,3},{3,2},{4,5},{5,4},{6,7},{7,6},{8,9},{9,8},{10,11... | collective-permute-start | bytes 589832 | tf_op jit(solution)/shard_map/ppermute | solution.py:29
  83.7 28.5 %collective-permute-start.13 = (bf16[768,512]{1,0:T(8,128)(2,1)}, bf16[768,512]{1,0:T(8,128)(2,1)S(1)}, u32[]{:S(2)}, u32[]{:S(2)}) collective-permute-start(bf16[768,512]{1,0:T(8,128)(2,1)} %get-tuple-element.66), channel_id=1, source_target_pairs={{0,4},{4,0},{1,5},{5,1},{2,6},{6,2},{3,7},{7,3},{8,12},{12,8},{9,1... | collective-permute-start | bytes 2359304 | tf_op jit(solution)/shard_map/ppermute | solution.py:25
  85.4 35.7 %collective-permute-start.14 = (bf16[768,512]{1,0:T(8,128)(2,1)}, bf16[768,512]{1,0:T(8,128)(2,1)S(1)}, u32[]{:S(2)}, u32[]{:S(2)}) collective-permute-start(bf16[768,512]{1,0:T(8,128)(2,1)} %get-tuple-element.70), channel_id=1, source_target_pairs={{0,4},{4,0},{1,5},{5,1},{2,6},{6,2},{3,7},{7,3},{8,12},{12,8},{9,1... | collective-permute-start | bytes 2359304 | tf_op jit(solution)/shard_map/ppermute | solution.py:25
  85.8 6.3 %collective-permute-start.12 = (bf16[768,128]{1,0:T(8,128)(2,1)S(1)}, bf16[768,128]{1,0:T(8,128)(2,1)S(1)}, u32[]{:S(2)}, u32[]{:S(2)}) collective-permute-start(bf16[768,128]{1,0:T(8,128)(2,1)S(1)} %add_convert_fusion.9), channel_id=1, source_target_pairs={{0,2},{1,3},{2,0},{3,1},{4,6},{5,7},{6,4},{7,5},{8,10},{9,11},{10,... | collective-permute-start | bytes 589832 | tf_op jit(solution)/shard_map/ppermute | solution.py:29
  103.1 66.5 %all-to-all-start.1 = ((bf16[16,48,1024]{2,1,0:T(8,128)(2,1)}), bf16[16,48,1024]{2,1,0:T(8,128)(2,1)S(1)}, u32[]{:S(2)}, u32[]{:S(2)}) async-start(bf16[16,48,1024]{2,1,0:T(8,128)(2,1)} %bitcast.39), calls=%async_computation.1 | async-start | bytes 3145728 | tf_op jit(solution)/shard_map/all_to_all | solution.py:20
  110.6 58.9 %collective-permute-start.22 = (bf16[192,2048]{1,0:T(8,128)(2,1)S(1)}, bf16[192,2048]{1,0:T(8,128)(2,1)}, u32[]{:S(2)}, u32[]{:S(2)}) collective-permute-start(bf16[192,2048]{1,0:T(8,128)(2,1)S(1)} %bitcast.40), channel_id=1, source_target_pairs={{0,4},{4,0},{1,5},{5,1},{2,6},{6,2},{3,7},{7,3},{8,12},{12,8},{9,1... | collective-permute-start | bytes 2359304 | tf_op jit(solution)/shard_map/ppermute | solution.py:25
  112.2 0.9 copy-start.11
  119.4 10.8 %copy-start.6 = (bf16[768,1024]{1,0:T(8,128)(2,1)S(1)}, bf16[768,1024]{1,0:T(8,128)(2,1)}, u32[]{:S(2)}) copy-start(bf16[768,1024]{1,0:T(8,128)(2,1)} %convolution_convert_fusion) | copy-start | bytes 4718596
  121.2 0.9 copy-start.10
  128.4 8.3 %copy-start.15 = (bf16[768,128]{1,0:T(8,128)(2,1)S(1)}, bf16[768,128]{1,0:T(8,128)(2,1)}, u32[]{:S(2)}) copy-start(bf16[768,128]{1,0:T(8,128)(2,1)} %get-tuple-element.72) | copy-start | bytes 589828
  128.4 8.5 %copy-start.8 = (bf16[768,512]{1,0:T(8,128)(2,1)S(1)}, bf16[768,512]{1,0:T(8,128)(2,1)}, u32[]{:S(2)}) copy-start(bf16[768,512]{1,0:T(8,128)(2,1)} %get-tuple-element.76) | copy-start | bytes 2359300
  128.4 8.6 %copy-start.2 = (bf16[768,128]{1,0:T(8,128)(2,1)S(1)}, bf16[768,128]{1,0:T(8,128)(2,1)}, u32[]{:S(2)}) copy-start(bf16[768,128]{1,0:T(8,128)(2,1)} %add_convert_fusion.8.refs_0_) | copy-start | bytes 589828
  128.4 12.4 %copy-start.7 = (bf16[768,512]{1,0:T(8,128)(2,1)S(1)}, bf16[768,512]{1,0:T(8,128)(2,1)}, u32[]{:S(2)}) copy-start(bf16[768,512]{1,0:T(8,128)(2,1)} %get-tuple-element.75) | copy-start | bytes 2359300
  128.4 8.3 %collective-permute-start.15 = (bf16[768,128]{1,0:T(8,128)(2,1)}, bf16[768,128]{1,0:T(8,128)(2,1)S(1)}, u32[]{:S(2)}, u32[]{:S(2)}) collective-permute-start(bf16[768,128]{1,0:T(8,128)(2,1)} %get-tuple-element.72), channel_id=1, source_target_pairs={{0,2},{1,3},{2,0},{3,1},{4,6},{5,7},{6,4},{7,5},{8,10},{9,11},{10,... | collective-permute-start | bytes 589832 | tf_op jit(solution)/shard_map/ppermute | solution.py:29
  130.3 18.9 %collective-permute-start.4 = (bf16[768,512]{1,0:T(8,128)(2,1)S(1)}, bf16[768,512]{1,0:T(8,128)(2,1)S(1)}, u32[]{:S(2)}, u32[]{:S(2)}) collective-permute-start(bf16[768,512]{1,0:T(8,128)(2,1)S(1)} %pad_maximum_fusion.3), channel_id=1, source_target_pairs={{0,1},{1,0},{2,3},{3,2},{4,5},{5,4},{6,7},{7,6},{8,9},{9,8},{10,11... | collective-permute-start | bytes 2359304 | tf_op jit(solution)/shard_map/ppermute | solution.py:29
  136.8 4.8 %collective-permute-start.16 = (bf16[768,128]{1,0:T(8,128)(2,1)S(1)}, bf16[768,128]{1,0:T(8,128)(2,1)S(1)}, u32[]{:S(2)}, u32[]{:S(2)}) collective-permute-start(bf16[768,128]{1,0:T(8,128)(2,1)S(1)} %add_convert_fusion.7), channel_id=1, source_target_pairs={{0,1},{1,0},{2,3},{3,2},{4,5},{5,4},{6,7},{7,6},{8,9},{9,8},{10,11... | collective-permute-start | bytes 589832 | tf_op jit(solution)/shard_map/ppermute | solution.py:29
  137.7 17.2 %collective-permute-start.20 = (bf16[384,512]{1,0:T(8,128)(2,1)S(1)}, bf16[384,512]{1,0:T(8,128)(2,1)S(1)}, u32[]{:S(2)}, u32[]{:S(2)}) collective-permute-start(bf16[384,512]{1,0:T(8,128)(2,1)S(1)} %get-tuple-element.116), channel_id=1, source_target_pairs={{0,8},{8,0},{1,9},{9,1},{2,10},{10,2},{3,11},{11,3},{4,12},{12,4},... | collective-permute-start | bytes 1179656 | tf_op jit(solution)/shard_map/ppermute | solution.py:25
  141.6 21.8 %collective-permute-start.19 = (bf16[384,512]{1,0:T(8,128)(2,1)}, bf16[384,512]{1,0:T(8,128)(2,1)S(1)}, u32[]{:S(2)}, u32[]{:S(2)}) collective-permute-start(bf16[384,512]{1,0:T(8,128)(2,1)} %get-tuple-element.118), channel_id=1, source_target_pairs={{0,8},{8,0},{1,9},{9,1},{2,10},{10,2},{3,11},{11,3},{4,12},{12,4},... | collective-permute-start | bytes 1179656 | tf_op jit(solution)/shard_map/ppermute | solution.py:25
  141.6 10.0 %collective-permute-start.21 = (bf16[768,64]{1,0:T(8,128)(2,1)}, bf16[768,64]{1,0:T(8,128)(2,1)}, u32[]{:S(2)}, u32[]{:S(2)}) collective-permute-start(bf16[768,64]{1,0:T(8,128)(2,1)} %slice.87), channel_id=1, source_target_pairs={{0,4},{4,0},{1,5},{5,1},{2,6},{6,2},{3,7},{7,3},{8,12},{12,8},{9,1... | collective-permute-start | bytes 294920 | tf_op jit(solution)/shard_map/ppermute | solution.py:25
  149.2 18.1 %collective-permute-start.18 = (bf16[384,256]{1,0:T(8,128)(2,1)S(1)}, bf16[384,256]{1,0:T(8,128)(2,1)S(1)}, u32[]{:S(2)}, u32[]{:S(2)}) collective-permute-start(bf16[384,256]{1,0:T(8,128)(2,1)S(1)} %get-tuple-element.124), channel_id=1, source_target_pairs={{0,8},{8,0},{1,9},{9,1},{2,10},{10,2},{3,11},{11,3},{4,12},{12,4},... | collective-permute-start | bytes 589832 | tf_op jit(solution)/shard_map/ppermute | solution.py:25
  151.6 17.1 %collective-permute-start.17 = (bf16[768,256]{1,0:T(8,128)(2,1)S(1)}, bf16[768,256]{1,0:T(8,128)(2,1)S(1)}, u32[]{:S(2)}, u32[]{:S(2)}) collective-permute-start(bf16[768,256]{1,0:T(8,128)(2,1)S(1)} %get-tuple-element.74), channel_id=1, source_target_pairs={{0,2},{1,3},{2,0},{3,1},{4,6},{5,7},{6,4},{7,5},{8,10},{9,11},{10,... | collective-permute-start | bytes 1179656 | tf_op jit(solution)/shard_map/ppermute | solution.py:29
  169.6 24.4 %copy-start.3 = (bf16[16,48,1024]{2,1,0:T(8,128)(2,1)}, bf16[16,48,1024]{2,1,0:T(8,128)(2,1)S(1)}, u32[]{:S(2)}) copy-start(bf16[16,48,1024]{2,1,0:T(8,128)(2,1)S(1)} %all-to-all-done.1.refs_0_) | copy-start | bytes 4718596
  169.6 28.3 %all-to-all-start.2 = ((bf16[8,48,1280]{2,1,0:T(8,128)(2,1)}), bf16[8,48,1280]{2,1,0:T(8,128)(2,1)S(1)}, u32[]{:S(2)}, u32[]{:S(2)}) async-start(bf16[8,48,1280]{2,1,0:T(8,128)(2,1)} %bitcast.16), calls=%async_computation.2 | async-start | bytes 1966080 | tf_op jit(solution)/shard_map/all_to_all | solution.py:20
  176.4 17.6 %collective-permute-start.23 = (bf16[768,256]{1,0:T(8,128)(2,1)}, bf16[768,256]{1,0:T(8,128)(2,1)S(1)}, u32[]{:S(2)}, u32[]{:S(2)}) collective-permute-start(bf16[768,256]{1,0:T(8,128)(2,1)} %shard_map.117), channel_id=1, source_target_pairs={{0,4},{4,0},{1,5},{5,1},{2,6},{6,2},{3,7},{7,3},{8,12},{12,8},{9,1... | collective-permute-start | bytes 1179656 | tf_op jit(solution)/shard_map/ppermute | solution.py:25
  194.0 0.7 copy-start.12
  197.8 1.0 copy-start.5
